TPU v7x, 512 devices: a whole 4x8x8 slice. The times are simulated.
512 devices in a mesh: ctx: 64 (over z, x, y_lo), tp: 8 (over y_hi, core).
Axes of the slice: x: 4, y: 8 (y_hi: 4, y_lo: 2; y = y_hi * 2 + y_lo), z: 8, core: 2. Of those that a mesh axis runs over, the one named last changes fastest.
Arguments:
- tokens: bfloat16 [8192, 4096], P('ctx'), may hold values from -6 to 6
- new_token_states: bfloat16 [4, 4096], replicated, may hold values from -6.0625 to 6.0625
- w_query: bfloat16 [4096, 2048], P('ctx', 'tp'), may hold values from -0.12162204 to 0.12162204
- key_matrix: bfloat16 [4096, 1024], P('ctx', 'tp'), may hold values from -0.12162204 to 0.12162204
- value_matrix: bfloat16 [4096, 1024], P('ctx', 'tp'), may hold values from -0.09375 to 0.09375
- w_out: bfloat16 [2048, 4096], P('tp', 'ctx'), may hold values from -0.125 to 0.125
- lengths: int32 [4], replicated, may hold values from 1 to 4096, 8192 in all
- block_map: int32 [128], replicated, may hold values from 0 to 127, each once
Outputs:
- prefill_out: bfloat16 [8192, 4096], P('ctx', 'tp')
- decode_out: bfloat16 [4, 4096], P(None, 'tp')
Inputs may be any that keep to these rules, and one draw needn't show every extreme that they name: The lengths sum to 8192, and some request has exactly 4096 tokens. `block_map`: each of the 128 initial blocks is held exactly once.
All inputs are finite; a program needn't handle non-finite values.
Results may differ from a plain program's by a relative error of at most 0.015.
Values may be sent and summed in bfloat16 or wider, within the bound.
A program may use at most 64 MiB of HBM per device.

v0:
```python
import math

import jax
import jax.numpy as jnp
from jax import lax
from jax.sharding import PartitionSpec as P

HEAD_SIZE = 128


floor_value = -1e30


def initial_positions(block_map, first_row, row_count, block_rows):
    row_ids = first_row + jnp.arange(row_count, dtype=jnp.int32)
    block_ids = row_ids // block_rows
    table_ids = jnp.arange(block_map.shape[0], dtype=jnp.int32)
    mapped = jnp.sum(
        jnp.where(block_ids[:, None] == table_ids[None, :], block_map[None, :], 0), axis=1
    )
    return mapped * block_rows + row_ids % block_rows


def request_index(positions, request_ends):
    return jnp.sum((positions[:, None] >= request_ends[None, :]).astype(jnp.int32), axis=1)


def round_weights(weights):
    rounded = weights.astype(jnp.bfloat16)
    rounded = lax.optimization_barrier(rounded)
    return rounded.astype(jnp.float32)


def softmax_parts(
    dec_heads, projected_key_rows, projected_value_rows, owned, kv_heads, head_dim, score_scale
):
    row_count = projected_key_rows.shape[0]
    scores = (
        jnp.einsum(
            "rgjd,tgd->rgjt",
            dec_heads,
            projected_key_rows.reshape(row_count, kv_heads, head_dim),
            preferred_element_type=jnp.float32,
        )
        * score_scale
    )
    scores = jnp.where(owned, scores, floor_value)
    part_peak = jnp.max(scores, axis=3)
    weights = jnp.where(owned, jnp.exp(scores - part_peak[..., None]), 0.0)
    part_total = jnp.sum(weights, axis=3)
    part_mixed = jnp.einsum(
        "rgjt,tgd->rgjd",
        weights.astype(jnp.bfloat16),
        projected_value_rows.reshape(row_count, kv_heads, head_dim),
        preferred_element_type=jnp.float32,
    )
    return (part_peak, part_total, part_mixed)


def on_device(
    tokens, new_token_states, w_query, key_matrix, value_matrix, w_out, lengths, block_map
):
    local_rows = tokens.shape[0]
    block_rows = local_rows // 2
    request_count = new_token_states.shape[0]
    head_dim = HEAD_SIZE
    query_width = w_query.shape[1]
    kv_width = key_matrix.shape[1]
    kv_heads = kv_width // head_dim
    query_group_count = query_width // kv_width
    score_scale = 1.0 / math.sqrt(head_dim)
    device = lax.axis_index("ctx")
    request_ends = jnp.cumsum(lengths)
    inputs = jnp.concatenate([tokens, new_token_states], axis=0)
    shard_pieces = (
        lax.all_gather(w_query, "ctx", axis=0, tiled=True),
        lax.all_gather(key_matrix, "ctx", axis=0, tiled=True),
        lax.all_gather(value_matrix, "ctx", axis=0, tiled=True),
    )
    query_all, key_all, value_all = tuple(
        (jnp.dot(inputs, weight, preferred_element_type=jnp.float32) for weight in shard_pieces)
    )
    query_all = query_all.astype(jnp.bfloat16)
    key_all = key_all.astype(jnp.bfloat16)
    value_all = value_all.astype(jnp.bfloat16)
    local_query = query_all[:local_rows]
    local_keys = key_all[:local_rows]
    local_values = value_all[:local_rows]
    dec_query = query_all[local_rows:]
    decode_key_rows = key_all[local_rows:]
    decode_value_rows = value_all[local_rows:]
    token_pos = initial_positions(block_map, device * local_rows, local_rows, block_rows)
    token_request = request_index(token_pos, request_ends)
    query_heads = local_query.reshape(local_rows, kv_heads, query_group_count, head_dim)

    def attend(running, shard_pieces, first_row):
        peak_run, total_run, mixed_run = running
        key_piece, value_piece = shard_pieces
        row_count = key_piece.shape[0]
        key_pos = initial_positions(block_map, first_row, row_count, block_rows)
        key_request = request_index(key_pos, request_ends)
        allowed = (key_request[None, :] == token_request[:, None]) & (
            key_pos[None, :] <= token_pos[:, None]
        )
        scores = (
            jnp.einsum(
                "tgjd,kgd->gjtk",
                query_heads,
                key_piece.reshape(row_count, kv_heads, head_dim),
                preferred_element_type=jnp.float32,
            )
            * score_scale
        )
        scores = jnp.where(allowed, scores, floor_value)
        peak_new = jnp.maximum(peak_run, jnp.max(scores, axis=3))
        weights = jnp.where(allowed, jnp.exp(scores - peak_new[..., None]), 0.0)
        rescale = jnp.exp(peak_run - peak_new)
        total_new = total_run * rescale + jnp.sum(weights, axis=3)
        mixed_new = mixed_run * rescale[..., None] + jnp.einsum(
            "gjtk,kgd->gjtd",
            weights.astype(jnp.bfloat16),
            value_piece.reshape(row_count, kv_heads, head_dim),
            preferred_element_type=jnp.float32,
        )
        return (peak_new, total_new, mixed_new)

    start_state = (
        jnp.full((kv_heads, query_group_count, local_rows), floor_value, jnp.float32),
        jnp.zeros((kv_heads, query_group_count, local_rows), jnp.float32),
        jnp.zeros((kv_heads, query_group_count, local_rows, head_dim), jnp.float32),
    )
    dec_heads = dec_query.reshape(request_count, kv_heads, query_group_count, head_dim)
    request_ids = jnp.arange(request_count, dtype=jnp.int32)
    cache_keys, cache_values = (
        lax.all_gather(local_keys, "ctx", axis=0, tiled=True),
        lax.all_gather(local_values, "ctx", axis=0, tiled=True),
    )
    total_rows = cache_keys.shape[0]
    shard_count = total_rows // local_rows
    limit = max(1, 1024 // local_rows)
    step_rows = local_rows * math.gcd(shard_count, 1 << limit.bit_length() - 1)

    def key_step(running, step_index):
        first_row = step_index * step_rows
        pieces = (
            lax.dynamic_slice_in_dim(cache_keys, first_row, step_rows, 0),
            lax.dynamic_slice_in_dim(cache_values, first_row, step_rows, 0),
        )
        return (attend(running, pieces, first_row), None)

    final_state, unused = lax.scan(
        key_step, start_state, jnp.arange(total_rows // step_rows, dtype=jnp.int32)
    )
    peak_run, total_run, mixed_run = final_state
    cache_pos = (
        block_map[:, None] * block_rows + jnp.arange(block_rows, dtype=jnp.int32)[None, :]
    ).reshape(total_rows)
    cache_request = request_index(cache_pos, request_ends)
    owned = (cache_request[None, :] == request_ids[:, None])[:, None, None, :]
    cache_peak, cache_total, cache_mixed = softmax_parts(
        dec_heads, cache_keys, cache_values, owned, kv_heads, head_dim, score_scale
    )
    attended = (
        (mixed_run / total_run[..., None]).transpose(2, 0, 1, 3).reshape(local_rows, query_width)
    )
    attended = attended.astype(jnp.bfloat16)
    own_keys = decode_key_rows.reshape(request_count, kv_heads, 1, head_dim).astype(jnp.float32)
    own_values = decode_value_rows.reshape(request_count, kv_heads, 1, head_dim).astype(jnp.float32)
    self_scores = jnp.sum(dec_heads.astype(jnp.float32) * own_keys, axis=3) * score_scale
    peak_all = jnp.maximum(cache_peak, self_scores)
    rescale = jnp.exp(cache_peak - peak_all)
    self_weights = jnp.exp(self_scores - peak_all)
    dec_total = cache_total * rescale + self_weights
    dec_mixed = (
        cache_mixed * rescale[..., None] + round_weights(self_weights)[..., None] * own_values
    )
    dec_attn = (
        (dec_mixed / dec_total[..., None]).reshape(request_count, query_width).astype(jnp.bfloat16)
    )
    attended_all = jnp.concatenate([attended, dec_attn], axis=0)
    projected = jnp.dot(
        attended_all,
        lax.all_gather(w_out, "ctx", axis=1, tiled=True),
        preferred_element_type=jnp.float32,
    )
    summed_rows = lax.psum_scatter(
        projected.astype(jnp.bfloat16), "tp", scatter_dimension=1, tiled=True
    ).astype(jnp.float32)
    summed_rows = summed_rows.astype(jnp.bfloat16)
    return (summed_rows[:local_rows], summed_rows[local_rows:])


def solution(mesh):
    return jax.shard_map(
        on_device,
        mesh=mesh,
        in_specs=(
            P("ctx", None),
            P(),
            P("ctx", "tp"),
            P("ctx", "tp"),
            P("ctx", "tp"),
            P("tp", "ctx"),
            P(),
            P(),
        ),
        out_specs=(P("ctx", "tp"), P(None, "tp")),
        check_vma=False,
    )
```

profile of v0, /device:TPU:1, one launch (start us, length us, event | category | flops | bytes accessed | tf_op | source)
XLA Modules:
  0.0 1874.8 jit_solution(13340912142481138147)
XLA Ops:
  7.2 0.7 all-gather.7.cloned.1.call-update
  8.0 0.7 all-gather.13.cloned.1.call-update
  8.7 0.7 all-gather.11.cloned.1.call-update
  9.4 1.3 constant_dynamic-update-slice_fusion.1
  10.8 259.0 %all-gather.7.cloned.1.call-done = bf16[4096,128]{1,0:T(8,128)(2,1)} async-done(((bf16[64,128]{1,0:T(8,128)(2,1)}), bf16[4096,128]{1,0:T(8,128)(2,1)}) %all-gather.7.cloned.1.call-update) | async-done | bytes 1048592 | tf_op jit(solution)/shard_map/all_gather | solution.py:77
  269.8 1.7 convolution_convert_fusion.3
  271.5 0.6 slice.32
  272.2 296.4 %all-gather.13.cloned.1.call-done = bf16[4096,128]{1,0:T(8,128)(2,1)} async-done(((bf16[64,128]{1,0:T(8,128)(2,1)}), bf16[4096,128]{1,0:T(8,128)(2,1)}) %all-gather.13.cloned.1.call-update) | async-done | bytes 1048592 | tf_op jit(solution)/shard_map/all_gather | solution.py:78
  568.5 1.7 convolution_convert_fusion.2
  570.2 0.6 slice.34
  570.9 0.5 all-gather.17.cloned.1.call-update
  572.4 301.5 %all-gather.11.cloned.1.call-done = bf16[4096,256]{1,0:T(8,128)(2,1)} async-done(((bf16[64,256]{1,0:T(8,128)(2,1)}), bf16[4096,256]{1,0:T(8,128)(2,1)}) %all-gather.11.cloned.1.call-update) | async-done | bytes 2097168 | tf_op jit(solution)/shard_map/all_gather | solution.py:76
  873.8 2.1 convolution_convert_fusion.1
  876.2 300.6 %all-gather.9.cloned.1.call-done = bf16[8192,128]{1,0:T(8,128)(2,1)} async-done(((bf16[128,128]{1,0:T(8,128)(2,1)}), bf16[8192,128]{1,0:T(8,128)(2,1)}) %all-gather.9.cloned.1.call-update) | async-done | bytes 2097168 | tf_op jit(solution)/shard_map/all_gather | solution.py:135
  1176.7 302.3 %all-gather.15.cloned.1.call-done = bf16[8192,128]{1,0:T(8,128)(2,1)} async-done(((bf16[128,128]{1,0:T(8,128)(2,1)}), bf16[8192,128]{1,0:T(8,128)(2,1)}) %all-gather.15.cloned.1.call-update) | async-done | bytes 2097168 | tf_op jit(solution)/shard_map/all_gather | solution.py:136
  1479.1 40.4 %while.17 = (s32[]{:T(128)}, f32[1,2,128]{2,1,0:T(2,128)S(1)}, f32[1,2,128]{2,1,0:T(2,128)S(1)}, f32[1,2,128,128]{3,2,1,0:T(8,128)S(1)}, s32[8]{0:T(128)S(1)}, /...) while((s32[]{:T(128)}, f32[1,2,128]{2,1,0:T(2,128)S(1)}, ...), condition=%wide.region_8.9_spmd.clone, body=%wide.region_3.8_spmd.clone.sunk | while | flops 137504256 | bytes 4577019 | solution.py:151
  1479.1 0.6 dynamic_slice.37
  1480.3 0.4 select_reduce_fusion.3
  1481.1 1.3 fusion.90
  1482.5 1.4 fusion.93
  1484.1 0.6 dynamic_slice.37
  1486.2 1.3 fusion.90
  1487.5 1.4 fusion.93
  1489.2 0.6 dynamic_slice.37
  1491.2 1.3 fusion.90
  1492.6 1.4 fusion.93
  1494.2 0.6 dynamic_slice.37
  1496.3 1.3 fusion.90
  1497.6 1.4 fusion.93
  1499.3 0.6 dynamic_slice.37
  1501.3 1.3 fusion.90
  1502.7 1.4 fusion.93
  1504.3 0.6 dynamic_slice.37
  1506.4 1.3 fusion.90
  1507.7 1.4 fusion.93
  1509.4 0.6 dynamic_slice.37
  1511.4 1.3 fusion.90
  1512.8 1.4 fusion.93
  1514.4 0.6 dynamic_slice.37
  1516.5 1.3 fusion.90
  1517.8 1.4 fusion.93
  1519.5 2.5 fusion.72
  1522.3 0.5 fusion.48
  1523.1 258.5 %all-gather.17.cloned.1.call-done = bf16[256,4096]{0,1:T(8,128)(2,1)} async-done(((bf16[256,64]{0,1:T(8,128)(2,1)}), bf16[256,4096]{0,1:T(8,128)(2,1)}) %all-gather.17.cloned.1.call-update) | async-done | bytes 2097168 | tf_op jit(solution)/shard_map/all_gather | solution.py:183
  1781.6 3.4 convolution_convert_fusion
  1785.0 80.1 %reduce-scatter.2.cloned.1.call-done = bf16[132,512]{1,0:T(8,128)(2,1)} async-done(((bf16[132,4096]{1,0:T(8,128)(2,1)}), bf16[132,512]{1,0:T(8,128)(2,1)}) %reduce-scatter.2.cloned.1.call-update) | async-done | bytes 135184 | tf_op jit(solution)/shard_map/reduce_scatter | solution.py:186
  1865.1 1.6 slice.38
  1866.7 1.3 slice.39
  (120 shorter events, 10.1 us)
Async XLA Ops:
  7.2 3.6 copy-start
  7.2 262.6 %all-gather.7.cloned.1.call-start = ((), (), s32[]{:S(2)}) async-start(), calls=%async_computation.1 | async-start | bytes 1064960 | tf_op jit(solution)/shard_map/all_gather | solution.py:77
  7.9 560.6 %all-gather.13.cloned.1.call-start = ((), (), s32[]{:S(2)}) async-start(), calls=%async_computation.4 | async-start | bytes 1064960 | tf_op jit(solution)/shard_map/all_gather | solution.py:78
  8.7 865.2 %all-gather.11.cloned.1.call-start = ((), (), s32[]{:S(2)}) async-start(), calls=%async_computation.3 | async-start | bytes 2129920 | tf_op jit(solution)/shard_map/all_gather | solution.py:76
  9.4 1167.3 %all-gather.9.cloned.1.call-start = ((), (), s32[]{:S(2)}) async-start(), calls=%async_computation.2 | async-start | bytes 2129920 | tf_op jit(solution)/shard_map/all_gather | solution.py:135
  10.8 560.7 %copy-start.3 = (s32[4]{0:T(128)S(1)}, s32[4]{0:T(128)}, u32[]{:S(2)}) copy-start(s32[4]{0:T(128)} %param.16) | copy-start | bytes 52
  10.8 560.9 %copy-start.1 = (s32[128]{0:T(128)S(1)}, s32[128]{0:T(128)}, u32[]{:S(2)}) copy-start(s32[128]{0:T(128)} %param.17) | copy-start | bytes 1540
  272.1 1206.9 %all-gather.15.cloned.1.call-start = ((), (), s32[]{:S(2)}) async-start(), calls=%async_computation.5 | async-start | bytes 2129920 | tf_op jit(solution)/shard_map/all_gather | solution.py:136
  570.8 1210.7 %all-gather.17.cloned.1.call-start = ((), (), s32[]{:S(2)}) async-start(), calls=%async_computation.6 | async-start | bytes 2129920 | tf_op jit(solution)/shard_map/all_gather | solution.py:183
  571.4 1293.7 %reduce-scatter.2.cloned.1.call-start = ((), (), s32[]{:S(2)}) async-start(), calls=%async_computation.7 | async-start | bytes 1253376 | tf_op jit(solution)/shard_map/reduce_scatter | solution.py:186
  1519.5 2.8 copy-start.2
Sparse Core Ops, SparseCore 0:
  10.1 259.6 all-gather.6
  271.9 296.6 all-gather.12
  570.6 303.1 all-gather.10
  876.4 300.3 all-gather.8
  1178.7 300.3 all-gather.14
  1481.0 300.5 all-gather.16
  1785.1 79.9 reduce-scatter.1
where the time goes:
time: 1880 us; the launch traced here: 1870 us
  waiting for transfers between devices  1800 us (96%)
  matrix products  33.2 us (2%)
    all_gather x1, waiting for transfers between devices, on_device(): lax.all_gather(local_values, 'ctx', axis=0, tiled=True)  302 us
    all_gather x1, waiting for transfers between devices, on_device(): lax.all_gather(w_query, 'ctx', axis=0, tiled=True)  301 us
    all_gather x1, waiting for transfers between devices, on_device(): lax.all_gather(local_keys, 'ctx', axis=0, tiled=True)  301 us
    all_gather x1, waiting for transfers between devices, on_device(): lax.all_gather(value_matrix, 'ctx', axis=0, tiled=True)  296 us
    all_gather x1, waiting for transfers between devices, on_device(): lax.all_gather(key_matrix, 'ctx', axis=0, tiled=True)  259 us
    all_gather x1, waiting for transfers between devices, on_device(): lax.all_gather(w_out, 'ctx', axis=1, tiled=True)  259 us
    reduce_scatter x1, waiting for transfers between devices, on_device(): lax.psum_scatter(projected.astype(jnp.bfloat16), 'tp', scatter_dimension=...  80.1 us
  transfers between devices with their start and end apart: 7, of which 7 were waited for; matrix products, arithmetic and copies ran while one was open for 3% of the time, Pallas kernels for 0%

commit v1 on v0

--- a/solution.py
+++ b/solution.py
@@ -72,17 +72,20 @@
     device = lax.axis_index("ctx")
     request_ends = jnp.cumsum(lengths)
     inputs = jnp.concatenate([tokens, new_token_states], axis=0)
-    shard_pieces = (
-        lax.all_gather(w_query, "ctx", axis=0, tiled=True),
-        lax.all_gather(key_matrix, "ctx", axis=0, tiled=True),
-        lax.all_gather(value_matrix, "ctx", axis=0, tiled=True),
-    )
-    query_all, key_all, value_all = tuple(
-        (jnp.dot(inputs, weight, preferred_element_type=jnp.float32) for weight in shard_pieces)
-    )
-    query_all = query_all.astype(jnp.bfloat16)
-    key_all = key_all.astype(jnp.bfloat16)
-    value_all = value_all.astype(jnp.bfloat16)
+    joined = lax.all_gather(
+        jnp.concatenate([w_query, key_matrix, value_matrix, w_out.T], axis=1),
+        "ctx",
+        axis=0,
+        tiled=True,
+    )
+    qkv_width = query_width + 2 * kv_width
+    projected_all = jnp.dot(
+        inputs, joined[:, :qkv_width], preferred_element_type=jnp.float32
+    ).astype(jnp.bfloat16)
+    out_weight = joined[:, qkv_width:].T
+    query_all = projected_all[:, :query_width]
+    key_all = projected_all[:, query_width : query_width + kv_width]
+    value_all = projected_all[:, query_width + kv_width :]
     local_query = query_all[:local_rows]
     local_keys = key_all[:local_rows]
     local_values = value_all[:local_rows]
@@ -131,10 +134,11 @@
     )
     dec_heads = dec_query.reshape(request_count, kv_heads, query_group_count, head_dim)
     request_ids = jnp.arange(request_count, dtype=jnp.int32)
-    cache_keys, cache_values = (
-        lax.all_gather(local_keys, "ctx", axis=0, tiled=True),
-        lax.all_gather(local_values, "ctx", axis=0, tiled=True),
-    )
+    cache_both = lax.all_gather(
+        jnp.concatenate([local_keys, local_values], axis=1), "ctx", axis=0, tiled=True
+    )
+    cache_keys = cache_both[:, :kv_width]
+    cache_values = cache_both[:, kv_width:]
     total_rows = cache_keys.shape[0]
     shard_count = total_rows // local_rows
     limit = max(1, 1024 // local_rows)
@@ -180,7 +184,7 @@
     attended_all = jnp.concatenate([attended, dec_attn], axis=0)
     projected = jnp.dot(
         attended_all,
-        lax.all_gather(w_out, "ctx", axis=1, tiled=True),
+        out_weight,
         preferred_element_type=jnp.float32,
     )
     summed_rows = lax.psum_scatter(

time: 1880 us -> 757 us (0.40)
  waiting for transfers between devices: 1800 us -> 673 us
    all_gather x6 -> x2, waiting for transfers between devices: 1720 us -> 597 us  [the longest x1 308 us: on_device(): lax.all_gather(jnp.concatenate([local_keys, local_values], axis=1), 'ctx'...]
  transfers between devices with their start and end apart: 7 -> 3, of which waited for: 7 -> 3; matrix products, arithmetic and copies ran while one was open for 3% -> 1% of each run, Pallas kernels for 0% -> 0%
where the time goes in v1:
time: 757 us; the launch traced here: 756 us
  waiting for transfers between devices  673 us (89%)
  matrix products  24.9 us (3%)
  other arithmetic  24.7 us (3%)
  between operations  13.9 us (2%)
  local copies, waits for them, and re-layouts  12.5 us (2%)
    all_gather x1, waiting for transfers between devices, on_device(): lax.all_gather(jnp.concatenate([local_keys, local_values], axis=1), 'ctx'...  308 us
    all_gather x1, waiting for transfers between devices, on_device(): lax.all_gather(jnp.concatenate([w_query, key_matrix, value_matrix, w_out....  289 us
    reduce_scatter x1, waiting for transfers between devices, on_device(): lax.psum_scatter(projected.astype(jnp.bfloat16), 'tp', scatter_dimension=...  75.9 us
  transfers between devices with their start and end apart: 3, of which 3 were waited for; matrix products, arithmetic and copies ran while one was open for 1% of the time, Pallas kernels for 0%

profile of v1, /device:TPU:1, one launch (start us, length us, event | category | flops | bytes accessed | tf_op | source)
XLA Modules:
  0.0 755.6 jit_solution(10160451759107932689)
XLA Ops:
  7.2 1.5 pad_maximum_fusion
  8.8 289.3 %all-gather.3.cloned.1.call-done = bf16[4096,768]{1,0:T(8,128)(2,1)} async-done(((bf16[64,768]{1,0:T(8,128)(2,1)}), bf16[4096,768]{1,0:T(8,128)(2,1)}) %all-gather.3.cloned.1.call-update) | async-done | bytes 6291472 | tf_op jit(solution)/shard_map/all_gather | solution.py:75
  298.0 3.3 fusion.33
  301.3 0.6 fusion.85
  302.3 0.7 broadcast_multiply_fusion
  303.1 0.8 select_reduce_fusion.1
  304.5 1.3 convert_reduce_fusion.2
  306.2 308.1 %all-gather.5.cloned.1.call-done = bf16[8192,256]{1,0:T(8,128)(2,1)} async-done(((bf16[128,256]{1,0:T(8,128)(2,1)}), bf16[8192,256]{1,0:T(8,128)(2,1)}) %all-gather.5.cloned.1.call-update) | async-done | bytes 4194320 | tf_op jit(solution)/shard_map/all_gather | solution.py:137
  614.3 2.3 fusion.86
  617.0 2.0 fusion.57
  619.2 3.8 fusion.84
  623.0 43.6 %while.17 = (s32[]{:T(128)}, f32[1,2,128]{2,1,0:T(2,128)S(1)}, f32[1,2,128]{2,1,0:T(2,128)S(1)}, f32[1,2,128,128]{3,2,1,0:T(8,128)S(1)}, s32[8]{0:T(128)S(1)}, /...) while((s32[]{:T(128)}, f32[1,2,128]{2,1,0:T(2,128)S(1)}, ...), condition=%wide.region_8.9_spmd.clone, body=%wide.region_3.8_spmd.clone.sunk | while | flops 137504256 | bytes 4577331 | solution.py:155
  623.0 0.6 dynamic_slice.37
  624.2 1.0 select_reduce_fusion.3
  625.3 1.0 compare_and_fusion.2
  626.8 1.4 fusion.100
  628.4 0.6 dynamic_slice.37
  629.7 1.0 select_reduce_fusion.3
  630.8 1.0 compare_and_fusion.2
  632.2 1.4 fusion.100
  633.9 0.6 dynamic_slice.37
  635.1 1.0 select_reduce_fusion.3
  636.3 1.0 compare_and_fusion.2
  637.7 1.4 fusion.100
  639.3 0.6 dynamic_slice.37
  640.6 1.0 select_reduce_fusion.3
  641.7 1.0 compare_and_fusion.2
  643.1 1.4 fusion.100
  644.8 0.6 dynamic_slice.37
  646.1 1.0 select_reduce_fusion.3
  647.2 1.0 compare_and_fusion.2
  648.6 1.4 fusion.100
  650.3 0.6 dynamic_slice.37
  651.5 1.0 select_reduce_fusion.3
  652.6 1.0 compare_and_fusion.2
  654.0 1.4 fusion.100
  655.7 0.6 dynamic_slice.37
  657.0 1.0 select_reduce_fusion.3
  658.1 1.0 compare_and_fusion.2
  659.5 1.4 fusion.100
  661.2 0.6 dynamic_slice.37
  662.4 1.0 select_reduce_fusion.3
  663.6 1.0 compare_and_fusion.2
  665.0 1.4 fusion.100
  666.7 3.5 convolution_convert_fusion
  670.2 75.9 %reduce-scatter.2.cloned.1.call-done = bf16[132,512]{1,0:T(8,128)(2,1)} async-done(((bf16[132,4096]{1,0:T(8,128)(2,1)}), bf16[132,512]{1,0:T(8,128)(2,1)}) %reduce-scatter.2.cloned.1.call-update) | async-done | bytes 135184 | tf_op jit(solution)/shard_map/reduce_scatter | solution.py:190
  746.2 1.6 slice.60
  747.8 1.3 slice.61
  (129 shorter events, 7.8 us)
Async XLA Ops:
  7.2 290.9 %all-gather.3.cloned.1.call-start = ((), (), s32[]{:S(2)}) async-start(), calls=%async_computation.1 | async-start | bytes 6389760 | tf_op jit(solution)/shard_map/all_gather | solution.py:75
  8.7 293.4 %copy-start = (s32[4]{0:T(128)S(1)}, s32[4]{0:T(128)}, u32[]{:S(2)}) copy-start(s32[4]{0:T(128)} %param.16) | copy-start | bytes 52
  8.7 605.6 %all-gather.5.cloned.1.call-start = ((), (), s32[]{:S(2)}) async-start(), calls=%async_computation.2 | async-start | bytes 4259840 | tf_op jit(solution)/shard_map/all_gather | solution.py:137
  302.0 444.2 %reduce-scatter.2.cloned.1.call-start = ((), (), s32[]{:S(2)}) async-start(), calls=%async_computation.3 | async-start | bytes 1253376 | tf_op jit(solution)/shard_map/reduce_scatter | solution.py:190
  623.0 3.4 copy-start.1
  626.7 1.6 copy-start.2
  628.4 3.4 copy-start.1
  632.2 1.6 copy-start.2
  633.9 3.4 copy-start.1
  637.7 1.6 copy-start.2
  639.3 3.4 copy-start.1
  643.1 1.6 copy-start.2
  644.8 3.4 copy-start.1
  648.6 1.6 copy-start.2
  650.2 3.4 copy-start.1
  654.0 1.6 copy-start.2
  655.7 3.4 copy-start.1
  659.5 1.6 copy-start.2
  661.2 3.4 copy-start.1
  665.0 1.6 copy-start.2
Sparse Core Ops, SparseCore 0:
  10.7 287.3 all-gather.2
  302.1 312.1 all-gather.4
  670.4 75.7 reduce-scatter.1

commit v2 on v1

--- a/solution.py
+++ b/solution.py
@@ -1,14 +1,75 @@
+import functools
 import math
 
 import jax
 import jax.numpy as jnp
 from jax import lax
+from jax.experimental import pallas as pl
+from jax.experimental.pallas import tpu as pltpu
 from jax.sharding import PartitionSpec as P
 
 HEAD_SIZE = 128
 
 
 floor_value = -1e30
+
+
+def _gather_kernel(count, piece_ref, out_ref, send_sems, recv_sems, local_sem):
+    me = lax.axis_index("ctx")
+    mesh_ids = pl.DeviceIdType.MESH
+    barrier = pltpu.get_barrier_semaphore()
+
+    def greet(step, carry):
+        peer = lax.rem(me + step, count)
+        pl.semaphore_signal(barrier, 1, device_id={"ctx": peer}, device_id_type=mesh_ids)
+        return carry
+
+    lax.fori_loop(1, count, greet, 0)
+    pl.semaphore_wait(barrier, count - 1)
+    own = pltpu.make_async_copy(piece_ref, out_ref.at[me], local_sem)
+    own.start()
+
+    def remote(peer, slot):
+        return pltpu.make_async_remote_copy(
+            src_ref=piece_ref,
+            dst_ref=out_ref.at[slot],
+            send_sem=send_sems.at[peer],
+            recv_sem=recv_sems.at[slot],
+            device_id={"ctx": peer},
+            device_id_type=mesh_ids,
+        )
+
+    def send(step, carry):
+        remote(lax.rem(me + step, count), me).start()
+        return carry
+
+    lax.fori_loop(1, count, send, 0)
+
+    def finish(step, carry):
+        peer = lax.rem(me + step, count)
+        remote(peer, me).wait_send()
+        remote(peer, peer).wait_recv()
+        return carry
+
+    lax.fori_loop(1, count, finish, 0)
+    own.wait()
+
+
+def gather_ctx(piece, count, kernel_id):
+    rows, cols = piece.shape
+    gathered = pl.pallas_call(
+        functools.partial(_gather_kernel, count),
+        out_shape=jax.ShapeDtypeStruct((count, rows, cols), piece.dtype),
+        in_specs=[pl.BlockSpec(memory_space=pl.ANY)],
+        out_specs=pl.BlockSpec(memory_space=pl.ANY),
+        scratch_shapes=[
+            pltpu.SemaphoreType.DMA((count,)),
+            pltpu.SemaphoreType.DMA((count,)),
+            pltpu.SemaphoreType.DMA(()),
+        ],
+        compiler_params=pltpu.CompilerParams(collective_id=kernel_id, has_side_effects=True),
+    )(piece)
+    return gathered.reshape(count * rows, cols)
 
 
 def initial_positions(block_map, first_row, row_count, block_rows):
@@ -58,7 +119,7 @@
 
 
 def on_device(
-    tokens, new_token_states, w_query, key_matrix, value_matrix, w_out, lengths, block_map
+    ctx_count, tokens, new_token_states, w_query, key_matrix, value_matrix, w_out, lengths, block_map
 ):
     local_rows = tokens.shape[0]
     block_rows = local_rows // 2
@@ -72,11 +133,8 @@
     device = lax.axis_index("ctx")
     request_ends = jnp.cumsum(lengths)
     inputs = jnp.concatenate([tokens, new_token_states], axis=0)
-    joined = lax.all_gather(
-        jnp.concatenate([w_query, key_matrix, value_matrix, w_out.T], axis=1),
-        "ctx",
-        axis=0,
-        tiled=True,
+    joined = gather_ctx(
+        jnp.concatenate([w_query, key_matrix, value_matrix, w_out.T], axis=1), ctx_count, 0
     )
     qkv_width = query_width + 2 * kv_width
     projected_all = jnp.dot(
@@ -134,8 +192,8 @@
     )
     dec_heads = dec_query.reshape(request_count, kv_heads, query_group_count, head_dim)
     request_ids = jnp.arange(request_count, dtype=jnp.int32)
-    cache_both = lax.all_gather(
-        jnp.concatenate([local_keys, local_values], axis=1), "ctx", axis=0, tiled=True
+    cache_both = gather_ctx(
+        jnp.concatenate([local_keys, local_values], axis=1), ctx_count, 1
     )
     cache_keys = cache_both[:, :kv_width]
     cache_values = cache_both[:, kv_width:]
@@ -196,7 +254,7 @@
 
 def solution(mesh):
     return jax.shard_map(
-        on_device,
+        functools.partial(on_device, mesh.shape["ctx"]),
         mesh=mesh,
         in_specs=(
             P("ctx", None),

time: 757 us -> 397 us (0.52)
  waiting for transfers between devices: 673 us -> 46.1 us
  Pallas kernels: 0 us -> 264 us
    all_gather x2 -> x0, waiting for transfers between devices: 597 us -> none  [the longest x1 308 us: on_device(): lax.all_gather(jnp.concatenate([local_keys, local_values], axis=1), 'ctx'...]
    pallas_call x0 -> x2, Pallas kernels: none -> 264 us  [gather_ctx(): pl.pallas_call(functools.partial(_gather_kernel, count), out_shape=jax.Sh...]
    reduce_scatter x1, waiting for transfers between devices: 75.9 us -> 46.1 us  [on_device(): lax.psum_scatter(projected.astype(jnp.bfloat16), 'tp', scatter_dimension=...]
  transfers between devices with their start and end apart: 3 -> 1, of which waited for: 3 -> 1; matrix products, arithmetic and copies ran while one was open for 1% -> 0% of each run, Pallas kernels for 0% -> 0%
where the time goes in v2:
time: 397 us; the launch traced here: 396 us
  Pallas kernels  264 us (66%)
  waiting for transfers between devices  46.1 us (12%)
  other arithmetic  23 us (6%)
  matrix products  23 us (6%)
  local copies, waits for them, and re-layouts  19 us (5%)
  between operations  14.2 us (4%)
  loops' own time  5.96 us (2%)
    pallas_call x2, Pallas kernels, gather_ctx(): pl.pallas_call(functools.partial(_gather_kernel, count), out_shape=jax.Sh...  264 us
    reduce_scatter x1, waiting for transfers between devices, on_device(): lax.psum_scatter(projected.astype(jnp.bfloat16), 'tp', scatter_dimension=...  46.1 us
    dot_general x8, matrix products, attend(): jnp.einsum('gjtk,kgd->gjtd', weights.astype(jnp.bfloat16), value_piece.re...  11 us
    dynamic_slice x8, local copies, waits for them, and re-layouts, on_device(): lax.scan(key_step, start_state, jnp.arange(total_rows // step_rows, dtype...  10.5 us
    reduce_sum x9, other arithmetic, initial_positions(): jnp.sum(jnp.where(block_ids[:, None] == table_ids[None, :], block_map[Non...  8.96 us
  transfers between devices with their start and end apart: 1, of which 1 were waited for; matrix products, arithmetic and copies ran while one was open for 0% of the time, Pallas kernels for 0%

profile of v2, /device:TPU:1, one launch (start us, length us, event | category | flops | bytes accessed | tf_op | source)
XLA Modules:
  0.0 395.7 jit_solution(4761800311158468265)
XLA Ops:
  7.2 1.5 pad_maximum_fusion.piece_ref
  8.7 159.4 %shard_map.95 = bf16[64,64,768]{2,1,0:T(8,128)(2,1)} custom-call(bf16[64,768]{1,0:T(8,128)(2,1)} %pad_maximum_fusion.piece_ref), custom_call_target="tpu_custom_call" | custom-call | tf_op jit(solution)/shard_map/pallas_call | solution.py:60
  168.1 2.9 fusion.33
  171.1 0.6 fusion.85
  171.8 105.0 %shard_map.96 = bf16[64,128,256]{2,1,0:T(8,128)(2,1)} custom-call(bf16[128,256]{1,0:T(8,128)(2,1)} %get-tuple-element.299.piece_ref), custom_call_target="tpu_custom_call" | custom-call | tf_op jit(solution)/shard_map/pallas_call | solution.py:60
  276.9 0.7 broadcast_multiply_fusion
  278.0 3.9 fusion.84
  281.9 0.7 fusion.86
  283.2 2.1 fusion.57
  285.5 0.8 select_reduce_fusion.1
  286.3 0.6 convert_reduce_fusion.2
  287.5 48.8 %while.17 = (s32[]{:T(128)}, f32[1,2,128]{2,1,0:T(2,128)S(1)}, f32[1,2,128]{2,1,0:T(2,128)S(1)}, f32[1,2,128,128]{3,2,1,0:T(8,128)S(1)}, s32[8]{0:T(128)}, /*ind...) while((s32[]{:T(128)}, f32[1,2,128]{2,1,0:T(2,128)S(1)}, ...), condition=%wide.region_8.9_spmd.clone, body=%wide.region_3.8_spmd.clone.sunk | while | flops 137504256 | bytes 4581171 | solution.py:213
  287.5 1.3 dynamic_slice.37
  289.4 1.0 select_reduce_fusion.3
  290.5 0.9 compare_and_fusion.2
  291.9 1.4 fusion.100
  293.6 1.3 dynamic_slice.37
  295.5 1.0 select_reduce_fusion.3
  296.6 0.9 compare_and_fusion.2
  298.0 1.4 fusion.100
  299.7 1.3 dynamic_slice.37
  301.6 1.0 select_reduce_fusion.3
  302.7 0.9 compare_and_fusion.2
  304.1 1.4 fusion.100
  305.8 1.3 dynamic_slice.37
  307.7 1.0 select_reduce_fusion.3
  308.9 0.9 compare_and_fusion.2
  310.2 1.4 fusion.100
  311.9 1.3 dynamic_slice.37
  313.8 1.0 select_reduce_fusion.3
  315.0 0.9 compare_and_fusion.2
  316.3 1.4 fusion.100
  318.0 1.3 dynamic_slice.37
  319.9 1.0 select_reduce_fusion.3
  321.1 0.9 compare_and_fusion.2
  322.4 1.4 fusion.100
  324.1 1.3 dynamic_slice.37
  326.0 1.0 select_reduce_fusion.3
  327.2 0.9 compare_and_fusion.2
  328.5 1.4 fusion.100
  330.2 1.3 dynamic_slice.37
  332.1 1.0 select_reduce_fusion.3
  333.3 0.9 compare_and_fusion.2
  334.6 1.4 fusion.100
  336.4 3.5 convolution_convert_fusion
  339.9 46.1 %reduce-scatter.2.cloned.1.call-done = bf16[132,512]{1,0:T(8,128)(2,1)} async-done(((bf16[132,4096]{1,0:T(8,128)(2,1)}), bf16[132,512]{1,0:T(8,128)(2,1)}) %reduce-scatter.2.cloned.1.call-update) | async-done | bytes 135184 | tf_op jit(solution)/shard_map/reduce_scatter | solution.py:248
  386.0 1.6 slice.60
  387.5 1.3 slice.61
  (131 shorter events, 7.7 us)
Async XLA Ops:
  7.2 378.8 %reduce-scatter.2.cloned.1.call-start = ((), (), s32[]{:S(2)}) async-start(), calls=%async_computation.1 | async-start | bytes 1253376 | tf_op jit(solution)/shard_map/reduce_scatter | solution.py:248
  8.7 159.5 %copy-start.3 = (bf16[128,4096]{1,0:T(8,128)(2,1)S(1)}, bf16[128,4096]{1,0:T(8,128)(2,1)}, u32[]{:S(2)}) copy-start(bf16[128,4096]{1,0:T(8,128)(2,1)} %param.10) | copy-start | bytes 3145732
  8.7 159.5 %copy-start.4 = (bf16[4,4096]{1,0:T(4,128)(2,1)S(1)}, bf16[4,4096]{1,0:T(4,128)(2,1)}, u32[]{:S(2)}) copy-start(bf16[4,4096]{1,0:T(4,128)(2,1)} %param.11) | copy-start | bytes 98308
  171.7 105.0 %copy-start.5 = (s32[4]{0:T(128)S(1)}, s32[4]{0:T(128)}, u32[]{:S(2)}) copy-start(s32[4]{0:T(128)} %param.16) | copy-start | bytes 52
  278.0 4.0 copy-start
  287.5 4.0 %copy-start.1 = (s32[128]{0:T(128)}, s32[128]{0:T(128)S(1)}, u32[]{:S(2)}) copy-start(s32[128]{0:T(128)S(1)} %get-tuple-element.427) | copy-start | bytes 1540 | tf_op jit(solution)/shard_map/while
  291.9 1.6 copy-start.2
  293.5 4.1 %copy-start.1 = (s32[128]{0:T(128)}, s32[128]{0:T(128)S(1)}, u32[]{:S(2)}) copy-start(s32[128]{0:T(128)S(1)} %get-tuple-element.427) | copy-start | bytes 1540 | tf_op jit(solution)/shard_map/while
  298.0 1.6 copy-start.2
  299.7 4.1 %copy-start.1 = (s32[128]{0:T(128)}, s32[128]{0:T(128)S(1)}, u32[]{:S(2)}) copy-start(s32[128]{0:T(128)S(1)} %get-tuple-element.427) | copy-start | bytes 1540 | tf_op jit(solution)/shard_map/while
  304.1 1.6 copy-start.2
  305.8 4.1 %copy-start.1 = (s32[128]{0:T(128)}, s32[128]{0:T(128)S(1)}, u32[]{:S(2)}) copy-start(s32[128]{0:T(128)S(1)} %get-tuple-element.427) | copy-start | bytes 1540 | tf_op jit(solution)/shard_map/while
  310.2 1.6 copy-start.2
  311.9 4.1 %copy-start.1 = (s32[128]{0:T(128)}, s32[128]{0:T(128)S(1)}, u32[]{:S(2)}) copy-start(s32[128]{0:T(128)S(1)} %get-tuple-element.427) | copy-start | bytes 1540 | tf_op jit(solution)/shard_map/while
  316.3 1.6 copy-start.2
  318.0 4.1 %copy-start.1 = (s32[128]{0:T(128)}, s32[128]{0:T(128)S(1)}, u32[]{:S(2)}) copy-start(s32[128]{0:T(128)S(1)} %get-tuple-element.427) | copy-start | bytes 1540 | tf_op jit(solution)/shard_map/while
  322.4 1.6 copy-start.2
  324.1 4.1 %copy-start.1 = (s32[128]{0:T(128)}, s32[128]{0:T(128)S(1)}, u32[]{:S(2)}) copy-start(s32[128]{0:T(128)S(1)} %get-tuple-element.427) | copy-start | bytes 1540 | tf_op jit(solution)/shard_map/while
  328.5 1.6 copy-start.2
  330.2 4.1 %copy-start.1 = (s32[128]{0:T(128)}, s32[128]{0:T(128)S(1)}, u32[]{:S(2)}) copy-start(s32[128]{0:T(128)S(1)} %get-tuple-element.427) | copy-start | bytes 1540 | tf_op jit(solution)/shard_map/while
  334.6 1.6 copy-start.2
Sparse Core Ops, SparseCore 0:
  340.0 45.8 reduce-scatter.1

commit v3 on v2

--- a/solution.py
+++ b/solution.py
@@ -14,62 +14,123 @@
 floor_value = -1e30
 
 
-def _gather_kernel(count, piece_ref, out_ref, send_sems, recv_sems, local_sem):
+def _gather_kernel(
+    z_count, p_count, piece_ref, out_ref, z_send, z_recv, p_send, p_recv, local_sem
+):
     me = lax.axis_index("ctx")
+    z_me = me // p_count
+    p_me = lax.rem(me, p_count)
     mesh_ids = pl.DeviceIdType.MESH
     barrier = pltpu.get_barrier_semaphore()
 
-    def greet(step, carry):
-        peer = lax.rem(me + step, count)
-        pl.semaphore_signal(barrier, 1, device_id={"ctx": peer}, device_id_type=mesh_ids)
-        return carry
-
-    lax.fori_loop(1, count, greet, 0)
-    pl.semaphore_wait(barrier, count - 1)
-    own = pltpu.make_async_copy(piece_ref, out_ref.at[me], local_sem)
+    def z_peer(step):
+        return lax.rem(z_me + step, z_count)
+
+    def p_peer(step):
+        return lax.rem(p_me + step, p_count)
+
+    def greet_z(step, carry):
+        target = z_peer(step) * p_count + p_me
+        pl.semaphore_signal(barrier, 1, device_id={"ctx": target}, device_id_type=mesh_ids)
+        return carry
+
+    def greet_p(step, carry):
+        target = z_me * p_count + p_peer(step)
+        pl.semaphore_signal(barrier, 1, device_id={"ctx": target}, device_id_type=mesh_ids)
+        return carry
+
+    lax.fori_loop(1, z_count, greet_z, 0)
+    lax.fori_loop(1, p_count, greet_p, 0)
+    pl.semaphore_wait(barrier, z_count + p_count - 2)
+    own = pltpu.make_async_copy(piece_ref, out_ref.at[p_me, z_me], local_sem)
     own.start()
 
-    def remote(peer, slot):
+    def z_copy(peer, slot):
         return pltpu.make_async_remote_copy(
             src_ref=piece_ref,
+            dst_ref=out_ref.at[p_me, slot],
+            send_sem=z_send.at[peer],
+            recv_sem=z_recv.at[slot],
+            device_id={"ctx": peer * p_count + p_me},
+            device_id_type=mesh_ids,
+        )
+
+    def z_start(step, carry):
+        z_copy(z_peer(step), z_me).start()
+        return carry
+
+    def z_finish(step, carry):
+        peer = z_peer(step)
+        z_copy(peer, z_me).wait_send()
+        z_copy(peer, peer).wait_recv()
+        return carry
+
+    lax.fori_loop(1, z_count, z_start, 0)
+    lax.fori_loop(1, z_count, z_finish, 0)
+    own.wait()
+
+    def p_copy(peer, slot):
+        return pltpu.make_async_remote_copy(
+            src_ref=out_ref.at[slot],
             dst_ref=out_ref.at[slot],
-            send_sem=send_sems.at[peer],
-            recv_sem=recv_sems.at[slot],
-            device_id={"ctx": peer},
+            send_sem=p_send.at[peer],
+            recv_sem=p_recv.at[slot],
+            device_id={"ctx": z_me * p_count + peer},
             device_id_type=mesh_ids,
         )
 
-    def send(step, carry):
-        remote(lax.rem(me + step, count), me).start()
-        return carry
-
-    lax.fori_loop(1, count, send, 0)
-
-    def finish(step, carry):
-        peer = lax.rem(me + step, count)
-        remote(peer, me).wait_send()
-        remote(peer, peer).wait_recv()
-        return carry
-
-    lax.fori_loop(1, count, finish, 0)
-    own.wait()
-
-
-def gather_ctx(piece, count, kernel_id):
+    def p_start(step, carry):
+        p_copy(p_peer(step), p_me).start()
+        return carry
+
+    def p_finish(step, carry):
+        peer = p_peer(step)
+        p_copy(peer, p_me).wait_send()
+        p_copy(peer, peer).wait_recv()
+        return carry
+
+    lax.fori_loop(1, p_count, p_start, 0)
+    lax.fori_loop(1, p_count, p_finish, 0)
+
+
+def gather_ctx(piece, layout, kernel_id):
+    z_count, p_count = layout
     rows, cols = piece.shape
     gathered = pl.pallas_call(
-        functools.partial(_gather_kernel, count),
-        out_shape=jax.ShapeDtypeStruct((count, rows, cols), piece.dtype),
+        functools.partial(_gather_kernel, z_count, p_count),
+        out_shape=jax.ShapeDtypeStruct((p_count, z_count, rows, cols), piece.dtype),
         in_specs=[pl.BlockSpec(memory_space=pl.ANY)],
         out_specs=pl.BlockSpec(memory_space=pl.ANY),
         scratch_shapes=[
-            pltpu.SemaphoreType.DMA((count,)),
-            pltpu.SemaphoreType.DMA((count,)),
+            pltpu.SemaphoreType.DMA((z_count,)),
+            pltpu.SemaphoreType.DMA((z_count,)),
+            pltpu.SemaphoreType.DMA((p_count,)),
+            pltpu.SemaphoreType.DMA((p_count,)),
             pltpu.SemaphoreType.DMA(()),
         ],
         compiler_params=pltpu.CompilerParams(collective_id=kernel_id, has_side_effects=True),
     )(piece)
-    return gathered.reshape(count * rows, cols)
+    return gathered.transpose(1, 0, 2, 3).reshape(z_count * p_count * rows, cols)
+
+
+def ctx_layout(mesh):
+    count = mesh.shape["ctx"]
+    column = mesh.devices.transpose(
+        mesh.axis_names.index("ctx"), mesh.axis_names.index("tp")
+    )[:, 0]
+    try:
+        planes = [device.coords[2] for device in column]
+    except (AttributeError, IndexError, TypeError):
+        return (count, 1)
+    p_count = 1
+    while p_count < count and planes[p_count] == planes[0]:
+        p_count += 1
+    if count % p_count:
+        return (count, 1)
+    for index in range(count):
+        if planes[index] != planes[(index // p_count) * p_count]:
+            return (count, 1)
+    return (count // p_count, p_count)
 
 
 def initial_positions(block_map, first_row, row_count, block_rows):
@@ -119,7 +180,7 @@
 
 
 def on_device(
-    ctx_count, tokens, new_token_states, w_query, key_matrix, value_matrix, w_out, lengths, block_map
+    layout, tokens, new_token_states, w_query, key_matrix, value_matrix, w_out, lengths, block_map
 ):
     local_rows = tokens.shape[0]
     block_rows = local_rows // 2
@@ -134,7 +195,7 @@
     request_ends = jnp.cumsum(lengths)
     inputs = jnp.concatenate([tokens, new_token_states], axis=0)
     joined = gather_ctx(
-        jnp.concatenate([w_query, key_matrix, value_matrix, w_out.T], axis=1), ctx_count, 0
+        jnp.concatenate([w_query, key_matrix, value_matrix, w_out.T], axis=1), layout, 0
     )
     qkv_width = query_width + 2 * kv_width
     projected_all = jnp.dot(
@@ -193,7 +254,7 @@
     dec_heads = dec_query.reshape(request_count, kv_heads, query_group_count, head_dim)
     request_ids = jnp.arange(request_count, dtype=jnp.int32)
     cache_both = gather_ctx(
-        jnp.concatenate([local_keys, local_values], axis=1), ctx_count, 1
+        jnp.concatenate([local_keys, local_values], axis=1), layout, 1
     )
     cache_keys = cache_both[:, :kv_width]
     cache_values = cache_both[:, kv_width:]
@@ -254,7 +315,7 @@
 
 def solution(mesh):
     return jax.shard_map(
-        functools.partial(on_device, mesh.shape["ctx"]),
+        functools.partial(on_device, ctx_layout(mesh)),
         mesh=mesh,
         in_specs=(
             P("ctx", None),

time: 397 us -> 303 us (0.76)
  Pallas kernels: 264 us -> 166 us
  local copies, waits for them, and re-layouts: 19 us -> 28.8 us
  waiting for transfers between devices: 46.1 us -> 42.1 us
    pallas_call x2, Pallas kernels: 264 us -> 166 us  [gather_ctx(): pl.pallas_call(functools.partial(_gather_kernel, z_count, p_count), out_s...]
    transpose x0 -> x2, local copies, waits for them, and re-layouts: none -> 8 us  [gather_ctx(): gathered.transpose(1, 0, 2, 3).reshape(z_count * p_count * rows, cols)]
    reduce_scatter x1, waiting for transfers between devices: 46.1 us -> 42.1 us  [on_device(): lax.psum_scatter(projected.astype(jnp.bfloat16), 'tp', scatter_dimension=...]
where the time goes in v3:
time: 303 us; the launch traced here: 301 us
  Pallas kernels  166 us (55%)
  waiting for transfers between devices  42.1 us (14%)
  local copies, waits for them, and re-layouts  28.8 us (10%)
  other arithmetic  23 us (8%)
  matrix products  20.8 us (7%)
  between operations  14.2 us (5%)
  loops' own time  5.96 us (2%)
    pallas_call x2, Pallas kernels, gather_ctx(): pl.pallas_call(functools.partial(_gather_kernel, z_count, p_count), out_s...  166 us
    reduce_scatter x1, waiting for transfers between devices, on_device(): lax.psum_scatter(projected.astype(jnp.bfloat16), 'tp', scatter_dimension=...  42.1 us
    dot_general x8, matrix products, attend(): jnp.einsum('gjtk,kgd->gjtd', weights.astype(jnp.bfloat16), value_piece.re...  11 us
    dynamic_slice x8, local copies, waits for them, and re-layouts, on_device(): lax.scan(key_step, start_state, jnp.arange(total_rows // step_rows, dtype...  10.5 us
    reduce_sum x9, other arithmetic, initial_positions(): jnp.sum(jnp.where(block_ids[:, None] == table_ids[None, :], block_map[Non...  8.96 us
    transpose x2, local copies, waits for them, and re-layouts, gather_ctx(): gathered.transpose(1, 0, 2, 3).reshape(z_count * p_count * rows, cols)  8 us
    and x8, other arithmetic, attend(): (key_request[None, :] == token_request[:, None]) & (key_pos[None, :] <= t...  7.55 us
  transfers between devices with their start and end apart: 1, of which 1 were waited for; matrix products, arithmetic and copies ran while one was open for 0% of the time, Pallas kernels for 0%

profile of v3, /device:TPU:1, one launch (start us, length us, event | category | flops | bytes accessed | tf_op | source)
XLA Modules:
  0.0 300.7 jit_solution(15803452864927730265)
XLA Ops:
  7.2 1.5 pad_maximum_fusion.piece_ref
  8.7 99.7 %shard_map.95 = bf16[8,8,64,768]{3,2,1,0:T(8,128)(2,1)} custom-call(bf16[64,768]{1,0:T(8,128)(2,1)} %pad_maximum_fusion.piece_ref), custom_call_target="tpu_custom_call" | custom-call | tf_op jit(solution)/shard_map/pallas_call | solution.py:99
  108.4 3.3 %copy.47 = bf16[8,8,64,768]{3,2,1,0:T(8,128)(2,1)S(1)} copy(bf16[8,8,64,768]{3,2,0,1:T(8,128)(2,1)} %bitcast.133) | data formatting | bytes 12582912 | tf_op jit(solution)/shard_map/transpose | solution.py:113
  111.7 0.8 fusion.33
  112.5 1.9 copy-done.1
  115.0 66.1 %shard_map.96 = bf16[8,8,128,256]{3,2,1,0:T(8,128)(2,1)} custom-call(bf16[128,256]{1,0:T(8,128)(2,1)} %get-tuple-element.299.piece_ref), custom_call_target="tpu_custom_call" | custom-call | tf_op jit(solution)/shard_map/pallas_call | solution.py:99
  181.1 4.7 %copy.48 = bf16[8,8,128,256]{3,2,1,0:T(8,128)(2,1)} copy(bf16[8,8,128,256]{3,2,0,1:T(8,128)(2,1)} %bitcast.137) | data formatting | bytes 8388608 | tf_op jit(solution)/shard_map/transpose | solution.py:113
  187.1 3.9 %fusion.84 = (bf16[8192,128]{1,0:T(8,128)(2,1)}, bf16[8192,128]{1,0:T(8,128)(2,1)S(1)}) fusion(bf16[8192,256]{1,0:T(8,128)(2,1)} %bitcast.134), kind=kLoop, calls=%fused_computation.112 | loop fusion | bytes 8388608 | tf_op jit(solution)/shard_map/slice | solution.py:260
  191.0 0.7 fusion.86
  192.3 2.1 fusion.57
  194.6 0.8 select_reduce_fusion.1
  196.6 48.8 %while.17 = (s32[]{:T(128)}, f32[1,2,128]{2,1,0:T(2,128)S(1)}, f32[1,2,128]{2,1,0:T(2,128)S(1)}, f32[1,2,128,128]{3,2,1,0:T(8,128)S(1)}, s32[8]{0:T(128)}, /*ind...) while((s32[]{:T(128)}, f32[1,2,128]{2,1,0:T(2,128)S(1)}, ...), condition=%wide.region_8.9_spmd.clone, body=%wide.region_3.8_spmd.clone.sunk | while | flops 137504256 | bytes 4581171 | solution.py:274
  196.6 1.3 dynamic_slice.37
  198.5 1.0 select_reduce_fusion.3
  199.6 0.9 compare_and_fusion.2
  201.0 1.4 fusion.100
  202.7 1.3 dynamic_slice.37
  204.6 1.0 select_reduce_fusion.3
  205.7 0.9 compare_and_fusion.2
  207.1 1.4 fusion.100
  208.8 1.3 dynamic_slice.37
  210.7 1.0 select_reduce_fusion.3
  211.9 0.9 compare_and_fusion.2
  213.2 1.4 fusion.100
  214.9 1.3 dynamic_slice.37
  216.8 1.0 select_reduce_fusion.3
  218.0 0.9 compare_and_fusion.2
  219.3 1.4 fusion.100
  221.0 1.3 dynamic_slice.37
  222.9 1.0 select_reduce_fusion.3
  224.1 0.9 compare_and_fusion.2
  225.4 1.4 fusion.100
  227.1 1.3 dynamic_slice.37
  229.0 1.0 select_reduce_fusion.3
  230.2 0.9 compare_and_fusion.2
  231.5 1.4 fusion.100
  233.2 1.3 dynamic_slice.37
  235.1 1.0 select_reduce_fusion.3
  236.3 0.9 compare_and_fusion.2
  237.6 1.4 fusion.100
  239.3 1.3 dynamic_slice.37
  241.2 1.0 select_reduce_fusion.3
  242.4 0.9 compare_and_fusion.2
  243.7 1.4 fusion.100
  245.5 3.5 %convolution_convert_fusion = bf16[132,4096]{1,0:T(8,128)(2,1)} fusion(bf16[4096,768]{1,0:T(8,128)(2,1)} %bitcast.139, bf16[4,256]{0,1:T(8,128)(2,1)S(1)} %copy.53, bf16[128,256]{0,1:T(8,128)(2,1)S(1)} %bitcast.142), kind=kOutput, calls=%fused_computation.47 | convolution fusion | flops 277499904 | bytes 3246080 | tf_op jit(solution)/shard_map/dot_general | solution.py:304
  249.0 42.1 %reduce-scatter.2.cloned.1.call-done = bf16[132,512]{1,0:T(8,128)(2,1)} async-done(((bf16[132,4096]{1,0:T(8,128)(2,1)}), bf16[132,512]{1,0:T(8,128)(2,1)}) %reduce-scatter.2.cloned.1.call-update) | async-done | bytes 135184 | tf_op jit(solution)/shard_map/reduce_scatter | solution.py:309
  291.0 1.6 slice.60
  292.6 1.3 slice.61
  (135 shorter events, 9.6 us)
Async XLA Ops:
  7.2 283.9 %reduce-scatter.2.cloned.1.call-start = ((), (), s32[]{:S(2)}) async-start(), calls=%async_computation.1 | async-start | bytes 1253376 | tf_op jit(solution)/shard_map/reduce_scatter | solution.py:309
  108.4 3.3 %copy-start.4 = (bf16[128,4096]{1,0:T(8,128)(2,1)S(1)}, bf16[128,4096]{1,0:T(8,128)(2,1)}, u32[]{:S(2)}) copy-start(bf16[128,4096]{1,0:T(8,128)(2,1)} %param.10) | copy-start | bytes 3145732
  108.4 3.3 %copy-start.5 = (bf16[4,4096]{1,0:T(4,128)(2,1)S(1)}, bf16[4,4096]{1,0:T(4,128)(2,1)}, u32[]{:S(2)}) copy-start(bf16[4,4096]{1,0:T(4,128)(2,1)} %param.11) | copy-start | bytes 98308
  111.7 2.7 copy-start.1
  181.1 4.7 %copy-start.6 = (s32[4]{0:T(128)S(1)}, s32[4]{0:T(128)}, u32[]{:S(2)}) copy-start(s32[4]{0:T(128)} %param.16) | copy-start | bytes 52
  187.1 4.0 %copy-start = (bf16[8,8,128,256]{3,2,1,0:T(8,128)(2,1)S(1)}, bf16[8,8,128,256]{3,2,1,0:T(8,128)(2,1)}, u32[]{:S(2)}) copy-start(bf16[8,8,128,256]{3,2,1,0:T(8,128)(2,1)} %copy.48) | copy-start | bytes 12582916
  196.6 4.0 %copy-start.2 = (s32[128]{0:T(128)}, s32[128]{0:T(128)S(1)}, u32[]{:S(2)}) copy-start(s32[128]{0:T(128)S(1)} %get-tuple-element.427) | copy-start | bytes 1540 | tf_op jit(solution)/shard_map/while
  201.0 1.6 copy-start.3
  202.7 4.1 %copy-start.2 = (s32[128]{0:T(128)}, s32[128]{0:T(128)S(1)}, u32[]{:S(2)}) copy-start(s32[128]{0:T(128)S(1)} %get-tuple-element.427) | copy-start | bytes 1540 | tf_op jit(solution)/shard_map/while
  207.1 1.6 copy-start.3
  208.8 4.1 %copy-start.2 = (s32[128]{0:T(128)}, s32[128]{0:T(128)S(1)}, u32[]{:S(2)}) copy-start(s32[128]{0:T(128)S(1)} %get-tuple-element.427) | copy-start | bytes 1540 | tf_op jit(solution)/shard_map/while
  213.2 1.6 copy-start.3
  214.9 4.1 %copy-start.2 = (s32[128]{0:T(128)}, s32[128]{0:T(128)S(1)}, u32[]{:S(2)}) copy-start(s32[128]{0:T(128)S(1)} %get-tuple-element.427) | copy-start | bytes 1540 | tf_op jit(solution)/shard_map/while
  219.3 1.6 copy-start.3
  221.0 4.1 %copy-start.2 = (s32[128]{0:T(128)}, s32[128]{0:T(128)S(1)}, u32[]{:S(2)}) copy-start(s32[128]{0:T(128)S(1)} %get-tuple-element.427) | copy-start | bytes 1540 | tf_op jit(solution)/shard_map/while
  225.4 1.6 copy-start.3
  227.1 4.1 %copy-start.2 = (s32[128]{0:T(128)}, s32[128]{0:T(128)S(1)}, u32[]{:S(2)}) copy-start(s32[128]{0:T(128)S(1)} %get-tuple-element.427) | copy-start | bytes 1540 | tf_op jit(solution)/shard_map/while
  231.5 1.6 copy-start.3
  233.2 4.1 %copy-start.2 = (s32[128]{0:T(128)}, s32[128]{0:T(128)S(1)}, u32[]{:S(2)}) copy-start(s32[128]{0:T(128)S(1)} %get-tuple-element.427) | copy-start | bytes 1540 | tf_op jit(solution)/shard_map/while
  237.6 1.6 copy-start.3
  239.3 4.1 %copy-start.2 = (s32[128]{0:T(128)}, s32[128]{0:T(128)S(1)}, u32[]{:S(2)}) copy-start(s32[128]{0:T(128)S(1)} %get-tuple-element.427) | copy-start | bytes 1540 | tf_op jit(solution)/shard_map/while
  243.7 1.6 copy-start.3
Sparse Core Ops, SparseCore 0:
  249.1 41.8 reduce-scatter.1

commit v4 on v3

--- a/solution.py
+++ b/solution.py
@@ -113,6 +113,68 @@
     return gathered.transpose(1, 0, 2, 3).reshape(z_count * p_count * rows, cols)
 
 
+def _scatter_kernel(count, part_ref, out_ref, send_sems, recv_sems, local_sem):
+    me = lax.axis_index("tp")
+    width = out_ref.shape[2]
+    mesh_ids = pl.DeviceIdType.MESH
+    barrier = pltpu.get_barrier_semaphore()
+
+    def greet(step, carry):
+        peer = lax.rem(me + step, count)
+        pl.semaphore_signal(barrier, 1, device_id={"tp": peer}, device_id_type=mesh_ids)
+        return carry
+
+    lax.fori_loop(1, count, greet, 0)
+    pl.semaphore_wait(barrier, count - 1)
+
+    def columns(index):
+        return pl.ds(pl.multiple_of(index * width, width), width)
+
+    own = pltpu.make_async_copy(part_ref.at[:, columns(me)], out_ref.at[me], local_sem)
+    own.start()
+
+    def remote(peer, slot):
+        return pltpu.make_async_remote_copy(
+            src_ref=part_ref.at[:, columns(peer)],
+            dst_ref=out_ref.at[slot],
+            send_sem=send_sems.at[peer],
+            recv_sem=recv_sems.at[slot],
+            device_id={"tp": peer},
+            device_id_type=mesh_ids,
+        )
+
+    def send(step, carry):
+        remote(lax.rem(me + step, count), me).start()
+        return carry
+
+    def finish(step, carry):
+        peer = lax.rem(me + step, count)
+        remote(peer, me).wait_send()
+        remote(peer, peer).wait_recv()
+        return carry
+
+    lax.fori_loop(1, count, send, 0)
+    lax.fori_loop(1, count, finish, 0)
+    own.wait()
+
+
+def scatter_sum_tp(part, count, kernel_id):
+    rows, cols = part.shape
+    pieces = pl.pallas_call(
+        functools.partial(_scatter_kernel, count),
+        out_shape=jax.ShapeDtypeStruct((count, rows, cols // count), part.dtype),
+        in_specs=[pl.BlockSpec(memory_space=pl.ANY)],
+        out_specs=pl.BlockSpec(memory_space=pl.ANY),
+        scratch_shapes=[
+            pltpu.SemaphoreType.DMA((count,)),
+            pltpu.SemaphoreType.DMA((count,)),
+            pltpu.SemaphoreType.DMA(()),
+        ],
+        compiler_params=pltpu.CompilerParams(collective_id=kernel_id, has_side_effects=True),
+    )(part)
+    return jnp.sum(pieces.astype(jnp.float32), axis=0)
+
+
 def ctx_layout(mesh):
     count = mesh.shape["ctx"]
     column = mesh.devices.transpose(
@@ -180,7 +242,7 @@
 
 
 def on_device(
-    layout, tokens, new_token_states, w_query, key_matrix, value_matrix, w_out, lengths, block_map
+    layout, tp_count, tokens, new_token_states, w_query, key_matrix, value_matrix, w_out, lengths, block_map
 ):
     local_rows = tokens.shape[0]
     block_rows = local_rows // 2
@@ -306,16 +368,14 @@
         out_weight,
         preferred_element_type=jnp.float32,
     )
-    summed_rows = lax.psum_scatter(
-        projected.astype(jnp.bfloat16), "tp", scatter_dimension=1, tiled=True
-    ).astype(jnp.float32)
+    summed_rows = scatter_sum_tp(projected.astype(jnp.bfloat16), tp_count, 2)
     summed_rows = summed_rows.astype(jnp.bfloat16)
     return (summed_rows[:local_rows], summed_rows[local_rows:])
 
 
 def solution(mesh):
     return jax.shard_map(
-        functools.partial(on_device, ctx_layout(mesh)),
+        functools.partial(on_device, ctx_layout(mesh), mesh.shape["tp"]),
         mesh=mesh,
         in_specs=(
             P("ctx", None),

time: 303 us -> 280 us (0.924)
  waiting for transfers between devices: 42.1 us -> 0 us
  Pallas kernels: 166 us -> 198 us
  between operations: 14.2 us -> 0.82 us
    reduce_scatter x1 -> x0, waiting for transfers between devices: 42.1 us -> none  [on_device(): lax.psum_scatter(projected.astype(jnp.bfloat16), 'tp', scatter_dimension=...]
    pallas_call x0 -> x1, Pallas kernels: none -> 32.6 us  [scatter_sum_tp(): pl.pallas_call(functools.partial(_scatter_kernel, count), out_shape=jax.S...]
  transfers between devices with their start and end apart: 1 -> 0, of which waited for: 1 -> 0; matrix products, arithmetic and copies ran while one was open for 0% -> 0% of each run, Pallas kernels for 0% -> 0%
where the time goes in v4:
time: 280 us; the launch traced here: 279 us
  Pallas kernels  198 us (71%)
  local copies, waits for them, and re-layouts  27.1 us (10%)
  other arithmetic  24.4 us (9%)
  matrix products  22.4 us (8%)
  loops' own time  5.96 us (2%)
    pallas_call x2, Pallas kernels, gather_ctx(): pl.pallas_call(functools.partial(_gather_kernel, z_count, p_count), out_s...  166 us
    pallas_call x1, Pallas kernels, scatter_sum_tp(): pl.pallas_call(functools.partial(_scatter_kernel, count), out_shape=jax.S...  32.6 us
    dot_general x8, matrix products, attend(): jnp.einsum('gjtk,kgd->gjtd', weights.astype(jnp.bfloat16), value_piece.re...  11 us
    dynamic_slice x8, local copies, waits for them, and re-layouts, on_device(): lax.scan(key_step, start_state, jnp.arange(total_rows // step_rows, dtype...  10.4 us
    reduce_sum x9, other arithmetic, initial_positions(): jnp.sum(jnp.where(block_ids[:, None] == table_ids[None, :], block_map[Non...  8.96 us
    transpose x2, local copies, waits for them, and re-layouts, gather_ctx(): gathered.transpose(1, 0, 2, 3).reshape(z_count * p_count * rows, cols)  8 us
    and x8, other arithmetic, attend(): (key_request[None, :] == token_request[:, None]) & (key_pos[None, :] <= t...  7.55 us
    another operation x1, loops' own time, on_device(): lax.scan(key_step, start_state, jnp.arange(total_rows // step_rows, dtype...  5.96 us

profile of v4, /device:TPU:1, one launch (start us, length us, event | category | flops | bytes accessed | tf_op | source)
XLA Modules:
  0.0 279.1 jit_solution(17465600834155640847)
XLA Ops:
  0.6 1.5 pad_maximum_fusion.piece_ref
  2.1 99.7 %shard_map.95 = bf16[8,8,64,768]{3,2,1,0:T(8,128)(2,1)} custom-call(bf16[64,768]{1,0:T(8,128)(2,1)} %pad_maximum_fusion.piece_ref), custom_call_target="tpu_custom_call" | custom-call | tf_op jit(solution)/shard_map/pallas_call | solution.py:99
  101.8 3.3 %copy.47 = bf16[8,8,64,768]{3,2,1,0:T(8,128)(2,1)S(1)} copy(bf16[8,8,64,768]{3,2,0,1:T(8,128)(2,1)} %bitcast.133) | data formatting | bytes 12582912 | tf_op jit(solution)/shard_map/transpose | solution.py:113
  105.2 0.8 fusion.33
  105.9 1.9 copy-done
  108.4 66.1 %shard_map.96 = bf16[8,8,128,256]{3,2,1,0:T(8,128)(2,1)} custom-call(bf16[128,256]{1,0:T(8,128)(2,1)} %get-tuple-element.299.piece_ref), custom_call_target="tpu_custom_call" | custom-call | tf_op jit(solution)/shard_map/pallas_call | solution.py:99
  174.5 4.7 %copy.48 = bf16[8,8,128,256]{3,2,1,0:T(8,128)(2,1)} copy(bf16[8,8,128,256]{3,2,0,1:T(8,128)(2,1)} %bitcast.137) | data formatting | bytes 8388608 | tf_op jit(solution)/shard_map/transpose | solution.py:113
  180.5 2.3 fusion.86
  183.4 2.1 fusion.57
  185.6 3.8 %fusion.84 = (bf16[8192,128]{1,0:T(8,128)(2,1)}, bf16[8192,128]{1,0:T(8,128)(2,1)S(1)}) fusion(bf16[8192,256]{1,0:T(8,128)(2,1)} %bitcast.136), kind=kLoop, calls=%fused_computation.112 | loop fusion | bytes 8388608 | tf_op jit(solution)/shard_map/slice | solution.py:322
  189.4 0.8 select_reduce_fusion.1
  191.4 48.8 %while.17 = (s32[]{:T(128)}, f32[1,2,128]{2,1,0:T(2,128)S(1)}, f32[1,2,128]{2,1,0:T(2,128)S(1)}, f32[1,2,128,128]{3,2,1,0:T(8,128)S(1)}, s32[8]{0:T(128)}, /*ind...) while((s32[]{:T(128)}, f32[1,2,128]{2,1,0:T(2,128)S(1)}, ...), condition=%wide.region_8.9_spmd.clone, body=%wide.region_3.8_spmd.clone.sunk | while | flops 137504256 | bytes 4581171 | solution.py:336
  191.4 1.3 dynamic_slice.37
  193.4 1.0 select_reduce_fusion.3
  194.5 0.9 compare_and_fusion.2
  195.8 1.4 fusion.100
  197.5 1.3 dynamic_slice.37
  199.5 1.0 select_reduce_fusion.3
  200.6 0.9 compare_and_fusion.2
  201.9 1.4 fusion.100
  203.6 1.3 dynamic_slice.37
  205.6 1.0 select_reduce_fusion.3
  206.7 0.9 compare_and_fusion.2
  208.1 1.4 fusion.100
  209.7 1.3 dynamic_slice.37
  211.7 1.0 select_reduce_fusion.3
  212.8 0.9 compare_and_fusion.2
  214.2 1.4 fusion.100
  215.8 1.3 dynamic_slice.37
  217.8 1.0 select_reduce_fusion.3
  218.9 0.9 compare_and_fusion.2
  220.3 1.4 fusion.100
  221.9 1.3 dynamic_slice.37
  223.9 1.0 select_reduce_fusion.3
  225.0 0.9 compare_and_fusion.2
  226.4 1.4 fusion.100
  228.0 1.3 dynamic_slice.37
  230.0 1.0 select_reduce_fusion.3
  231.1 0.9 compare_and_fusion.2
  232.5 1.4 fusion.100
  234.1 1.3 dynamic_slice.37
  236.1 1.0 select_reduce_fusion.3
  237.2 0.9 compare_and_fusion.2
  238.6 1.4 fusion.100
  240.4 3.5 %convolution_convert_fusion.part_ref = bf16[132,4096]{1,0:T(8,128)(2,1)} fusion(bf16[4096,768]{1,0:T(8,128)(2,1)} %bitcast.139, bf16[4,256]{0,1:T(8,128)(2,1)S(1)} %copy.53, bf16[128,256]{0,1:T(8,128)(2,1)S(1)} %bitcast.142), kind=kOutput, calls=%fused_computation.47 | convolution fusion | flops 277499904 | bytes 3246080 | tf_op jit(solution)/shard_map/dot_general | solution.py:366
  243.8 32.6 %shard_map.97 = bf16[8,132,512]{2,1,0:T(8,128)(2,1)} custom-call(bf16[132,4096]{1,0:T(8,128)(2,1)} %convolution_convert_fusion.part_ref), custom_call_target="tpu_custom_call" | custom-call | tf_op jit(solution)/shard_map/pallas_call | solution.py:163
  276.4 1.4 reduce_sum.97
  277.8 0.7 slice.60
  (132 shorter events, 10.1 us)
Async XLA Ops:
  101.8 3.3 %copy-start.3 = (bf16[128,4096]{1,0:T(8,128)(2,1)S(1)}, bf16[128,4096]{1,0:T(8,128)(2,1)}, u32[]{:S(2)}) copy-start(bf16[128,4096]{1,0:T(8,128)(2,1)} %param.10) | copy-start | bytes 3145732
  101.8 3.3 %copy-start.4 = (bf16[4,4096]{1,0:T(4,128)(2,1)S(1)}, bf16[4,4096]{1,0:T(4,128)(2,1)}, u32[]{:S(2)}) copy-start(bf16[4,4096]{1,0:T(4,128)(2,1)} %param.11) | copy-start | bytes 98308
  105.1 2.7 copy-start
  174.5 4.7 %copy-start.5 = (s32[4]{0:T(128)S(1)}, s32[4]{0:T(128)}, u32[]{:S(2)}) copy-start(s32[4]{0:T(128)} %param.16) | copy-start | bytes 52
  191.4 4.0 %copy-start.1 = (s32[128]{0:T(128)}, s32[128]{0:T(128)S(1)}, u32[]{:S(2)}) copy-start(s32[128]{0:T(128)S(1)} %get-tuple-element.427) | copy-start | bytes 1540 | tf_op jit(solution)/shard_map/while
  195.8 1.6 copy-start.2
  197.5 4.1 %copy-start.1 = (s32[128]{0:T(128)}, s32[128]{0:T(128)S(1)}, u32[]{:S(2)}) copy-start(s32[128]{0:T(128)S(1)} %get-tuple-element.427) | copy-start | bytes 1540 | tf_op jit(solution)/shard_map/while
  201.9 1.6 copy-start.2
  203.6 4.1 %copy-start.1 = (s32[128]{0:T(128)}, s32[128]{0:T(128)S(1)}, u32[]{:S(2)}) copy-start(s32[128]{0:T(128)S(1)} %get-tuple-element.427) | copy-start | bytes 1540 | tf_op jit(solution)/shard_map/while
  208.0 1.6 copy-start.2
  209.7 4.1 %copy-start.1 = (s32[128]{0:T(128)}, s32[128]{0:T(128)S(1)}, u32[]{:S(2)}) copy-start(s32[128]{0:T(128)S(1)} %get-tuple-element.427) | copy-start | bytes 1540 | tf_op jit(solution)/shard_map/while
  214.1 1.6 copy-start.2
  215.8 4.1 %copy-start.1 = (s32[128]{0:T(128)}, s32[128]{0:T(128)S(1)}, u32[]{:S(2)}) copy-start(s32[128]{0:T(128)S(1)} %get-tuple-element.427) | copy-start | bytes 1540 | tf_op jit(solution)/shard_map/while
  220.3 1.6 copy-start.2
  221.9 4.1 %copy-start.1 = (s32[128]{0:T(128)}, s32[128]{0:T(128)S(1)}, u32[]{:S(2)}) copy-start(s32[128]{0:T(128)S(1)} %get-tuple-element.427) | copy-start | bytes 1540 | tf_op jit(solution)/shard_map/while
  226.4 1.6 copy-start.2
  228.0 4.1 %copy-start.1 = (s32[128]{0:T(128)}, s32[128]{0:T(128)S(1)}, u32[]{:S(2)}) copy-start(s32[128]{0:T(128)S(1)} %get-tuple-element.427) | copy-start | bytes 1540 | tf_op jit(solution)/shard_map/while
  232.5 1.6 copy-start.2
  234.1 4.1 %copy-start.1 = (s32[128]{0:T(128)}, s32[128]{0:T(128)S(1)}, u32[]{:S(2)}) copy-start(s32[128]{0:T(128)S(1)} %get-tuple-element.427) | copy-start | bytes 1540 | tf_op jit(solution)/shard_map/while
  238.6 1.6 copy-start.2

commit v5 on v4

--- a/solution.py
+++ b/solution.py
@@ -15,7 +15,17 @@
 
 
 def _gather_kernel(
-    z_count, p_count, piece_ref, out_ref, z_send, z_recv, p_send, p_recv, local_sem
+    z_count,
+    p_count,
+    first_ref,
+    second_ref,
+    first_out,
+    second_out,
+    first_z,
+    first_p,
+    second_p,
+    second_z,
+    local_sems,
 ):
     me = lax.axis_index("ctx")
     z_me = me // p_count
@@ -29,88 +39,120 @@
     def p_peer(step):
         return lax.rem(p_me + step, p_count)
 
-    def greet_z(step, carry):
-        target = z_peer(step) * p_count + p_me
-        pl.semaphore_signal(barrier, 1, device_id={"ctx": target}, device_id_type=mesh_ids)
-        return carry
-
-    def greet_p(step, carry):
-        target = z_me * p_count + p_peer(step)
-        pl.semaphore_signal(barrier, 1, device_id={"ctx": target}, device_id_type=mesh_ids)
-        return carry
-
-    lax.fori_loop(1, z_count, greet_z, 0)
-    lax.fori_loop(1, p_count, greet_p, 0)
+    def z_target(peer):
+        return peer * p_count + p_me
+
+    def p_target(peer):
+        return z_me * p_count + peer
+
+    def greet(peer_of, target_of):
+        def body(step, carry):
+            pl.semaphore_signal(
+                barrier, 1, device_id={"ctx": target_of(peer_of(step))}, device_id_type=mesh_ids
+            )
+            return carry
+
+        return body
+
+    lax.fori_loop(1, z_count, greet(z_peer, z_target), 0)
+    lax.fori_loop(1, p_count, greet(p_peer, p_target), 0)
     pl.semaphore_wait(barrier, z_count + p_count - 2)
-    own = pltpu.make_async_copy(piece_ref, out_ref.at[p_me, z_me], local_sem)
-    own.start()
-
-    def z_copy(peer, slot):
-        return pltpu.make_async_remote_copy(
-            src_ref=piece_ref,
-            dst_ref=out_ref.at[p_me, slot],
-            send_sem=z_send.at[peer],
-            recv_sem=z_recv.at[slot],
-            device_id={"ctx": peer * p_count + p_me},
-            device_id_type=mesh_ids,
-        )
-
-    def z_start(step, carry):
-        z_copy(z_peer(step), z_me).start()
-        return carry
-
-    def z_finish(step, carry):
-        peer = z_peer(step)
-        z_copy(peer, z_me).wait_send()
-        z_copy(peer, peer).wait_recv()
-        return carry
-
-    lax.fori_loop(1, z_count, z_start, 0)
-    lax.fori_loop(1, z_count, z_finish, 0)
-    own.wait()
-
-    def p_copy(peer, slot):
-        return pltpu.make_async_remote_copy(
-            src_ref=out_ref.at[slot],
-            dst_ref=out_ref.at[slot],
-            send_sem=p_send.at[peer],
-            recv_sem=p_recv.at[slot],
-            device_id={"ctx": z_me * p_count + peer},
-            device_id_type=mesh_ids,
-        )
-
-    def p_start(step, carry):
-        p_copy(p_peer(step), p_me).start()
-        return carry
-
-    def p_finish(step, carry):
-        peer = p_peer(step)
-        p_copy(peer, p_me).wait_send()
-        p_copy(peer, peer).wait_recv()
-        return carry
-
-    lax.fori_loop(1, p_count, p_start, 0)
-    lax.fori_loop(1, p_count, p_finish, 0)
+
+    def exchange(count, peer_of, target_of, own_slot, src_of, dst_of, sems):
+        send_sems, recv_sems = sems
+
+        def copy(peer, slot):
+            return pltpu.make_async_remote_copy(
+                src_ref=src_of(slot),
+                dst_ref=dst_of(slot),
+                send_sem=send_sems.at[peer],
+                recv_sem=recv_sems.at[slot],
+                device_id={"ctx": target_of(peer)},
+                device_id_type=mesh_ids,
+            )
+
+        def start(step, carry):
+            copy(peer_of(step), own_slot).start()
+            return carry
+
+        def finish(step, carry):
+            peer = peer_of(step)
+            copy(peer, own_slot).wait_send()
+            copy(peer, peer).wait_recv()
+            return carry
+
+        return (lambda: lax.fori_loop(1, count, start, 0), lambda: lax.fori_loop(1, count, finish, 0))
+
+    first_own = pltpu.make_async_copy(first_ref, first_out.at[p_me, z_me], local_sems.at[0])
+    second_own = pltpu.make_async_copy(second_ref, second_out.at[z_me, p_me], local_sems.at[1])
+    first_own.start()
+    second_own.start()
+    first_one = exchange(
+        z_count, z_peer, z_target, z_me,
+        lambda slot: first_ref, lambda slot: first_out.at[p_me, slot], first_z,
+    )
+    second_one = exchange(
+        p_count, p_peer, p_target, p_me,
+        lambda slot: second_ref, lambda slot: second_out.at[z_me, slot], second_p,
+    )
+    first_two = exchange(
+        p_count, p_peer, p_target, p_me,
+        lambda slot: first_out.at[slot], lambda slot: first_out.at[slot], first_p,
+    )
+    second_two = exchange(
+        z_count, z_peer, z_target, z_me,
+        lambda slot: second_out.at[slot], lambda slot: second_out.at[slot], second_z,
+    )
+    first_one[0]()
+    second_one[0]()
+    first_one[1]()
+    first_own.wait()
+    first_two[0]()
+    second_one[1]()
+    second_own.wait()
+    second_two[0]()
+    first_two[1]()
+    second_two[1]()
 
 
 def gather_ctx(piece, layout, kernel_id):
     z_count, p_count = layout
     rows, cols = piece.shape
-    gathered = pl.pallas_call(
-        functools.partial(_gather_kernel, z_count, p_count),
-        out_shape=jax.ShapeDtypeStruct((p_count, z_count, rows, cols), piece.dtype),
-        in_specs=[pl.BlockSpec(memory_space=pl.ANY)],
-        out_specs=pl.BlockSpec(memory_space=pl.ANY),
-        scratch_shapes=[
-            pltpu.SemaphoreType.DMA((z_count,)),
-            pltpu.SemaphoreType.DMA((z_count,)),
-            pltpu.SemaphoreType.DMA((p_count,)),
-            pltpu.SemaphoreType.DMA((p_count,)),
-            pltpu.SemaphoreType.DMA(()),
+    half = cols // 2
+    dma_pairs = [
+        pltpu.SemaphoreType.DMA((z_count,)),
+        pltpu.SemaphoreType.DMA((z_count,)),
+        pltpu.SemaphoreType.DMA((p_count,)),
+        pltpu.SemaphoreType.DMA((p_count,)),
+    ]
+
+    def kernel(first_ref, second_ref, first_out, second_out, *sems):
+        _gather_kernel(
+            z_count, p_count, first_ref, second_ref, first_out, second_out,
+            (sems[0], sems[1]), (sems[2], sems[3]), (sems[4], sems[5]), (sems[6], sems[7]),
+            sems[8],
+        )
+
+    first, second = pl.pallas_call(
+        kernel,
+        out_shape=(
+            jax.ShapeDtypeStruct((p_count, z_count, rows, half), piece.dtype),
+            jax.ShapeDtypeStruct((z_count, p_count, rows, cols - half), piece.dtype),
+        ),
+        in_specs=[pl.BlockSpec(memory_space=pl.ANY)] * 2,
+        out_specs=(pl.BlockSpec(memory_space=pl.ANY),) * 2,
+        scratch_shapes=dma_pairs + [dma_pairs[2], dma_pairs[3], dma_pairs[0], dma_pairs[1]]
+        + [pltpu.SemaphoreType.DMA((2,))],
+        compiler_params=pltpu.CompilerParams(collective_id=kernel_id, has_side_effects=True),
+    )(piece[:, :half], piece[:, half:])
+    total = z_count * p_count * rows
+    return jnp.concatenate(
+        [
+            first.transpose(1, 0, 2, 3).reshape(total, half),
+            second.reshape(total, cols - half),
         ],
-        compiler_params=pltpu.CompilerParams(collective_id=kernel_id, has_side_effects=True),
-    )(piece)
-    return gathered.transpose(1, 0, 2, 3).reshape(z_count * p_count * rows, cols)
+        axis=1,
+    )
 
 
 def _scatter_kernel(count, part_ref, out_ref, send_sems, recv_sems, local_sem):

time: 280 us -> 255 us (0.911); the launches traced: 279 us -> 250 us
  Pallas kernels: 198 us -> 179 us
  local copies, waits for them, and re-layouts: 27.1 us -> 18.3 us
    pallas_call x2, Pallas kernels: 166 us -> 150 us  [gather_ctx(): pl.pallas_call(kernel, out_shape=(jax.ShapeDtypeStruct((p_count, z_count,...]
    transpose x2, local copies, waits for them, and re-layouts: 8 us -> 4.2 us  [gather_ctx(): first.transpose(1, 0, 2, 3).reshape(total, half)]
    pallas_call x1, Pallas kernels: 32.6 us -> 29.3 us  [scatter_sum_tp(): pl.pallas_call(functools.partial(_scatter_kernel, count), out_shape=jax.S...]
    slice x1, local copies, waits for them, and re-layouts: 3.79 us -> 0.62 us  [on_device(): local_values = value_all[:local_rows]]
where the time goes in v5:
time: 255 us; the launch traced here: 250 us
  Pallas kernels  179 us (70%)
  other arithmetic  24.6 us (10%)
  matrix products  20.8 us (8%)
  local copies, waits for them, and re-layouts  18.3 us (7%)
  loops' own time  6.42 us (3%)
    pallas_call x2, Pallas kernels, gather_ctx(): pl.pallas_call(kernel, out_shape=(jax.ShapeDtypeStruct((p_count, z_count,...  150 us
    pallas_call x1, Pallas kernels, scatter_sum_tp(): pl.pallas_call(functools.partial(_scatter_kernel, count), out_shape=jax.S...  29.3 us
    dot_general x8, matrix products, attend(): jnp.einsum('gjtk,kgd->gjtd', weights.astype(jnp.bfloat16), value_piece.re...  11 us
    dynamic_slice x8, local copies, waits for them, and re-layouts, on_device(): lax.scan(key_step, start_state, jnp.arange(total_rows // step_rows, dtype...  10.6 us
    reduce_sum x9, other arithmetic, initial_positions(): jnp.sum(jnp.where(block_ids[:, None] == table_ids[None, :], block_map[Non...  8.96 us
    and x8, other arithmetic, attend(): (key_request[None, :] == token_request[:, None]) & (key_pos[None, :] <= t...  7.7 us
    another operation x1, loops' own time, on_device(): lax.scan(key_step, start_state, jnp.arange(total_rows // step_rows, dtype...  6.42 us

profile of v5, /device:TPU:1, one launch (start us, length us, event | category | flops | bytes accessed | tf_op | source)
XLA Modules:
  0.0 250.3 jit_solution(6381003981710935893)
XLA Ops:
  0.6 1.4 pad_maximum_fusion.4
  2.1 89.5 %shard_map.95 = (bf16[8,8,64,384]{3,2,1,0:T(8,128)(2,1)}, bf16[8,8,64,384]{3,2,1,0:T(8,128)(2,1)}) custom-call(bf16[64,384]{1,0:T(8,128)(2,1)} %get-tuple-element.312.first_ref, bf16[64,384]{1,0:T(8,128)(2,1)} %get-tuple-element.313.second_ref), custom_call_target="tpu_custom_call" | custom-call | tf_op jit(solution)/shard_map/pallas_call | solution.py:136
  91.6 2.5 copy.47
  94.7 0.8 fusion.30
  96.1 60.6 %shard_map.96 = (bf16[8,8,128,128]{3,2,1,0:T(8,128)(2,1)}, bf16[8,8,128,128]{3,2,1,0:T(8,128)(2,1)}) custom-call(bf16[128,128]{1,0:T(8,128)(2,1)} %get-tuple-element.307.first_ref, bf16[128,128]{1,0:T(8,128)(2,1)} %get-tuple-element.306.second_ref), custom_call_target="tpu_custom_call" | custom-call | tf_op jit(solution)/shard_map/pallas_call | solution.py:136
  156.7 1.7 copy.48
  158.4 0.7 broadcast_multiply_fusion
  159.6 0.7 fusion.63
  160.9 2.1 fusion.39
  163.7 0.8 select_reduce_fusion.1
  164.5 0.6 convert_reduce_fusion.2
  165.2 49.5 %while.17 = (s32[]{:T(128)}, f32[1,2,128]{2,1,0:T(2,128)S(1)}, f32[1,2,128]{2,1,0:T(2,128)S(1)}, f32[1,2,128,128]{3,2,1,0:T(8,128)S(1)}, s32[8]{0:T(128)}, /*ind...) while((s32[]{:T(128)}, f32[1,2,128]{2,1,0:T(2,128)S(1)}, ...), condition=%wide.region_8.9_spmd.clone, body=%wide.region_3.8_spmd.clone.sunk | while | flops 137504256 | bytes 4581179 | solution.py:378
  165.2 1.3 dynamic_slice.37
  167.3 1.0 select_reduce_fusion.3
  168.4 1.0 compare_and_fusion.2
  170.0 1.4 fusion.79
  171.4 1.3 dynamic_slice.37
  173.5 1.0 select_reduce_fusion.3
  174.6 1.0 compare_and_fusion.2
  176.2 1.4 fusion.79
  177.6 1.3 dynamic_slice.37
  179.7 1.0 select_reduce_fusion.3
  180.8 1.0 compare_and_fusion.2
  182.4 1.4 fusion.79
  183.8 1.3 dynamic_slice.37
  185.8 1.0 select_reduce_fusion.3
  187.0 1.0 compare_and_fusion.2
  188.6 1.4 fusion.79
  190.0 1.3 dynamic_slice.37
  192.0 1.0 select_reduce_fusion.3
  193.2 1.0 compare_and_fusion.2
  194.8 1.4 fusion.79
  196.2 1.3 dynamic_slice.37
  198.2 1.0 select_reduce_fusion.3
  199.4 1.0 compare_and_fusion.2
  201.0 1.4 fusion.79
  202.4 1.3 dynamic_slice.37
  204.4 1.0 select_reduce_fusion.3
  205.6 1.0 compare_and_fusion.2
  207.2 1.4 fusion.79
  208.6 1.3 dynamic_slice.37
  210.6 1.0 select_reduce_fusion.3
  211.7 1.0 compare_and_fusion.2
  213.4 1.4 fusion.79
  214.9 3.5 %convolution_convert_fusion.part_ref = bf16[132,4096]{1,0:T(8,128)(2,1)} fusion(bf16[4096,384]{1,0:T(8,128)(2,1)} %bitcast.124, bf16[4,256]{0,1:T(8,128)(2,1)S(1)} %copy.53, bf16[128,256]{0,1:T(8,128)(2,1)S(1)} %bitcast.128), kind=kOutput, calls=%fused_computation.47 | convolution fusion | flops 277499904 | bytes 3246080 | tf_op jit(solution)/shard_map/dot_general | solution.py:408
  218.3 29.3 %shard_map.97 = bf16[8,132,512]{2,1,0:T(8,128)(2,1)} custom-call(bf16[132,4096]{1,0:T(8,128)(2,1)} %convolution_convert_fusion.part_ref), custom_call_target="tpu_custom_call" | custom-call | tf_op jit(solution)/shard_map/pallas_call | solution.py:205
  247.6 1.4 reduce_sum.97
  249.0 0.7 slice.60
  (132 shorter events, 9.5 us)
Async XLA Ops:
  91.5 2.8 %copy-start = (bf16[8,8,64,384]{3,2,1,0:T(8,128)(2,1)S(1)}, bf16[8,8,64,384]{3,2,1,0:T(8,128)(2,1)}, u32[]{:S(2)}) copy-start(bf16[8,8,64,384]{3,2,1,0:T(8,128)(2,1)} %get-tuple-element.160) | copy-start | bytes 9437188
  91.5 3.1 %copy-start.3 = (bf16[128,4096]{1,0:T(8,128)(2,1)S(1)}, bf16[128,4096]{1,0:T(8,128)(2,1)}, u32[]{:S(2)}) copy-start(bf16[128,4096]{1,0:T(8,128)(2,1)} %param.10) | copy-start | bytes 3145732
  91.6 3.1 %copy-start.4 = (bf16[4,4096]{1,0:T(4,128)(2,1)S(1)}, bf16[4,4096]{1,0:T(4,128)(2,1)}, u32[]{:S(2)}) copy-start(bf16[4,4096]{1,0:T(4,128)(2,1)} %param.11) | copy-start | bytes 98308
  156.7 2.6 %copy-start.5 = (s32[4]{0:T(128)S(1)}, s32[4]{0:T(128)}, u32[]{:S(2)}) copy-start(s32[4]{0:T(128)} %param.16) | copy-start | bytes 52
  165.2 3.2 %copy-start.1 = (s32[128]{0:T(128)}, s32[128]{0:T(128)S(1)}, u32[]{:S(2)}) copy-start(s32[128]{0:T(128)S(1)} %get-tuple-element.435) | copy-start | bytes 1540 | tf_op jit(solution)/shard_map/while
  169.7 1.6 copy-start.2
  171.4 3.2 %copy-start.1 = (s32[128]{0:T(128)}, s32[128]{0:T(128)S(1)}, u32[]{:S(2)}) copy-start(s32[128]{0:T(128)S(1)} %get-tuple-element.435) | copy-start | bytes 1540 | tf_op jit(solution)/shard_map/while
  175.9 1.6 copy-start.2
  177.6 3.2 %copy-start.1 = (s32[128]{0:T(128)}, s32[128]{0:T(128)S(1)}, u32[]{:S(2)}) copy-start(s32[128]{0:T(128)S(1)} %get-tuple-element.435) | copy-start | bytes 1540 | tf_op jit(solution)/shard_map/while
  182.1 1.6 copy-start.2
  183.8 3.2 %copy-start.1 = (s32[128]{0:T(128)}, s32[128]{0:T(128)S(1)}, u32[]{:S(2)}) copy-start(s32[128]{0:T(128)S(1)} %get-tuple-element.435) | copy-start | bytes 1540 | tf_op jit(solution)/shard_map/while
  188.3 1.6 copy-start.2
  190.0 3.2 %copy-start.1 = (s32[128]{0:T(128)}, s32[128]{0:T(128)S(1)}, u32[]{:S(2)}) copy-start(s32[128]{0:T(128)S(1)} %get-tuple-element.435) | copy-start | bytes 1540 | tf_op jit(solution)/shard_map/while
  194.5 1.6 copy-start.2
  196.2 3.2 %copy-start.1 = (s32[128]{0:T(128)}, s32[128]{0:T(128)S(1)}, u32[]{:S(2)}) copy-start(s32[128]{0:T(128)S(1)} %get-tuple-element.435) | copy-start | bytes 1540 | tf_op jit(solution)/shard_map/while
  200.7 1.6 copy-start.2
  202.4 3.2 %copy-start.1 = (s32[128]{0:T(128)}, s32[128]{0:T(128)S(1)}, u32[]{:S(2)}) copy-start(s32[128]{0:T(128)S(1)} %get-tuple-element.435) | copy-start | bytes 1540 | tf_op jit(solution)/shard_map/while
  206.9 1.6 copy-start.2
  208.6 3.2 %copy-start.1 = (s32[128]{0:T(128)}, s32[128]{0:T(128)S(1)}, u32[]{:S(2)}) copy-start(s32[128]{0:T(128)S(1)} %get-tuple-element.435) | copy-start | bytes 1540 | tf_op jit(solution)/shard_map/while
  213.1 1.6 copy-start.2

commit v6 on v5

--- a/solution.py
+++ b/solution.py
@@ -323,8 +323,8 @@
         peak_run, total_run, mixed_run = running
         key_piece, value_piece = shard_pieces
         row_count = key_piece.shape[0]
-        key_pos = initial_positions(block_map, first_row, row_count, block_rows)
-        key_request = request_index(key_pos, request_ends)
+        key_pos = lax.dynamic_slice_in_dim(cache_pos, first_row, row_count, 0)
+        key_request = lax.dynamic_slice_in_dim(cache_request, first_row, row_count, 0)
         allowed = (key_request[None, :] == token_request[:, None]) & (
             key_pos[None, :] <= token_pos[:, None]
         )
@@ -363,9 +363,11 @@
     cache_keys = cache_both[:, :kv_width]
     cache_values = cache_both[:, kv_width:]
     total_rows = cache_keys.shape[0]
-    shard_count = total_rows // local_rows
-    limit = max(1, 1024 // local_rows)
-    step_rows = local_rows * math.gcd(shard_count, 1 << limit.bit_length() - 1)
+    step_rows = total_rows
+    cache_pos = (
+        block_map[:, None] * block_rows + jnp.arange(block_rows, dtype=jnp.int32)[None, :]
+    ).reshape(total_rows)
+    cache_request = request_index(cache_pos, request_ends)
 
     def key_step(running, step_index):
         first_row = step_index * step_rows
@@ -379,10 +381,6 @@
         key_step, start_state, jnp.arange(total_rows // step_rows, dtype=jnp.int32)
     )
     peak_run, total_run, mixed_run = final_state
-    cache_pos = (
-        block_map[:, None] * block_rows + jnp.arange(block_rows, dtype=jnp.int32)[None, :]
-    ).reshape(total_rows)
-    cache_request = request_index(cache_pos, request_ends)
     owned = (cache_request[None, :] == request_ids[:, None])[:, None, None, :]
     cache_peak, cache_total, cache_mixed = softmax_parts(
         dec_heads, cache_keys, cache_values, owned, kv_heads, head_dim, score_scale

time: 255 us -> 210 us (0.82)
  the two profiles are of different devices: /device:TPU:1 before, /device:TPU:21 now
where the time goes in v6:
time: 210 us; the launch traced here: 209 us
  Pallas kernels  184 us (88%)
  other arithmetic  10.4 us (5%)
  matrix products  7.38 us (4%)
  local copies, waits for them, and re-layouts  7.27 us (3%)
    pallas_call x2, Pallas kernels, gather_ctx(): pl.pallas_call(kernel, out_shape=(jax.ShapeDtypeStruct((p_count, z_count,...  149 us
    pallas_call x1, Pallas kernels, scatter_sum_tp(): pl.pallas_call(functools.partial(_scatter_kernel, count), out_shape=jax.S...  34.4 us
    transpose x2, local copies, waits for them, and re-layouts, gather_ctx(): first.transpose(1, 0, 2, 3).reshape(total, half)  4.34 us

profile of v6, /device:TPU:21, one launch (start us, length us, event | category | flops | bytes accessed | tf_op | source)
XLA Modules:
  0.0 209.4 jit_solution(10853725710837957870)
XLA Ops:
  0.6 0.8 reduce-window.8
  1.5 0.7 broadcast_multiply_fusion
  2.1 0.8 select_reduce_fusion
  3.0 0.1 convert_reduce_fusion.1
  3.1 0.1 iota_add_fusion
  3.2 0.1 add.96
  3.2 0.2 convert_reduce_fusion
  3.4 1.4 pad_maximum_fusion.4
  4.9 2.8 %compare_and_fusion = pred[128,8192]{0,1:T(8,128)(4,1)S(1)} fusion(s32[128]{0:T(128)S(1)} %fusion.53, s32[128]{0:T(128)S(1)} %convert_reduce_fusion.1, s32[8192]{0:T(1024)S(1)} %add.96, s32[8192]{0:T(1024)S(1)} %convert_reduce_fusion), kind=kLoop, calls=%fused_computation.18 | loop fusion | flops 3145728 | bytes 1115136 | tf_op jit(solution)/shard_map/while/body/eval_jaxpr/and | solution.py:328
  7.6 90.6 %shard_map.95 = (bf16[8,8,64,384]{3,2,1,0:T(8,128)(2,1)}, bf16[8,8,64,384]{3,2,1,0:T(8,128)(2,1)}) custom-call(bf16[64,384]{1,0:T(8,128)(2,1)} %get-tuple-element.55.first_ref, bf16[64,384]{1,0:T(8,128)(2,1)} %get-tuple-element.56.second_ref), custom_call_target="tpu_custom_call" | custom-call | tf_op jit(solution)/shard_map/pallas_call | solution.py:136
  98.2 0.0 copy-start
  98.2 0.0 copy-start.4
  98.2 0.0 copy-start.5
  98.3 2.5 %copy.41 = bf16[8,8,64,384]{3,2,1,0:T(8,128)(2,1)S(1)} copy(bf16[8,8,64,384]{3,2,0,1:T(8,128)(2,1)} %bitcast.94) | data formatting | bytes 6291456 | tf_op jit(solution)/shard_map/transpose | solution.py:151
  100.7 0.3 copy-done
  101.1 0.3 copy-done.4
  101.3 0.0 copy-done.5
  101.3 0.8 fusion.15
  102.1 0.1 multiply_reduce_fusion
  102.2 0.1 copy.47
  102.3 0.6 fusion.59
  102.9 58.6 %shard_map.96 = (bf16[8,8,128,128]{3,2,1,0:T(8,128)(2,1)}, bf16[8,8,128,128]{3,2,1,0:T(8,128)(2,1)}) custom-call(bf16[128,128]{1,0:T(8,128)(2,1)} %get-tuple-element.46.first_ref, bf16[128,128]{1,0:T(8,128)(2,1)} %get-tuple-element.45.second_ref), custom_call_target="tpu_custom_call" | custom-call | tf_op jit(solution)/shard_map/pallas_call | solution.py:136
  161.5 0.0 copy-start.2
  161.6 1.9 copy.42
  163.4 0.7 fusion.60
  164.2 0.3 fusion.34
  164.5 0.0 copy-done.2
  164.5 0.5 fusion.27
  165.0 0.1 copy.48
  165.2 1.8 fusion.61
  166.9 0.0 copy-start.3
  166.9 1.7 fusion.4
  168.6 0.0 copy-done.3
  168.6 0.0 copy-start.1
  168.7 1.8 fusion.31
  170.5 0.1 copy-done.1
  170.5 1.8 convolution_convert_fusion.part_ref
  172.4 34.4 %shard_map.97 = bf16[8,132,512]{2,1,0:T(8,128)(2,1)} custom-call(bf16[132,4096]{1,0:T(8,128)(2,1)} %convolution_convert_fusion.part_ref), custom_call_target="tpu_custom_call" | custom-call | tf_op jit(solution)/shard_map/pallas_call | solution.py:205
  206.8 1.4 reduce_sum.73
  208.2 0.6 slice.61
  208.8 0.7 slice.60
  (11 shorter events, 0.1 us)
Async XLA Ops:
  98.2 2.8 %copy-start = (bf16[8,8,64,384]{3,2,1,0:T(8,128)(2,1)S(1)}, bf16[8,8,64,384]{3,2,1,0:T(8,128)(2,1)}, u32[]{:S(2)}) copy-start(bf16[8,8,64,384]{3,2,1,0:T(8,128)(2,1)} %get-tuple-element.29) | copy-start | bytes 9437188
  98.2 3.1 %copy-start.4 = (bf16[128,4096]{1,0:T(8,128)(2,1)S(1)}, bf16[128,4096]{1,0:T(8,128)(2,1)}, u32[]{:S(2)}) copy-start(bf16[128,4096]{1,0:T(8,128)(2,1)} %param.8) | copy-start | bytes 3145732
  98.2 3.1 %copy-start.5 = (bf16[4,4096]{1,0:T(4,128)(2,1)S(1)}, bf16[4,4096]{1,0:T(4,128)(2,1)}, u32[]{:S(2)}) copy-start(bf16[4,4096]{1,0:T(4,128)(2,1)} %param.9) | copy-start | bytes 98308
  161.5 3.0 %copy-start.2 = (bf16[8,8,128,128]{3,2,1,0:T(8,128)(2,1)S(1)}, bf16[8,8,128,128]{3,2,1,0:T(8,128)(2,1)}, u32[]{:S(2)}) copy-start(bf16[8,8,128,128]{3,2,1,0:T(8,128)(2,1)} %get-tuple-element.31) | copy-start | bytes 6291460
  166.9 1.7 copy-start.3
  168.6 1.9 copy-start.1

commit v7 on v6

--- a/solution.py
+++ b/solution.py
@@ -118,7 +118,9 @@
 def gather_ctx(piece, layout, kernel_id):
     z_count, p_count = layout
     rows, cols = piece.shape
-    half = cols // 2
+    tile = 16
+    head = min(rows - tile, max(tile, round(rows * 2 / (3 * tile)) * tile))
+    tail = rows - head
     dma_pairs = [
         pltpu.SemaphoreType.DMA((z_count,)),
         pltpu.SemaphoreType.DMA((z_count,)),
@@ -136,23 +138,17 @@
     first, second = pl.pallas_call(
         kernel,
         out_shape=(
-            jax.ShapeDtypeStruct((p_count, z_count, rows, half), piece.dtype),
-            jax.ShapeDtypeStruct((z_count, p_count, rows, cols - half), piece.dtype),
+            jax.ShapeDtypeStruct((p_count, z_count, head, cols), piece.dtype),
+            jax.ShapeDtypeStruct((z_count, p_count, tail, cols), piece.dtype),
         ),
         in_specs=[pl.BlockSpec(memory_space=pl.ANY)] * 2,
         out_specs=(pl.BlockSpec(memory_space=pl.ANY),) * 2,
         scratch_shapes=dma_pairs + [dma_pairs[2], dma_pairs[3], dma_pairs[0], dma_pairs[1]]
         + [pltpu.SemaphoreType.DMA((2,))],
         compiler_params=pltpu.CompilerParams(collective_id=kernel_id, has_side_effects=True),
-    )(piece[:, :half], piece[:, half:])
-    total = z_count * p_count * rows
-    return jnp.concatenate(
-        [
-            first.transpose(1, 0, 2, 3).reshape(total, half),
-            second.reshape(total, cols - half),
-        ],
-        axis=1,
-    )
+    )(piece[:head], piece[head:])
+    joined = jnp.concatenate([first.transpose(1, 0, 2, 3), second], axis=2)
+    return joined.reshape(z_count * p_count * rows, cols)
 
 
 def _scatter_kernel(count, part_ref, out_ref, send_sems, recv_sems, local_sem):

time: 210 us -> 202 us (0.962)
  the two profiles are of different devices: /device:TPU:21 before, /device:TPU:1 now
where the time goes in v7:
time: 202 us; the launch traced here: 201 us
  Pallas kernels  164 us (81%)
  other arithmetic  17.4 us (9%)
  matrix products  10.6 us (5%)
  local copies, waits for them, and re-layouts  8.78 us (4%)
    pallas_call x2, Pallas kernels, gather_ctx(): pl.pallas_call(kernel, out_shape=(jax.ShapeDtypeStruct((p_count, z_count,...  131 us
    pallas_call x1, Pallas kernels, scatter_sum_tp(): pl.pallas_call(functools.partial(_scatter_kernel, count), out_shape=jax.S...  33.2 us
    concatenate x2, other arithmetic, gather_ctx(): joined = jnp.concatenate([first.transpose(1, 0, 2, 3), second], axis=2)  6.23 us
    unnamed x10, local copies, waits for them, and re-layouts  4.11 us

profile of v7, /device:TPU:1, one launch (start us, length us, event | category | flops | bytes accessed | tf_op | source)
XLA Modules:
  0.0 201.4 jit_solution(4005979698027866970)
XLA Ops:
  0.6 0.8 reduce-window.8
  1.5 0.7 broadcast_multiply_fusion
  2.1 0.8 select_reduce_fusion
  3.0 0.1 convert_reduce_fusion.1
  3.1 1.4 pad_maximum_fusion.3.second_ref
  4.4 0.1 iota_add_fusion
  4.5 0.1 add.96
  4.6 0.2 convert_reduce_fusion
  4.8 0.8 pad_maximum_fusion.2
  5.6 0.6 slice.70.first_ref
  6.3 2.8 %compare_and_fusion = pred[128,8192]{0,1:T(8,128)(4,1)S(1)} fusion(s32[128]{0:T(128)S(1)} %fusion.57, s32[128]{0:T(128)S(1)} %convert_reduce_fusion.1, s32[8192]{0:T(1024)S(1)} %add.96, s32[8192]{0:T(1024)S(1)} %convert_reduce_fusion), kind=kLoop, calls=%fused_computation.19 | loop fusion | flops 3145728 | bytes 1115136 | tf_op jit(solution)/shard_map/while/body/eval_jaxpr/and | solution.py:324
  9.0 78.9 %shard_map.95 = (bf16[8,8,48,768]{3,2,1,0:T(8,128)(2,1)}, bf16[8,8,16,768]{3,2,1,0:T(8,128)(2,1)}) custom-call(bf16[48,768]{1,0:T(8,128)(2,1)} %slice.70.first_ref, bf16[16,768]{1,0:T(8,128)(2,1)} %pad_maximum_fusion.3.second_ref), custom_call_target="tpu_custom_call" | custom-call | tf_op jit(solution)/shard_map/pallas_call | solution.py:138
  87.9 3.8 %pad_maximum_fusion = bf16[8,8,64,768]{3,2,0,1:T(8,128)(2,1)S(1)} fusion(bf16[8,8,48,768]{3,2,0,1:T(8,128)(2,1)} %bitcast.120, bf16[8,8,16,768]{3,2,1,0:T(8,128)(2,1)} %get-tuple-element.29), kind=kLoop, calls=%fused_computation.9 | loop fusion | flops 12582912 | bytes 12582912 | tf_op jit(solution)/shard_map/concatenate | solution.py:150
  91.7 0.0 copy-start.3
  91.7 0.0 copy-start.4
  91.8 0.7 copy.53
  92.5 0.0 copy-start
  92.5 2.7 %copy-done = bf16[8,8,64,768]{3,2,1,0:T(8,128)(2,1)} copy-done((bf16[8,8,64,768]{3,2,1,0:T(8,128)(2,1)}, bf16[8,8,64,768]{3,2,1,0:T(8,128)(2,1)S(1)}, u32[]{:S(2)}) %copy-start) | copy-done | bytes 6291480
  95.2 0.0 copy-done.3
  95.2 0.0 copy-done.4
  95.2 0.8 fusion.16
  96.0 0.1 multiply_reduce_fusion
  96.1 0.1 copy.61
  96.2 0.6 slice.73.second_ref
  96.8 0.6 slice.72.first_ref
  97.4 51.7 %shard_map.96 = (bf16[8,8,80,256]{3,2,1,0:T(8,128)(2,1)}, bf16[8,8,48,256]{3,2,1,0:T(8,128)(2,1)}) custom-call(bf16[80,256]{1,0:T(8,128)(2,1)} %slice.72.first_ref, bf16[48,256]{1,0:T(8,128)(2,1)} %slice.73.second_ref), custom_call_target="tpu_custom_call" | custom-call | tf_op jit(solution)/shard_map/pallas_call | solution.py:138
  149.1 2.4 %pad_maximum_fusion.1 = bf16[8,8,128,256]{3,2,0,1:T(8,128)(2,1)S(1)} fusion(bf16[8,8,80,256]{3,2,0,1:T(8,128)(2,1)} %bitcast.125, bf16[8,8,48,256]{3,2,1,0:T(8,128)(2,1)} %get-tuple-element.31), kind=kLoop, calls=%fused_computation.15 | loop fusion | flops 8388608 | bytes 8388608 | tf_op jit(solution)/shard_map/concatenate | solution.py:150
  151.5 0.5 copy.55
  152.0 0.0 copy-start.1
  152.0 0.7 fusion.63
  152.8 0.3 fusion.38
  153.1 1.0 copy-done.1
  154.0 0.5 fusion.31
  154.5 0.1 copy.62
  154.7 3.4 %fusion.64 = (f32[2,128]{1,0:T(2,128)S(1)}, f32[1,2,128,8192]{2,3,1,0:T(8,128)S(1)}) fusion(bf16[8192,256]{1,0:T(8,128)(2,1)} %bitcast.123, pred[128,8192]{0,1:T(8,128)(4,1)S(1)} %compare_and_fusion, bf16[132,512]{1,0:T(8,128)(2,1)S(1)} %fusion.16), kind=kOutput, calls=%fused_computation.90 | convolution fusion | flops 543162112 | bytes 11600896 | tf_op jit(solution)/shard_map/while/body/eval_jaxpr/tgjd,kgd->gjtk/dot_general | solution.py:328
  158.0 0.0 copy-start.2
  158.0 1.7 fusion.4
  159.7 0.5 copy-done.2
  160.2 1.7 fusion.35
  162.0 3.5 %convolution_convert_fusion.part_ref = bf16[132,4096]{1,0:T(8,128)(2,1)} fusion(bf16[4096,768]{1,0:T(8,128)(2,1)} %bitcast.119, bf16[4,256]{0,1:T(8,128)(2,1)S(1)} %copy.62, bf16[128,256]{0,1:T(8,128)(2,1)S(1)} %bitcast.128), kind=kOutput, calls=%fused_computation.10 | convolution fusion | flops 277499904 | bytes 3246080 | tf_op jit(solution)/shard_map/dot_general | solution.py:402
  165.5 33.2 %shard_map.97 = bf16[8,132,512]{2,1,0:T(8,128)(2,1)} custom-call(bf16[132,4096]{1,0:T(8,128)(2,1)} %convolution_convert_fusion.part_ref), custom_call_target="tpu_custom_call" | custom-call | tf_op jit(solution)/shard_map/pallas_call | solution.py:201
  198.7 1.4 reduce_sum.73
  200.1 0.6 slice.82
  200.7 0.7 slice.81
  (11 shorter events, 0.1 us)
Async XLA Ops:
  91.7 3.4 %copy-start.3 = (bf16[128,4096]{1,0:T(8,128)(2,1)S(1)}, bf16[128,4096]{1,0:T(8,128)(2,1)}, u32[]{:S(2)}) copy-start(bf16[128,4096]{1,0:T(8,128)(2,1)} %param.8) | copy-start | bytes 3145732
  91.7 3.4 %copy-start.4 = (bf16[4,4096]{1,0:T(4,128)(2,1)S(1)}, bf16[4,4096]{1,0:T(4,128)(2,1)}, u32[]{:S(2)}) copy-start(bf16[4,4096]{1,0:T(4,128)(2,1)} %param.9) | copy-start | bytes 98308
  92.5 2.7 %copy-start = (bf16[8,8,64,768]{3,2,1,0:T(8,128)(2,1)}, bf16[8,8,64,768]{3,2,1,0:T(8,128)(2,1)S(1)}, u32[]{:S(2)}) copy-start(bf16[8,8,64,768]{3,2,1,0:T(8,128)(2,1)S(1)} %copy.53) | copy-start | bytes 18874372
  152.0 2.0 %copy-start.1 = (bf16[8,8,128,256]{3,2,1,0:T(8,128)(2,1)}, bf16[8,8,128,256]{3,2,1,0:T(8,128)(2,1)S(1)}, u32[]{:S(2)}) copy-start(bf16[8,8,128,256]{3,2,1,0:T(8,128)(2,1)S(1)} %copy.55) | copy-start | bytes 12582916
  158.0 2.2 %copy-start.2 = (bf16[8,8,128,256]{3,2,1,0:T(8,128)(2,1)S(1)}, bf16[8,8,128,256]{3,2,1,0:T(8,128)(2,1)}, u32[]{:S(2)}) copy-start(bf16[8,8,128,256]{3,2,1,0:T(8,128)(2,1)} %copy-done.1) | copy-start | bytes 12582916

commit v8 on v7

--- a/solution.py
+++ b/solution.py
@@ -58,61 +58,125 @@
     lax.fori_loop(1, p_count, greet(p_peer, p_target), 0)
     pl.semaphore_wait(barrier, z_count + p_count - 2)
 
-    def exchange(count, peer_of, target_of, own_slot, src_of, dst_of, sems):
-        send_sems, recv_sems = sems
-
-        def copy(peer, slot):
-            return pltpu.make_async_remote_copy(
-                src_ref=src_of(slot),
-                dst_ref=dst_of(slot),
-                send_sem=send_sems.at[peer],
-                recv_sem=recv_sems.at[slot],
-                device_id={"ctx": target_of(peer)},
-                device_id_type=mesh_ids,
-            )
-
-        def start(step, carry):
-            copy(peer_of(step), own_slot).start()
-            return carry
-
-        def finish(step, carry):
-            peer = peer_of(step)
-            copy(peer, own_slot).wait_send()
-            copy(peer, peer).wait_recv()
-            return carry
-
-        return (lambda: lax.fori_loop(1, count, start, 0), lambda: lax.fori_loop(1, count, finish, 0))
+    def remote(src, dst, send_sem, recv_sem, target):
+        return pltpu.make_async_remote_copy(
+            src_ref=src,
+            dst_ref=dst,
+            send_sem=send_sem,
+            recv_sem=recv_sem,
+            device_id={"ctx": target},
+            device_id_type=mesh_ids,
+        )
+
+    def first_one(peer, slot):
+        return remote(
+            first_ref, first_out.at[p_me, slot], first_z[0].at[peer], first_z[1].at[slot],
+            z_target(peer),
+        )
+
+    def second_one(peer, slot):
+        return remote(
+            second_ref, second_out.at[z_me, slot], second_p[0].at[peer], second_p[1].at[slot],
+            p_target(peer),
+        )
+
+    def first_two(peer, row, slot):
+        return remote(
+            first_out.at[row, slot], first_out.at[row, slot], first_p[0].at[peer],
+            first_p[1].at[row], p_target(peer),
+        )
+
+    def second_two(peer, row, slot):
+        return remote(
+            second_out.at[row, slot], second_out.at[row, slot], second_z[0].at[peer],
+            second_z[1].at[row], z_target(peer),
+        )
+
+    def first_rows(peer, row):
+        return remote(
+            first_out.at[row], first_out.at[row], first_p[0].at[peer], first_p[1].at[row],
+            p_target(peer),
+        )
+
+    def second_rows(peer, row):
+        return remote(
+            second_out.at[row], second_out.at[row], second_z[0].at[peer], second_z[1].at[row],
+            z_target(peer),
+        )
 
     first_own = pltpu.make_async_copy(first_ref, first_out.at[p_me, z_me], local_sems.at[0])
     second_own = pltpu.make_async_copy(second_ref, second_out.at[z_me, p_me], local_sems.at[1])
     first_own.start()
     second_own.start()
-    first_one = exchange(
-        z_count, z_peer, z_target, z_me,
-        lambda slot: first_ref, lambda slot: first_out.at[p_me, slot], first_z,
-    )
-    second_one = exchange(
-        p_count, p_peer, p_target, p_me,
-        lambda slot: second_ref, lambda slot: second_out.at[z_me, slot], second_p,
-    )
-    first_two = exchange(
-        p_count, p_peer, p_target, p_me,
-        lambda slot: first_out.at[slot], lambda slot: first_out.at[slot], first_p,
-    )
-    second_two = exchange(
-        z_count, z_peer, z_target, z_me,
-        lambda slot: second_out.at[slot], lambda slot: second_out.at[slot], second_z,
-    )
-    first_one[0]()
-    second_one[0]()
-    first_one[1]()
+
+    def start_one(step, carry):
+        @pl.when(step < z_count)
+        def _():
+            first_one(z_peer(step), z_me).start()
+
+        @pl.when(step < p_count)
+        def _():
+            second_one(p_peer(step), p_me).start()
+
+        return carry
+
+    rounds = max(z_count, p_count)
+    lax.fori_loop(1, rounds, start_one, 0)
+
+    def forward_first(slot):
+        def body(step, carry):
+            first_two(p_peer(step), p_me, slot).start()
+            return carry
+
+        lax.fori_loop(1, p_count, body, 0)
+
+    def forward_second(slot):
+        def body(step, carry):
+            second_two(z_peer(step), z_me, slot).start()
+            return carry
+
+        lax.fori_loop(1, z_count, body, 0)
+
     first_own.wait()
-    first_two[0]()
-    second_one[1]()
+    forward_first(z_me)
     second_own.wait()
-    second_two[0]()
-    first_two[1]()
-    second_two[1]()
+    forward_second(p_me)
+
+    def relay(step, carry):
+        @pl.when(step < z_count)
+        def _():
+            slot = z_peer(step)
+            first_one(slot, slot).wait_recv()
+            forward_first(slot)
+
+        @pl.when(step < p_count)
+        def _():
+            slot = p_peer(step)
+            second_one(slot, slot).wait_recv()
+            forward_second(slot)
+
+        return carry
+
+    lax.fori_loop(1, rounds, relay, 0)
+
+    def drain(step, carry):
+        @pl.when(step < z_count)
+        def _():
+            peer = z_peer(step)
+            first_one(peer, z_me).wait_send()
+            second_rows(peer, z_me).wait_send()
+            second_rows(peer, peer).wait_recv()
+
+        @pl.when(step < p_count)
+        def _():
+            peer = p_peer(step)
+            second_one(peer, p_me).wait_send()
+            first_rows(peer, p_me).wait_send()
+            first_rows(peer, peer).wait_recv()
+
+        return carry
+
+    lax.fori_loop(1, rounds, drain, 0)
 
 
 def gather_ctx(piece, layout, kernel_id):

time: 202 us -> 193 us (0.955)
  Pallas kernels: 164 us -> 155 us
    pallas_call x2, Pallas kernels: 131 us -> 123 us  [gather_ctx(): pl.pallas_call(kernel, out_shape=(jax.ShapeDtypeStruct((p_count, z_count,...]
where the time goes in v8:
time: 193 us
  Pallas kernels  155 us (80%)
  other arithmetic  17.4 us (9%)
  matrix products  10.6 us (5%)
  local copies, waits for them, and re-layouts  8.78 us (5%)
    pallas_call x2, Pallas kernels, gather_ctx(): pl.pallas_call(kernel, out_shape=(jax.ShapeDtypeStruct((p_count, z_count,...  123 us
    pallas_call x1, Pallas kernels, scatter_sum_tp(): pl.pallas_call(functools.partial(_scatter_kernel, count), out_shape=jax.S...  31.9 us
    concatenate x2, other arithmetic, gather_ctx(): joined = jnp.concatenate([first.transpose(1, 0, 2, 3), second], axis=2)  6.23 us
    unnamed x10, local copies, waits for them, and re-layouts  4.11 us

profile of v8, /device:TPU:1, one launch (start us, length us, event | category | flops | bytes accessed | tf_op | source)
XLA Modules:
  0.0 192.7 jit_solution(5567842452417135297)
XLA Ops:
  0.6 0.8 reduce-window.8
  1.5 0.7 broadcast_multiply_fusion
  2.1 0.8 select_reduce_fusion
  3.0 0.1 convert_reduce_fusion.1
  3.1 1.4 pad_maximum_fusion.3.second_ref
  4.4 0.1 iota_add_fusion
  4.5 0.1 add.96
  4.6 0.2 convert_reduce_fusion
  4.8 0.8 pad_maximum_fusion.2
  5.6 0.6 slice.70.first_ref
  6.3 2.8 %compare_and_fusion = pred[128,8192]{0,1:T(8,128)(4,1)S(1)} fusion(s32[128]{0:T(128)S(1)} %fusion.57, s32[128]{0:T(128)S(1)} %convert_reduce_fusion.1, s32[8192]{0:T(1024)S(1)} %add.96, s32[8192]{0:T(1024)S(1)} %convert_reduce_fusion), kind=kLoop, calls=%fused_computation.19 | loop fusion | flops 3145728 | bytes 1115136 | tf_op jit(solution)/shard_map/while/body/eval_jaxpr/and | solution.py:388
  9.0 69.6 %shard_map.95 = (bf16[8,8,48,768]{3,2,1,0:T(8,128)(2,1)}, bf16[8,8,16,768]{3,2,1,0:T(8,128)(2,1)}) custom-call(bf16[48,768]{1,0:T(8,128)(2,1)} %slice.70.first_ref, bf16[16,768]{1,0:T(8,128)(2,1)} %pad_maximum_fusion.3.second_ref), custom_call_target="tpu_custom_call" | custom-call | tf_op jit(solution)/shard_map/pallas_call | solution.py:202
  78.7 3.8 %pad_maximum_fusion = bf16[8,8,64,768]{3,2,0,1:T(8,128)(2,1)S(1)} fusion(bf16[8,8,48,768]{3,2,0,1:T(8,128)(2,1)} %bitcast.120, bf16[8,8,16,768]{3,2,1,0:T(8,128)(2,1)} %get-tuple-element.29), kind=kLoop, calls=%fused_computation.9 | loop fusion | flops 12582912 | bytes 12582912 | tf_op jit(solution)/shard_map/concatenate | solution.py:214
  82.5 0.0 copy-start.3
  82.5 0.0 copy-start.4
  82.5 0.7 copy.53
  83.2 0.0 copy-start
  83.2 2.7 %copy-done = bf16[8,8,64,768]{3,2,1,0:T(8,128)(2,1)} copy-done((bf16[8,8,64,768]{3,2,1,0:T(8,128)(2,1)}, bf16[8,8,64,768]{3,2,1,0:T(8,128)(2,1)S(1)}, u32[]{:S(2)}) %copy-start) | copy-done | bytes 6291480
  85.9 0.0 copy-done.3
  85.9 0.0 copy-done.4
  85.9 0.8 fusion.16
  86.7 0.1 multiply_reduce_fusion
  86.8 0.1 copy.61
  86.9 0.6 slice.73.second_ref
  87.5 0.6 slice.72.first_ref
  88.1 53.6 %shard_map.96 = (bf16[8,8,80,256]{3,2,1,0:T(8,128)(2,1)}, bf16[8,8,48,256]{3,2,1,0:T(8,128)(2,1)}) custom-call(bf16[80,256]{1,0:T(8,128)(2,1)} %slice.72.first_ref, bf16[48,256]{1,0:T(8,128)(2,1)} %slice.73.second_ref), custom_call_target="tpu_custom_call" | custom-call | tf_op jit(solution)/shard_map/pallas_call | solution.py:202
  141.7 2.4 %pad_maximum_fusion.1 = bf16[8,8,128,256]{3,2,0,1:T(8,128)(2,1)S(1)} fusion(bf16[8,8,80,256]{3,2,0,1:T(8,128)(2,1)} %bitcast.125, bf16[8,8,48,256]{3,2,1,0:T(8,128)(2,1)} %get-tuple-element.31), kind=kLoop, calls=%fused_computation.15 | loop fusion | flops 8388608 | bytes 8388608 | tf_op jit(solution)/shard_map/concatenate | solution.py:214
  144.1 0.5 copy.55
  144.6 0.0 copy-start.1
  144.6 0.7 fusion.63
  145.4 0.3 fusion.38
  145.7 1.0 copy-done.1
  146.7 0.5 fusion.31
  147.1 0.1 copy.62
  147.3 3.4 %fusion.64 = (f32[2,128]{1,0:T(2,128)S(1)}, f32[1,2,128,8192]{2,3,1,0:T(8,128)S(1)}) fusion(bf16[8192,256]{1,0:T(8,128)(2,1)} %bitcast.123, pred[128,8192]{0,1:T(8,128)(4,1)S(1)} %compare_and_fusion, bf16[132,512]{1,0:T(8,128)(2,1)S(1)} %fusion.16), kind=kOutput, calls=%fused_computation.90 | convolution fusion | flops 543162112 | bytes 11600896 | tf_op jit(solution)/shard_map/while/body/eval_jaxpr/tgjd,kgd->gjtk/dot_general | solution.py:392
  150.7 0.0 copy-start.2
  150.7 1.7 fusion.4
  152.4 0.5 copy-done.2
  152.8 1.7 fusion.35
  154.6 3.5 %convolution_convert_fusion.part_ref = bf16[132,4096]{1,0:T(8,128)(2,1)} fusion(bf16[4096,768]{1,0:T(8,128)(2,1)} %bitcast.119, bf16[4,256]{0,1:T(8,128)(2,1)S(1)} %copy.62, bf16[128,256]{0,1:T(8,128)(2,1)S(1)} %bitcast.128), kind=kOutput, calls=%fused_computation.10 | convolution fusion | flops 277499904 | bytes 3246080 | tf_op jit(solution)/shard_map/dot_general | solution.py:466
  158.1 31.9 %shard_map.97 = bf16[8,132,512]{2,1,0:T(8,128)(2,1)} custom-call(bf16[132,4096]{1,0:T(8,128)(2,1)} %convolution_convert_fusion.part_ref), custom_call_target="tpu_custom_call" | custom-call | tf_op jit(solution)/shard_map/pallas_call | solution.py:265
  190.0 1.4 reduce_sum.73
  191.4 0.6 slice.82
  192.0 0.7 slice.81
  (11 shorter events, 0.1 us)
Async XLA Ops:
  82.5 3.4 %copy-start.3 = (bf16[128,4096]{1,0:T(8,128)(2,1)S(1)}, bf16[128,4096]{1,0:T(8,128)(2,1)}, u32[]{:S(2)}) copy-start(bf16[128,4096]{1,0:T(8,128)(2,1)} %param.8) | copy-start | bytes 3145732
  82.5 3.4 %copy-start.4 = (bf16[4,4096]{1,0:T(4,128)(2,1)S(1)}, bf16[4,4096]{1,0:T(4,128)(2,1)}, u32[]{:S(2)}) copy-start(bf16[4,4096]{1,0:T(4,128)(2,1)} %param.9) | copy-start | bytes 98308
  83.2 2.7 %copy-start = (bf16[8,8,64,768]{3,2,1,0:T(8,128)(2,1)}, bf16[8,8,64,768]{3,2,1,0:T(8,128)(2,1)S(1)}, u32[]{:S(2)}) copy-start(bf16[8,8,64,768]{3,2,1,0:T(8,128)(2,1)S(1)} %copy.53) | copy-start | bytes 18874372
  144.6 2.0 %copy-start.1 = (bf16[8,8,128,256]{3,2,1,0:T(8,128)(2,1)}, bf16[8,8,128,256]{3,2,1,0:T(8,128)(2,1)S(1)}, u32[]{:S(2)}) copy-start(bf16[8,8,128,256]{3,2,1,0:T(8,128)(2,1)S(1)} %copy.55) | copy-start | bytes 12582916
  150.7 2.2 %copy-start.2 = (bf16[8,8,128,256]{3,2,1,0:T(8,128)(2,1)S(1)}, bf16[8,8,128,256]{3,2,1,0:T(8,128)(2,1)}, u32[]{:S(2)}) copy-start(bf16[8,8,128,256]{3,2,1,0:T(8,128)(2,1)} %copy-done.1) | copy-start | bytes 12582916

commit v9 on v8

--- a/solution.py
+++ b/solution.py
@@ -182,9 +182,17 @@
 def gather_ctx(piece, layout, kernel_id):
     z_count, p_count = layout
     rows, cols = piece.shape
-    tile = 16
-    head = min(rows - tile, max(tile, round(rows * 2 / (3 * tile)) * tile))
-    tail = rows - head
+    lane = 128
+    by_columns = cols % (3 * lane) == 0
+    if by_columns:
+        head = 2 * cols // 3
+        shapes = ((rows, head), (rows, cols - head))
+        pieces = (piece[:, :head], piece[:, head:])
+    else:
+        tile = 16
+        head = min(rows - tile, max(tile, round(rows * 2 / (3 * tile)) * tile))
+        shapes = ((head, cols), (rows - head, cols))
+        pieces = (piece[:head], piece[head:])
     dma_pairs = [
         pltpu.SemaphoreType.DMA((z_count,)),
         pltpu.SemaphoreType.DMA((z_count,)),
@@ -202,16 +210,16 @@
     first, second = pl.pallas_call(
         kernel,
         out_shape=(
-            jax.ShapeDtypeStruct((p_count, z_count, head, cols), piece.dtype),
-            jax.ShapeDtypeStruct((z_count, p_count, tail, cols), piece.dtype),
+            jax.ShapeDtypeStruct((p_count, z_count) + shapes[0], piece.dtype),
+            jax.ShapeDtypeStruct((z_count, p_count) + shapes[1], piece.dtype),
         ),
         in_specs=[pl.BlockSpec(memory_space=pl.ANY)] * 2,
         out_specs=(pl.BlockSpec(memory_space=pl.ANY),) * 2,
         scratch_shapes=dma_pairs + [dma_pairs[2], dma_pairs[3], dma_pairs[0], dma_pairs[1]]
         + [pltpu.SemaphoreType.DMA((2,))],
         compiler_params=pltpu.CompilerParams(collective_id=kernel_id, has_side_effects=True),
-    )(piece[:head], piece[head:])
-    joined = jnp.concatenate([first.transpose(1, 0, 2, 3), second], axis=2)
+    )(*pieces)
+    joined = jnp.concatenate([first.transpose(1, 0, 2, 3), second], axis=3 if by_columns else 2)
     return joined.reshape(z_count * p_count * rows, cols)
 
 

time: 193 us -> 186 us (0.964)
  Pallas kernels: 155 us -> 149 us
    pallas_call x2, Pallas kernels: 123 us -> 117 us  [gather_ctx(): pl.pallas_call(kernel, out_shape=(jax.ShapeDtypeStruct((p_count, z_count)...]
where the time goes in v9:
time: 186 us; the launch traced here: 184 us
  Pallas kernels  149 us (80%)
  other arithmetic  16.2 us (9%)
  matrix products  10.6 us (6%)
  local copies, waits for them, and re-layouts  8.14 us (4%)
    pallas_call x2, Pallas kernels, gather_ctx(): pl.pallas_call(kernel, out_shape=(jax.ShapeDtypeStruct((p_count, z_count)...  117 us
    pallas_call x1, Pallas kernels, scatter_sum_tp(): pl.pallas_call(functools.partial(_scatter_kernel, count), out_shape=jax.S...  31.7 us
    concatenate x2, other arithmetic, gather_ctx(): jnp.concatenate([first.transpose(1, 0, 2, 3), second], axis=3 if by_colum...  5.82 us
    unnamed x10, local copies, waits for them, and re-layouts  4.11 us

profile of v9, /device:TPU:1, one launch (start us, length us, event | category | flops | bytes accessed | tf_op | source)
XLA Modules:
  0.0 184.5 jit_solution(384835115273567570)
XLA Ops:
  0.6 0.8 reduce-window.8
  1.5 0.7 broadcast_multiply_fusion
  2.1 0.8 select_reduce_fusion
  3.0 0.1 convert_reduce_fusion.1
  3.1 0.1 iota_add_fusion
  3.2 0.1 add.96
  3.2 0.2 convert_reduce_fusion
  3.4 1.4 pad_maximum_fusion.2.first_ref
  4.9 2.8 %compare_and_fusion = pred[128,8192]{0,1:T(8,128)(4,1)S(1)} fusion(s32[128]{0:T(128)S(1)} %fusion.57, s32[128]{0:T(128)S(1)} %convert_reduce_fusion.1, s32[8192]{0:T(1024)S(1)} %add.96, s32[8192]{0:T(1024)S(1)} %convert_reduce_fusion), kind=kLoop, calls=%fused_computation.19 | loop fusion | flops 3145728 | bytes 1115136 | tf_op jit(solution)/shard_map/while/body/eval_jaxpr/and | solution.py:396
  7.6 70.3 %shard_map.95 = (bf16[8,8,64,512]{3,2,1,0:T(8,128)(2,1)}, bf16[8,8,64,256]{3,2,1,0:T(8,128)(2,1)}) custom-call(bf16[64,512]{1,0:T(8,128)(2,1)} %pad_maximum_fusion.2.first_ref, bf16[64,256]{1,0:T(8,128)(2,1)} %bitcast.127), custom_call_target="tpu_custom_call" | custom-call | tf_op jit(solution)/shard_map/pallas_call | solution.py:210
  77.9 3.4 %pad_maximum_fusion = bf16[8,8,64,768]{3,2,0,1:T(8,128)(2,1)S(1)} fusion(bf16[8,8,64,512]{3,2,0,1:T(8,128)(2,1)} %bitcast.120, bf16[8,8,64,256]{3,2,1,0:T(8,128)(2,1)} %get-tuple-element.29), kind=kLoop, calls=%fused_computation.9 | loop fusion | flops 12582912 | bytes 12582912 | tf_op jit(solution)/shard_map/concatenate | solution.py:222
  81.3 0.0 copy-start.3
  81.3 0.0 copy-start.4
  81.3 0.7 copy.53
  82.1 0.0 copy-start
  82.1 2.7 %copy-done = bf16[8,8,64,768]{3,2,1,0:T(8,128)(2,1)} copy-done((bf16[8,8,64,768]{3,2,1,0:T(8,128)(2,1)}, bf16[8,8,64,768]{3,2,1,0:T(8,128)(2,1)S(1)}, u32[]{:S(2)}) %copy-start) | copy-done | bytes 6291480
  84.7 0.0 copy-done.3
  84.7 0.0 copy-done.4
  84.8 0.8 fusion.16
  85.6 0.1 multiply_reduce_fusion
  85.7 0.1 copy.61
  85.7 0.6 slice.64.second_ref
  86.4 0.6 slice.63.first_ref
  87.0 46.7 %shard_map.96 = (bf16[8,8,80,256]{3,2,1,0:T(8,128)(2,1)}, bf16[8,8,48,256]{3,2,1,0:T(8,128)(2,1)}) custom-call(bf16[80,256]{1,0:T(8,128)(2,1)} %slice.63.first_ref, bf16[48,256]{1,0:T(8,128)(2,1)} %slice.64.second_ref), custom_call_target="tpu_custom_call" | custom-call | tf_op jit(solution)/shard_map/pallas_call | solution.py:210
  133.6 2.4 %pad_maximum_fusion.1 = bf16[8,8,128,256]{3,2,0,1:T(8,128)(2,1)S(1)} fusion(bf16[8,8,80,256]{3,2,0,1:T(8,128)(2,1)} %bitcast.125, bf16[8,8,48,256]{3,2,1,0:T(8,128)(2,1)} %get-tuple-element.31), kind=kLoop, calls=%fused_computation.15 | loop fusion | flops 8388608 | bytes 8388608 | tf_op jit(solution)/shard_map/concatenate | solution.py:222
  136.1 0.5 copy.55
  136.6 0.0 copy-start.1
  136.6 0.7 fusion.63
  137.4 0.3 fusion.38
  137.7 1.0 copy-done.1
  138.6 0.5 fusion.31
  139.1 0.1 copy.62
  139.2 3.4 %fusion.64 = (f32[2,128]{1,0:T(2,128)S(1)}, f32[1,2,128,8192]{2,3,1,0:T(8,128)S(1)}) fusion(bf16[8192,256]{1,0:T(8,128)(2,1)} %bitcast.123, pred[128,8192]{0,1:T(8,128)(4,1)S(1)} %compare_and_fusion, bf16[132,512]{1,0:T(8,128)(2,1)S(1)} %fusion.16), kind=kOutput, calls=%fused_computation.89 | convolution fusion | flops 543162112 | bytes 11600896 | tf_op jit(solution)/shard_map/while/body/eval_jaxpr/tgjd,kgd->gjtk/dot_general | solution.py:400
  142.6 0.0 copy-start.2
  142.6 1.7 fusion.4
  144.3 0.5 copy-done.2
  144.8 1.7 fusion.35
  146.6 3.5 %convolution_convert_fusion.part_ref = bf16[132,4096]{1,0:T(8,128)(2,1)} fusion(bf16[4096,768]{1,0:T(8,128)(2,1)} %bitcast.119, bf16[4,256]{0,1:T(8,128)(2,1)S(1)} %copy.62, bf16[128,256]{0,1:T(8,128)(2,1)S(1)} %bitcast.126), kind=kOutput, calls=%fused_computation.10 | convolution fusion | flops 277499904 | bytes 3246080 | tf_op jit(solution)/shard_map/dot_general | solution.py:474
  150.0 31.7 %shard_map.97 = bf16[8,132,512]{2,1,0:T(8,128)(2,1)} custom-call(bf16[132,4096]{1,0:T(8,128)(2,1)} %convolution_convert_fusion.part_ref), custom_call_target="tpu_custom_call" | custom-call | tf_op jit(solution)/shard_map/pallas_call | solution.py:273
  181.8 1.4 reduce_sum.73
  183.2 0.6 slice.73
  183.8 0.7 slice.72
  (11 shorter events, 0.1 us)
Async XLA Ops:
  81.3 3.4 %copy-start.3 = (bf16[128,4096]{1,0:T(8,128)(2,1)S(1)}, bf16[128,4096]{1,0:T(8,128)(2,1)}, u32[]{:S(2)}) copy-start(bf16[128,4096]{1,0:T(8,128)(2,1)} %param.8) | copy-start | bytes 3145732
  81.3 3.4 %copy-start.4 = (bf16[4,4096]{1,0:T(4,128)(2,1)S(1)}, bf16[4,4096]{1,0:T(4,128)(2,1)}, u32[]{:S(2)}) copy-start(bf16[4,4096]{1,0:T(4,128)(2,1)} %param.9) | copy-start | bytes 98308
  82.1 2.7 %copy-start = (bf16[8,8,64,768]{3,2,1,0:T(8,128)(2,1)}, bf16[8,8,64,768]{3,2,1,0:T(8,128)(2,1)S(1)}, u32[]{:S(2)}) copy-start(bf16[8,8,64,768]{3,2,1,0:T(8,128)(2,1)S(1)} %copy.53) | copy-start | bytes 18874372
  136.6 2.0 %copy-start.1 = (bf16[8,8,128,256]{3,2,1,0:T(8,128)(2,1)}, bf16[8,8,128,256]{3,2,1,0:T(8,128)(2,1)S(1)}, u32[]{:S(2)}) copy-start(bf16[8,8,128,256]{3,2,1,0:T(8,128)(2,1)S(1)} %copy.55) | copy-start | bytes 12582916
  142.6 2.2 %copy-start.2 = (bf16[8,8,128,256]{3,2,1,0:T(8,128)(2,1)S(1)}, bf16[8,8,128,256]{3,2,1,0:T(8,128)(2,1)}, u32[]{:S(2)}) copy-start(bf16[8,8,128,256]{3,2,1,0:T(8,128)(2,1)} %copy-done.1) | copy-start | bytes 12582916

commit v10 on v9

--- a/solution.py
+++ b/solution.py
@@ -285,6 +285,92 @@
     return jnp.sum(pieces.astype(jnp.float32), axis=0)
 
 
+def _exchange_kernel(count, stride, part_ref, out_ref, send_sems, recv_sems, local_sem):
+    me = lax.axis_index("tp")
+    pos = lax.rem(me // stride, count)
+    base = me - pos * stride
+    mesh_ids = pl.DeviceIdType.MESH
+    barrier = pltpu.get_barrier_semaphore()
+
+    def peer_of(step):
+        return lax.rem(pos + step, count)
+
+    def greet(step, carry):
+        target = base + peer_of(step) * stride
+        pl.semaphore_signal(barrier, 1, device_id={"tp": target}, device_id_type=mesh_ids)
+        return carry
+
+    lax.fori_loop(1, count, greet, 0)
+    pl.semaphore_wait(barrier, count - 1)
+    own = pltpu.make_async_copy(part_ref.at[pos], out_ref.at[pos], local_sem)
+    own.start()
+
+    def remote(peer, slot):
+        return pltpu.make_async_remote_copy(
+            src_ref=part_ref.at[peer],
+            dst_ref=out_ref.at[slot],
+            send_sem=send_sems.at[peer],
+            recv_sem=recv_sems.at[slot],
+            device_id={"tp": base + peer * stride},
+            device_id_type=mesh_ids,
+        )
+
+    def send(step, carry):
+        remote(peer_of(step), pos).start()
+        return carry
+
+    def finish(step, carry):
+        peer = peer_of(step)
+        remote(peer, pos).wait_send()
+        remote(peer, peer).wait_recv()
+        return carry
+
+    lax.fori_loop(1, count, send, 0)
+    lax.fori_loop(1, count, finish, 0)
+    own.wait()
+
+
+def exchange_tp(part, count, stride, kernel_id):
+    return pl.pallas_call(
+        functools.partial(_exchange_kernel, count, stride),
+        out_shape=jax.ShapeDtypeStruct(part.shape, part.dtype),
+        in_specs=[pl.BlockSpec(memory_space=pl.ANY)],
+        out_specs=pl.BlockSpec(memory_space=pl.ANY),
+        scratch_shapes=[
+            pltpu.SemaphoreType.DMA((count,)),
+            pltpu.SemaphoreType.DMA((count,)),
+            pltpu.SemaphoreType.DMA(()),
+        ],
+        compiler_params=pltpu.CompilerParams(collective_id=kernel_id, has_side_effects=True),
+    )(part)
+
+
+def scatter_sum_pairs(part, count):
+    rows, cols = part.shape
+    width = cols // count
+    outer = count // 2
+    pieces = part.reshape(rows, outer, 2, width).transpose(2, 1, 0, 3)
+    pieces = pieces.reshape(2, outer * rows, width)
+    paired = exchange_tp(pieces, 2, 1, 2)
+    paired = jnp.sum(paired.astype(jnp.float32), axis=0).astype(part.dtype)
+    spread = exchange_tp(paired.reshape(outer, rows, width), outer, 2, 3)
+    return jnp.sum(spread.astype(jnp.float32), axis=0)
+
+
+def tp_paired(mesh):
+    count = mesh.shape["tp"]
+    row = mesh.devices.transpose(
+        mesh.axis_names.index("ctx"), mesh.axis_names.index("tp")
+    )[0, :]
+    if count % 2 or count < 4:
+        return False
+    try:
+        chips = [tuple(device.coords) for device in row]
+    except (AttributeError, TypeError):
+        return False
+    return all(chips[index] == chips[index + 1] for index in range(0, count, 2))
+
+
 def ctx_layout(mesh):
     count = mesh.shape["ctx"]
     column = mesh.devices.transpose(
@@ -352,7 +438,7 @@
 
 
 def on_device(
-    layout, tp_count, tokens, new_token_states, w_query, key_matrix, value_matrix, w_out, lengths, block_map
+    layout, tp_count, paired, tokens, new_token_states, w_query, key_matrix, value_matrix, w_out, lengths, block_map
 ):
     local_rows = tokens.shape[0]
     block_rows = local_rows // 2
@@ -476,14 +562,17 @@
         out_weight,
         preferred_element_type=jnp.float32,
     )
-    summed_rows = scatter_sum_tp(projected.astype(jnp.bfloat16), tp_count, 2)
+    if paired:
+        summed_rows = scatter_sum_pairs(projected.astype(jnp.bfloat16), tp_count)
+    else:
+        summed_rows = scatter_sum_tp(projected.astype(jnp.bfloat16), tp_count, 2)
     summed_rows = summed_rows.astype(jnp.bfloat16)
     return (summed_rows[:local_rows], summed_rows[local_rows:])
 
 
 def solution(mesh):
     return jax.shard_map(
-        functools.partial(on_device, ctx_layout(mesh), mesh.shape["tp"]),
+        functools.partial(on_device, ctx_layout(mesh), mesh.shape["tp"], tp_paired(mesh)),
         mesh=mesh,
         in_specs=(
             P("ctx", None),

time: 186 us -> 196 us (1.054)
  Pallas kernels: 149 us -> 156 us
  local copies, waits for them, and re-layouts: 8.14 us -> 11.1 us
    pallas_call x1 -> x2, Pallas kernels: 31.7 us -> 39.1 us  [exchange_tp(): pl.pallas_call(functools.partial(_exchange_kernel, count, stride), out_sh...]
    reshape x0 -> x4, local copies, waits for them, and re-layouts: none -> 2.96 us  [the longest x1 1.11 us: scatter_sum_pairs(): pieces = pieces.reshape(2, outer * rows, width)]
where the time goes in v10:
time: 196 us; the launch traced here: 195 us
  Pallas kernels  156 us (80%)
  other arithmetic  17.7 us (9%)
  local copies, waits for them, and re-layouts  11.1 us (6%)
  matrix products  9.55 us (5%)
    pallas_call x2, Pallas kernels, gather_ctx(): pl.pallas_call(kernel, out_shape=(jax.ShapeDtypeStruct((p_count, z_count)...  117 us
    pallas_call x2, Pallas kernels, exchange_tp(): pl.pallas_call(functools.partial(_exchange_kernel, count, stride), out_sh...  39.1 us
    concatenate x2, other arithmetic, gather_ctx(): jnp.concatenate([first.transpose(1, 0, 2, 3), second], axis=3 if by_colum...  5.82 us
    unnamed x10, local copies, waits for them, and re-layouts  4.11 us

profile of v10, /device:TPU:1, one launch (start us, length us, event | category | flops | bytes accessed | tf_op | source)
XLA Modules:
  0.0 195.2 jit_solution(10232378779688458695)
XLA Ops:
  0.6 0.8 reduce-window.8
  1.5 0.7 broadcast_multiply_fusion
  2.1 0.8 select_reduce_fusion
  3.0 0.1 convert_reduce_fusion.1
  3.1 0.1 iota_add_fusion
  3.2 0.1 add.96
  3.2 0.2 convert_reduce_fusion
  3.4 1.4 pad_maximum_fusion.2.first_ref
  4.9 2.8 %compare_and_fusion = pred[128,8192]{0,1:T(8,128)(4,1)S(1)} fusion(s32[128]{0:T(128)S(1)} %fusion.57, s32[128]{0:T(128)S(1)} %convert_reduce_fusion.1, s32[8192]{0:T(1024)S(1)} %add.96, s32[8192]{0:T(1024)S(1)} %convert_reduce_fusion), kind=kLoop, calls=%fused_computation.19 | loop fusion | flops 3145728 | bytes 1115136 | tf_op jit(solution)/shard_map/while/body/eval_jaxpr/and | solution.py:482
  7.6 70.3 %shard_map.95 = (bf16[8,8,64,512]{3,2,1,0:T(8,128)(2,1)}, bf16[8,8,64,256]{3,2,1,0:T(8,128)(2,1)}) custom-call(bf16[64,512]{1,0:T(8,128)(2,1)} %pad_maximum_fusion.2.first_ref, bf16[64,256]{1,0:T(8,128)(2,1)} %bitcast.131), custom_call_target="tpu_custom_call" | custom-call | tf_op jit(solution)/shard_map/pallas_call | solution.py:210
  77.9 3.4 %pad_maximum_fusion = bf16[8,8,64,768]{3,2,0,1:T(8,128)(2,1)S(1)} fusion(bf16[8,8,64,512]{3,2,0,1:T(8,128)(2,1)} %bitcast.124, bf16[8,8,64,256]{3,2,1,0:T(8,128)(2,1)} %get-tuple-element.29), kind=kLoop, calls=%fused_computation.9 | loop fusion | flops 12582912 | bytes 12582912 | tf_op jit(solution)/shard_map/concatenate | solution.py:222
  81.3 0.0 copy-start.3
  81.3 0.0 copy-start.4
  81.3 0.7 copy.57
  82.1 0.0 copy-start
  82.1 2.7 %copy-done = bf16[8,8,64,768]{3,2,1,0:T(8,128)(2,1)} copy-done((bf16[8,8,64,768]{3,2,1,0:T(8,128)(2,1)}, bf16[8,8,64,768]{3,2,1,0:T(8,128)(2,1)S(1)}, u32[]{:S(2)}) %copy-start) | copy-done | bytes 6291480
  84.7 0.0 copy-done.3
  84.8 0.0 copy-done.4
  84.8 0.8 fusion.16
  85.6 0.1 multiply_reduce_fusion
  85.7 0.1 copy.65
  85.7 0.6 slice.64.second_ref
  86.4 0.6 slice.63.first_ref
  87.0 46.7 %shard_map.96 = (bf16[8,8,80,256]{3,2,1,0:T(8,128)(2,1)}, bf16[8,8,48,256]{3,2,1,0:T(8,128)(2,1)}) custom-call(bf16[80,256]{1,0:T(8,128)(2,1)} %slice.63.first_ref, bf16[48,256]{1,0:T(8,128)(2,1)} %slice.64.second_ref), custom_call_target="tpu_custom_call" | custom-call | tf_op jit(solution)/shard_map/pallas_call | solution.py:210
  133.6 2.4 %pad_maximum_fusion.1 = bf16[8,8,128,256]{3,2,0,1:T(8,128)(2,1)S(1)} fusion(bf16[8,8,80,256]{3,2,0,1:T(8,128)(2,1)} %bitcast.129, bf16[8,8,48,256]{3,2,1,0:T(8,128)(2,1)} %get-tuple-element.31), kind=kLoop, calls=%fused_computation.15 | loop fusion | flops 8388608 | bytes 8388608 | tf_op jit(solution)/shard_map/concatenate | solution.py:222
  136.1 0.5 copy.59
  136.6 0.0 copy-start.1
  136.6 0.7 fusion.63
  137.4 0.3 fusion.38
  137.7 1.0 copy-done.1
  138.6 0.5 fusion.31
  139.1 0.1 copy.66
  139.2 3.4 %fusion.64 = (f32[2,128]{1,0:T(2,128)S(1)}, f32[1,2,128,8192]{2,3,1,0:T(8,128)S(1)}) fusion(bf16[8192,256]{1,0:T(8,128)(2,1)} %bitcast.127, pred[128,8192]{0,1:T(8,128)(4,1)S(1)} %compare_and_fusion, bf16[132,512]{1,0:T(8,128)(2,1)S(1)} %fusion.16), kind=kOutput, calls=%fused_computation.90 | convolution fusion | flops 543162112 | bytes 11600896 | tf_op jit(solution)/shard_map/while/body/eval_jaxpr/tgjd,kgd->gjtk/dot_general | solution.py:486
  142.6 0.0 copy-start.2
  142.6 1.7 fusion.4
  144.3 0.5 copy-done.2
  144.8 1.8 fusion.35
  146.6 2.5 %convolution_convert_fusion = bf16[132,4096]{1,0:T(8,128)(2,1)S(1)} fusion(bf16[4096,768]{1,0:T(8,128)(2,1)} %bitcast.122, bf16[4,256]{0,1:T(8,128)(2,1)S(1)} %copy.66, bf16[128,256]{0,1:T(8,128)(2,1)S(1)} %bitcast.130), kind=kOutput, calls=%fused_computation.10 | convolution fusion | flops 277499904 | bytes 3246080 | tf_op jit(solution)/shard_map/dot_general | solution.py:560
  149.0 0.6 reshape.326
  149.7 0.3 copy.84
  150.0 1.1 reshape.327.part_ref
  151.1 21.4 %shard_map.97 = bf16[2,528,512]{2,1,0:T(8,128)(2,1)} custom-call(bf16[2,528,512]{2,1,0:T(8,128)(2,1)} %reshape.327.part_ref), custom_call_target="tpu_custom_call" | custom-call | tf_op jit(solution)/shard_map/pallas_call | solution.py:334
  172.5 1.7 reduce_sum.85
  174.2 0.9 reshape.328.part_ref
  175.1 17.7 %shard_map.98 = bf16[4,132,512]{2,1,0:T(8,128)(2,1)} custom-call(bf16[4,132,512]{2,1,0:T(8,128)(2,1)} %reshape.328.part_ref), custom_call_target="tpu_custom_call" | custom-call | tf_op jit(solution)/shard_map/pallas_call | solution.py:334
  192.8 1.1 reduce_sum.86
  193.9 0.6 slice.73
  194.5 0.7 slice.72
  (11 shorter events, 0.1 us)
Async XLA Ops:
  81.3 3.4 %copy-start.3 = (bf16[128,4096]{1,0:T(8,128)(2,1)S(1)}, bf16[128,4096]{1,0:T(8,128)(2,1)}, u32[]{:S(2)}) copy-start(bf16[128,4096]{1,0:T(8,128)(2,1)} %param.8) | copy-start | bytes 3145732
  81.3 3.4 %copy-start.4 = (bf16[4,4096]{1,0:T(4,128)(2,1)S(1)}, bf16[4,4096]{1,0:T(4,128)(2,1)}, u32[]{:S(2)}) copy-start(bf16[4,4096]{1,0:T(4,128)(2,1)} %param.9) | copy-start | bytes 98308
  82.1 2.7 %copy-start = (bf16[8,8,64,768]{3,2,1,0:T(8,128)(2,1)}, bf16[8,8,64,768]{3,2,1,0:T(8,128)(2,1)S(1)}, u32[]{:S(2)}) copy-start(bf16[8,8,64,768]{3,2,1,0:T(8,128)(2,1)S(1)} %copy.57) | copy-start | bytes 18874372
  136.6 2.0 %copy-start.1 = (bf16[8,8,128,256]{3,2,1,0:T(8,128)(2,1)}, bf16[8,8,128,256]{3,2,1,0:T(8,128)(2,1)S(1)}, u32[]{:S(2)}) copy-start(bf16[8,8,128,256]{3,2,1,0:T(8,128)(2,1)S(1)} %copy.59) | copy-start | bytes 12582916
  142.6 2.2 %copy-start.2 = (bf16[8,8,128,256]{3,2,1,0:T(8,128)(2,1)S(1)}, bf16[8,8,128,256]{3,2,1,0:T(8,128)(2,1)}, u32[]{:S(2)}) copy-start(bf16[8,8,128,256]{3,2,1,0:T(8,128)(2,1)} %copy-done.1) | copy-start | bytes 12582916

commit v11 on v9

--- a/solution.py
+++ b/solution.py
@@ -190,9 +190,11 @@
         pieces = (piece[:, :head], piece[:, head:])
     else:
         tile = 16
-        head = min(rows - tile, max(tile, round(rows * 2 / (3 * tile)) * tile))
-        shapes = ((head, cols), (rows - head, cols))
-        pieces = (piece[:head], piece[head:])
+        flat = piece.reshape(rows * cols // lane, lane)
+        count = flat.shape[0]
+        head = min(count - tile, max(tile, round(count * 2 / (3 * tile)) * tile))
+        shapes = ((head, lane), (count - head, lane))
+        pieces = (flat[:head], flat[head:])
     dma_pairs = [
         pltpu.SemaphoreType.DMA((z_count,)),
         pltpu.SemaphoreType.DMA((z_count,)),
@@ -220,6 +222,7 @@
         compiler_params=pltpu.CompilerParams(collective_id=kernel_id, has_side_effects=True),
     )(*pieces)
     joined = jnp.concatenate([first.transpose(1, 0, 2, 3), second], axis=3 if by_columns else 2)
+    joined = joined.reshape(z_count, p_count, rows, cols)
     return joined.reshape(z_count * p_count * rows, cols)
 
 

time: 186 us -> 193 us (1.038)
  local copies, waits for them, and re-layouts: 8.14 us -> 16.2 us
  Pallas kernels: 149 us -> 144 us
  matrix products: 10.6 us -> 13.7 us
    another operation x0 -> x1, local copies, waits for them, and re-layouts: none -> 7.1 us  [gather_ctx(): return joined.reshape(z_count * p_count * rows, cols)]
    pallas_call x2, Pallas kernels: 117 us -> 113 us  [gather_ctx(): pl.pallas_call(kernel, out_shape=(jax.ShapeDtypeStruct((p_count, z_count)...]
    unnamed x10 -> x8, local copies, waits for them, and re-layouts: 4.11 us -> 3.15 us
where the time goes in v11:
time: 193 us; the launch traced here: 191 us
  Pallas kernels  144 us (75%)
  other arithmetic  16.2 us (8%)
  local copies, waits for them, and re-layouts  16.2 us (8%)
  matrix products  13.7 us (7%)
    pallas_call x2, Pallas kernels, gather_ctx(): pl.pallas_call(kernel, out_shape=(jax.ShapeDtypeStruct((p_count, z_count)...  113 us
    pallas_call x1, Pallas kernels, scatter_sum_tp(): pl.pallas_call(functools.partial(_scatter_kernel, count), out_shape=jax.S...  31.1 us
    another operation x1, local copies, waits for them, and re-layouts, gather_ctx(): return joined.reshape(z_count * p_count * rows, cols)  7.1 us
    concatenate x2, other arithmetic, gather_ctx(): jnp.concatenate([first.transpose(1, 0, 2, 3), second], axis=3 if by_colum...  5.8 us

profile of v11, /device:TPU:1, one launch (start us, length us, event | category | flops | bytes accessed | tf_op | source)
XLA Modules:
  0.0 190.8 jit_solution(11701047186605755407)
XLA Ops:
  0.6 0.8 reduce-window.8
  1.5 0.7 broadcast_multiply_fusion
  2.1 0.8 select_reduce_fusion
  3.0 0.1 convert_reduce_fusion.1
  3.1 0.1 iota_add_fusion
  3.2 0.1 add.96
  3.2 0.2 convert_reduce_fusion
  3.4 1.4 pad_maximum_fusion.2.first_ref
  4.9 2.8 %compare_and_fusion = pred[128,8192]{0,1:T(8,128)(4,1)S(1)} fusion(s32[128]{0:T(128)S(1)} %fusion.57, s32[128]{0:T(128)S(1)} %convert_reduce_fusion.1, s32[8192]{0:T(1024)S(1)} %add.96, s32[8192]{0:T(1024)S(1)} %convert_reduce_fusion), kind=kLoop, calls=%fused_computation.19 | loop fusion | flops 3145728 | bytes 1115136 | tf_op jit(solution)/shard_map/while/body/eval_jaxpr/and | solution.py:399
  7.6 70.3 %shard_map.95 = (bf16[8,8,64,512]{3,2,1,0:T(8,128)(2,1)}, bf16[8,8,64,256]{3,2,1,0:T(8,128)(2,1)}) custom-call(bf16[64,512]{1,0:T(8,128)(2,1)} %pad_maximum_fusion.2.first_ref, bf16[64,256]{1,0:T(8,128)(2,1)} %bitcast.124), custom_call_target="tpu_custom_call" | custom-call | tf_op jit(solution)/shard_map/pallas_call | solution.py:212
  77.9 3.4 %pad_maximum_fusion = bf16[8,8,64,768]{3,2,0,1:T(8,128)(2,1)S(1)} fusion(bf16[8,8,64,512]{3,2,0,1:T(8,128)(2,1)} %bitcast.121, bf16[8,8,64,256]{3,2,1,0:T(8,128)(2,1)} %get-tuple-element.29), kind=kLoop, calls=%fused_computation.9 | loop fusion | flops 12582912 | bytes 12582912 | tf_op jit(solution)/shard_map/concatenate | solution.py:224
  81.3 0.0 copy-start.2
  81.3 0.0 copy-start.3
  81.3 0.7 copy.53
  82.1 0.0 copy-start
  82.1 2.7 %copy-done = bf16[8,8,64,768]{3,2,1,0:T(8,128)(2,1)} copy-done((bf16[8,8,64,768]{3,2,1,0:T(8,128)(2,1)}, bf16[8,8,64,768]{3,2,1,0:T(8,128)(2,1)S(1)}, u32[]{:S(2)}) %copy-start) | copy-done | bytes 6291480
  84.7 0.0 copy-done.2
  84.8 0.0 copy-done.3
  84.8 0.8 fusion.16
  85.6 0.1 multiply_reduce_fusion
  85.7 0.1 copy.61
  85.8 0.6 slice.60.second_ref
  86.4 0.6 slice.58.first_ref
  87.0 42.5 %shard_map.96 = (bf16[8,8,176,128]{3,2,1,0:T(8,128)(2,1)}, bf16[8,8,80,128]{3,2,1,0:T(8,128)(2,1)}) custom-call(bf16[176,128]{1,0:T(8,128)(2,1)} %slice.58.first_ref, bf16[80,128]{1,0:T(8,128)(2,1)} %slice.60.second_ref), custom_call_target="tpu_custom_call" | custom-call | tf_op jit(solution)/shard_map/pallas_call | solution.py:212
  129.5 2.4 %pad_maximum_fusion.1 = bf16[8,8,256,128]{3,2,0,1:T(8,128)(2,1)S(1)} fusion(bf16[8,8,176,128]{3,2,0,1:T(8,128)(2,1)} %bitcast.122, bf16[8,8,80,128]{3,2,1,0:T(8,128)(2,1)} %get-tuple-element.31), kind=kLoop, calls=%fused_computation.15 | loop fusion | flops 8388608 | bytes 8388608 | tf_op jit(solution)/shard_map/concatenate | solution.py:224
  131.9 2.3 %copy.55 = bf16[8,8,256,128]{3,2,1,0:T(8,128)(2,1)} copy(bf16[8,8,256,128]{3,2,0,1:T(8,128)(2,1)S(1)} %pad_maximum_fusion.1) | data formatting | bytes 8388608 | tf_op jit(solution)/shard_map/concatenate | solution.py:224
  134.3 7.1 %reshape_reshape.3 = bf16[8192,256]{1,0:T(8,128)(2,1)} reshape(bf16[8,8,256,128]{3,2,1,0:T(8,128)(2,1)} %copy.55) | data formatting | bytes 8388608 | tf_op jit(solution)/shard_map/reshape;reshape | solution.py:226
  141.4 2.3 %fusion.63 = (f32[4,2]{0,1:T(2,128)S(1)}, f32[4,1,2,8192]{3,0,2,1:T(4,128)S(1)}) fusion(bf16[132,512]{1,0:T(8,128)(2,1)S(1)} %fusion.16, bf16[8192,256]{1,0:T(8,128)(2,1)} %reshape_reshape.3, pred[4,8192]{1,0:T(4,128)(4,1)S(1)} %iota_compare_fusion), kind=kOutput, calls=%fused_computation.88 | convolution fusion | flops 16973816 | bytes 2394144 | tf_op jit(solution)/shard_map/rgjd,tgd->rgjt/dot_general | solution.py:336
  143.7 0.3 fusion.38
  144.0 2.1 %fusion.31 = bf16[4,256]{1,0:T(4,128)(2,1)S(1)} fusion(bf16[8192,256]{1,0:T(8,128)(2,1)} %reshape_reshape.3, f32[4,1,2,8192]{3,0,2,1:T(4,128)S(1)} %get-tuple-element.50, f32[4,2]{0,1:T(2,128)S(1)} %get-tuple-element.49, pred[4,8192]{1,0:T(4,128)(4,1)S(1)} %iota_compare_fusion, f32[4,2]{0,1:T(2,128)S(1)} %get-tuple-element.46, ...), kind=kOutput, calls=%fused_computation.35 | convolution fusion | flops 16978944 | bytes 2396288 | tf_op jit(solution)/shard_map/rgjt,tgd->rgjd/dot_general | solution.py:348
  146.1 0.1 copy.62
  146.2 3.4 %fusion.64 = (f32[2,128]{1,0:T(2,128)S(1)}, f32[1,2,128,8192]{2,3,1,0:T(8,128)S(1)}) fusion(bf16[8192,256]{1,0:T(8,128)(2,1)} %reshape_reshape.3, pred[128,8192]{0,1:T(8,128)(4,1)S(1)} %compare_and_fusion, bf16[132,512]{1,0:T(8,128)(2,1)S(1)} %fusion.16), kind=kOutput, calls=%fused_computation.89 | convolution fusion | flops 543162112 | bytes 11600896 | tf_op jit(solution)/shard_map/while/body/eval_jaxpr/tgjd,kgd->gjtk/dot_general | solution.py:403
  149.6 0.0 copy-start.1
  149.6 1.7 fusion.4
  151.3 0.5 copy-done.1
  151.8 1.7 fusion.35
  153.6 3.5 %convolution_convert_fusion.part_ref = bf16[132,4096]{1,0:T(8,128)(2,1)} fusion(bf16[4096,768]{1,0:T(8,128)(2,1)} %bitcast.120, bf16[4,256]{0,1:T(8,128)(2,1)S(1)} %copy.62, bf16[128,256]{0,1:T(8,128)(2,1)S(1)} %bitcast.123), kind=kOutput, calls=%fused_computation.10 | convolution fusion | flops 277499904 | bytes 3246080 | tf_op jit(solution)/shard_map/dot_general | solution.py:477
  157.0 31.1 %shard_map.97 = bf16[8,132,512]{2,1,0:T(8,128)(2,1)} custom-call(bf16[132,4096]{1,0:T(8,128)(2,1)} %convolution_convert_fusion.part_ref), custom_call_target="tpu_custom_call" | custom-call | tf_op jit(solution)/shard_map/pallas_call | solution.py:276
  188.1 1.4 reduce_sum.73
  189.6 0.6 slice.81
  190.2 0.7 slice.80
  (13 shorter events, 0.1 us)
Async XLA Ops:
  81.3 3.4 %copy-start.2 = (bf16[128,4096]{1,0:T(8,128)(2,1)S(1)}, bf16[128,4096]{1,0:T(8,128)(2,1)}, u32[]{:S(2)}) copy-start(bf16[128,4096]{1,0:T(8,128)(2,1)} %param.8) | copy-start | bytes 3145732
  81.3 3.4 %copy-start.3 = (bf16[4,4096]{1,0:T(4,128)(2,1)S(1)}, bf16[4,4096]{1,0:T(4,128)(2,1)}, u32[]{:S(2)}) copy-start(bf16[4,4096]{1,0:T(4,128)(2,1)} %param.9) | copy-start | bytes 98308
  82.1 2.7 %copy-start = (bf16[8,8,64,768]{3,2,1,0:T(8,128)(2,1)}, bf16[8,8,64,768]{3,2,1,0:T(8,128)(2,1)S(1)}, u32[]{:S(2)}) copy-start(bf16[8,8,64,768]{3,2,1,0:T(8,128)(2,1)S(1)} %copy.53) | copy-start | bytes 18874372
  149.6 2.2 %copy-start.1 = (bf16[8192,256]{1,0:T(8,128)(2,1)S(1)}, bf16[8192,256]{1,0:T(8,128)(2,1)}, u32[]{:S(2)}) copy-start(bf16[8192,256]{1,0:T(8,128)(2,1)} %reshape_reshape.3) | copy-start | bytes 12582916

commit v12 on v9

--- a/solution.py
+++ b/solution.py
@@ -179,7 +179,7 @@
     lax.fori_loop(1, rounds, drain, 0)
 
 
-def gather_ctx(piece, layout, kernel_id):
+def gather_ctx(piece, layout, kernel_id, parts=False):
     z_count, p_count = layout
     rows, cols = piece.shape
     lane = 128
@@ -219,6 +219,8 @@
         + [pltpu.SemaphoreType.DMA((2,))],
         compiler_params=pltpu.CompilerParams(collective_id=kernel_id, has_side_effects=True),
     )(*pieces)
+    if parts:
+        return first, second
     joined = jnp.concatenate([first.transpose(1, 0, 2, 3), second], axis=3 if by_columns else 2)
     return joined.reshape(z_count * p_count * rows, cols)
 
@@ -366,14 +368,32 @@
     device = lax.axis_index("ctx")
     request_ends = jnp.cumsum(lengths)
     inputs = jnp.concatenate([tokens, new_token_states], axis=0)
-    joined = gather_ctx(
-        jnp.concatenate([w_query, key_matrix, value_matrix, w_out.T], axis=1), layout, 0
-    )
+    z_count, p_count = layout
+    model_width = inputs.shape[1]
     qkv_width = query_width + 2 * kv_width
-    projected_all = jnp.dot(
-        inputs, joined[:, :qkv_width], preferred_element_type=jnp.float32
-    ).astype(jnp.bfloat16)
-    out_weight = joined[:, qkv_width:].T
+    if (qkv_width + w_out.shape[0]) % 384 == 0 and 2 * w_out.shape[0] == qkv_width:
+        qkv_rows, out_rows = gather_ctx(
+            jnp.concatenate([w_query, key_matrix, value_matrix, w_out.T], axis=1),
+            layout,
+            0,
+            parts=True,
+        )
+        row_block = model_width // (z_count * p_count)
+        permuted = inputs.reshape(-1, z_count, p_count, row_block).transpose(0, 2, 1, 3)
+        projected_all = jnp.dot(
+            permuted.reshape(-1, model_width),
+            qkv_rows.reshape(model_width, qkv_width),
+            preferred_element_type=jnp.float32,
+        ).astype(jnp.bfloat16)
+        out_weight_t = out_rows.reshape(model_width, w_out.shape[0])
+    else:
+        joined = gather_ctx(
+            jnp.concatenate([w_query, key_matrix, value_matrix, w_out.T], axis=1), layout, 0
+        )
+        projected_all = jnp.dot(
+            inputs, joined[:, :qkv_width], preferred_element_type=jnp.float32
+        ).astype(jnp.bfloat16)
+        out_weight_t = joined[:, qkv_width:]
     query_all = projected_all[:, :query_width]
     key_all = projected_all[:, query_width : query_width + kv_width]
     value_all = projected_all[:, query_width + kv_width :]
@@ -471,9 +491,10 @@
         (dec_mixed / dec_total[..., None]).reshape(request_count, query_width).astype(jnp.bfloat16)
     )
     attended_all = jnp.concatenate([attended, dec_attn], axis=0)
-    projected = jnp.dot(
+    projected = lax.dot_general(
         attended_all,
-        out_weight,
+        out_weight_t,
+        (((1,), (1,)), ((), ())),
         preferred_element_type=jnp.float32,
     )
     summed_rows = scatter_sum_tp(projected.astype(jnp.bfloat16), tp_count, 2)

time: 186 us -> 189 us (1.016)
  local copies, waits for them, and re-layouts: 8.14 us -> 11.9 us
  other arithmetic: 16.2 us -> 14.2 us
    reshape x0 -> x2, local copies, waits for them, and re-layouts: none -> 7.23 us  [on_device(): inputs.reshape(-1, z_count, p_count, row_block).transpose(0, 2, 1, 3)]
    concatenate x2 -> x1, other arithmetic: 5.82 us -> 2.43 us  [gather_ctx(): jnp.concatenate([first.transpose(1, 0, 2, 3), second], axis=3 if by_colum...]
    unnamed x10 -> x6, local copies, waits for them, and re-layouts: 4.11 us -> 1.33 us
where the time goes in v12:
time: 189 us; the launch traced here: 186 us
  Pallas kernels  148 us (78%)
  other arithmetic  14.2 us (8%)
  local copies, waits for them, and re-layouts  11.9 us (6%)
  matrix products  11.1 us (6%)
    pallas_call x2, Pallas kernels, gather_ctx(): pl.pallas_call(kernel, out_shape=(jax.ShapeDtypeStruct((p_count, z_count)...  117 us
    pallas_call x1, Pallas kernels, scatter_sum_tp(): pl.pallas_call(functools.partial(_scatter_kernel, count), out_shape=jax.S...  31.5 us
    reshape x2, local copies, waits for them, and re-layouts, on_device(): inputs.reshape(-1, z_count, p_count, row_block).transpose(0, 2, 1, 3)  7.23 us

profile of v12, /device:TPU:1, one launch (start us, length us, event | category | flops | bytes accessed | tf_op | source)
XLA Modules:
  0.0 186.5 jit_solution(17875169921069157030)
XLA Ops:
  0.6 0.8 reduce-window.8
  1.5 0.7 broadcast_multiply_fusion
  2.1 0.8 select_reduce_fusion
  3.0 0.1 convert_reduce_fusion.1
  3.1 0.1 iota_add_fusion
  3.2 0.1 add.96
  3.2 0.2 convert_reduce_fusion
  3.4 1.4 pad_maximum_fusion.2.first_ref
  4.9 2.8 %compare_and_fusion = pred[128,8192]{0,1:T(8,128)(4,1)S(1)} fusion(s32[128]{0:T(128)S(1)} %fusion.56, s32[128]{0:T(128)S(1)} %convert_reduce_fusion.1, s32[8192]{0:T(1024)S(1)} %add.96, s32[8192]{0:T(1024)S(1)} %convert_reduce_fusion), kind=kLoop, calls=%fused_computation.16 | loop fusion | flops 3145728 | bytes 1115136 | tf_op jit(solution)/shard_map/while/body/eval_jaxpr/and | solution.py:416
  7.6 1.3 pad_maximum_fusion.1
  9.0 3.6 %reshape.316 = bf16[132,8,8,64]{3,2,1,0:T(8,128)(2,1)} reshape(bf16[132,4096]{1,0:T(8,128)(2,1)S(1)} %pad_maximum_fusion.1) | data formatting | bytes 2162688 | tf_op jit(solution)/shard_map/reshape | solution.py:382
  12.6 3.6 %copy.48 = bf16[132,8,8,64]{0,3,1,2:T(8,128)(2,1)S(1)} copy(bf16[132,8,8,64]{3,2,1,0:T(8,128)(2,1)} %reshape.316) | data formatting | bytes 2162688 | tf_op jit(solution)/shard_map/reshape | solution.py:382
  16.2 70.3 %shard_map.95 = (bf16[8,8,64,512]{3,2,1,0:T(8,128)(2,1)}, bf16[8,8,64,256]{3,2,1,0:T(8,128)(2,1)}) custom-call(bf16[64,512]{1,0:T(8,128)(2,1)} %pad_maximum_fusion.2.first_ref, bf16[64,256]{1,0:T(8,128)(2,1)} %bitcast.139), custom_call_target="tpu_custom_call" | custom-call | tf_op jit(solution)/shard_map/pallas_call | solution.py:210
  86.5 3.0 %fusion.18 = bf16[132,512]{1,0:T(8,128)(2,1)S(1)} fusion(bf16[8,8,64,512]{3,2,1,0:T(8,128)(2,1)} %get-tuple-element.28, bf16[132,8,8,64]{0,3,1,2:T(8,128)(2,1)S(1)} %copy.48), kind=kOutput, calls=%fused_computation.23 | convolution fusion | flops 553715712 | bytes 5410816 | tf_op jit(solution)/shard_map/dot_general | solution.py:383
  89.5 0.1 multiply_reduce_fusion
  89.6 0.1 copy.56
  89.7 0.6 slice.55.second_ref
  90.3 0.6 slice.54.first_ref
  90.9 46.7 %shard_map.96 = (bf16[8,8,80,256]{3,2,1,0:T(8,128)(2,1)}, bf16[8,8,48,256]{3,2,1,0:T(8,128)(2,1)}) custom-call(bf16[80,256]{1,0:T(8,128)(2,1)} %slice.54.first_ref, bf16[48,256]{1,0:T(8,128)(2,1)} %slice.55.second_ref), custom_call_target="tpu_custom_call" | custom-call | tf_op jit(solution)/shard_map/pallas_call | solution.py:210
  137.6 2.4 %pad_maximum_fusion = bf16[8,8,128,256]{3,2,0,1:T(8,128)(2,1)S(1)} fusion(bf16[8,8,80,256]{3,2,0,1:T(8,128)(2,1)} %bitcast.136, bf16[8,8,48,256]{3,2,1,0:T(8,128)(2,1)} %get-tuple-element.30), kind=kLoop, calls=%fused_computation.12 | loop fusion | flops 8388608 | bytes 8388608 | tf_op jit(solution)/shard_map/concatenate | solution.py:224
  140.0 0.5 copy.50
  140.5 0.0 copy-start
  140.5 0.7 fusion.61
  141.3 0.3 fusion.37
  141.6 0.8 copy-done
  142.5 0.5 fusion.30
  142.9 0.1 copy.57
  143.1 3.4 %fusion.62 = (f32[2,128]{1,0:T(2,128)S(1)}, f32[1,2,128,8192]{2,3,1,0:T(8,128)S(1)}) fusion(bf16[8192,256]{1,0:T(8,128)(2,1)} %bitcast.134, pred[128,8192]{0,1:T(8,128)(4,1)S(1)} %compare_and_fusion, bf16[132,512]{1,0:T(8,128)(2,1)S(1)} %fusion.18), kind=kOutput, calls=%fused_computation.85 | convolution fusion | flops 543162112 | bytes 11600896 | tf_op jit(solution)/shard_map/while/body/eval_jaxpr/tgjd,kgd->gjtk/dot_general | solution.py:420
  146.4 0.0 copy-start.1
  146.4 1.7 fusion.4
  148.1 0.5 copy-done.1
  148.6 0.0 copy-start.2
  148.6 1.7 fusion.34
  150.4 0.0 copy-done.2
  150.4 1.8 convolution_convert_fusion.part_ref
  152.2 31.5 %shard_map.97 = bf16[8,132,512]{2,1,0:T(8,128)(2,1)} custom-call(bf16[132,4096]{1,0:T(8,128)(2,1)} %convolution_convert_fusion.part_ref), custom_call_target="tpu_custom_call" | custom-call | tf_op jit(solution)/shard_map/pallas_call | solution.py:275
  183.8 1.4 reduce_sum.73
  185.2 0.6 slice.63
  185.8 0.7 slice.62
  (11 shorter events, 0.1 us)
Async XLA Ops:
  140.5 1.9 %copy-start = (bf16[8,8,128,256]{3,2,1,0:T(8,128)(2,1)}, bf16[8,8,128,256]{3,2,1,0:T(8,128)(2,1)S(1)}, u32[]{:S(2)}) copy-start(bf16[8,8,128,256]{3,2,1,0:T(8,128)(2,1)S(1)} %copy.50) | copy-start | bytes 12582916
  146.4 2.2 %copy-start.1 = (bf16[8,8,128,256]{3,2,1,0:T(8,128)(2,1)S(1)}, bf16[8,8,128,256]{3,2,1,0:T(8,128)(2,1)}, u32[]{:S(2)}) copy-start(bf16[8,8,128,256]{3,2,1,0:T(8,128)(2,1)} %copy-done) | copy-start | bytes 12582916
  148.6 1.8 copy-start.2

commit v13 on v12

--- a/solution.py
+++ b/solution.py
@@ -70,7 +70,7 @@
 
     def first_one(peer, slot):
         return remote(
-            first_ref, first_out.at[p_me, slot], first_z[0].at[peer], first_z[1].at[slot],
+            first_ref, first_out.at[slot, p_me], first_z[0].at[peer], first_z[1].at[slot],
             z_target(peer),
         )
 
@@ -82,7 +82,7 @@
 
     def first_two(peer, row, slot):
         return remote(
-            first_out.at[row, slot], first_out.at[row, slot], first_p[0].at[peer],
+            first_out.at[slot, row], first_out.at[slot, row], first_p[0].at[peer],
             first_p[1].at[row], p_target(peer),
         )
 
@@ -94,7 +94,7 @@
 
     def first_rows(peer, row):
         return remote(
-            first_out.at[row], first_out.at[row], first_p[0].at[peer], first_p[1].at[row],
+            first_out.at[:, row], first_out.at[:, row], first_p[0].at[peer], first_p[1].at[row],
             p_target(peer),
         )
 
@@ -104,7 +104,7 @@
             z_target(peer),
         )
 
-    first_own = pltpu.make_async_copy(first_ref, first_out.at[p_me, z_me], local_sems.at[0])
+    first_own = pltpu.make_async_copy(first_ref, first_out.at[z_me, p_me], local_sems.at[0])
     second_own = pltpu.make_async_copy(second_ref, second_out.at[z_me, p_me], local_sems.at[1])
     first_own.start()
     second_own.start()
@@ -210,7 +210,7 @@
     first, second = pl.pallas_call(
         kernel,
         out_shape=(
-            jax.ShapeDtypeStruct((p_count, z_count) + shapes[0], piece.dtype),
+            jax.ShapeDtypeStruct((z_count, p_count) + shapes[0], piece.dtype),
             jax.ShapeDtypeStruct((z_count, p_count) + shapes[1], piece.dtype),
         ),
         in_specs=[pl.BlockSpec(memory_space=pl.ANY)] * 2,
@@ -221,7 +221,7 @@
     )(*pieces)
     if parts:
         return first, second
-    joined = jnp.concatenate([first.transpose(1, 0, 2, 3), second], axis=3 if by_columns else 2)
+    joined = jnp.concatenate([first, second], axis=3 if by_columns else 2)
     return joined.reshape(z_count * p_count * rows, cols)
 
 
@@ -378,10 +378,8 @@
             0,
             parts=True,
         )
-        row_block = model_width // (z_count * p_count)
-        permuted = inputs.reshape(-1, z_count, p_count, row_block).transpose(0, 2, 1, 3)
         projected_all = jnp.dot(
-            permuted.reshape(-1, model_width),
+            inputs,
             qkv_rows.reshape(model_width, qkv_width),
             preferred_element_type=jnp.float32,
         ).astype(jnp.bfloat16)

time: 189 us -> 180 us (0.952)
  local copies, waits for them, and re-layouts: 11.9 us -> 4.14 us
    reshape x2 -> x0, local copies, waits for them, and re-layouts: 7.23 us -> none  [on_device(): inputs.reshape(-1, z_count, p_count, row_block).transpose(0, 2, 1, 3)]
where the time goes in v13:
time: 180 us; the launch traced here: 178 us
  Pallas kernels  149 us (83%)
  other arithmetic  13.1 us (7%)
  matrix products  11.5 us (6%)
  local copies, waits for them, and re-layouts  4.14 us (2%)
    pallas_call x2, Pallas kernels, gather_ctx(): pl.pallas_call(kernel, out_shape=(jax.ShapeDtypeStruct((z_count, p_count)...  117 us
    pallas_call x1, Pallas kernels, scatter_sum_tp(): pl.pallas_call(functools.partial(_scatter_kernel, count), out_shape=jax.S...  31.7 us

profile of v13, /device:TPU:1, one launch (start us, length us, event | category | flops | bytes accessed | tf_op | source)
XLA Modules:
  0.0 178.2 jit_solution(10904224813107132003)
XLA Ops:
  0.6 0.8 reduce-window.8
  1.5 0.7 broadcast_multiply_fusion
  2.1 0.8 select_reduce_fusion
  3.0 0.1 convert_reduce_fusion.1
  3.1 0.1 iota_add_fusion
  3.2 0.1 add.96
  3.2 0.2 convert_reduce_fusion
  3.4 1.4 pad_maximum_fusion.1.first_ref
  4.9 2.8 %compare_and_fusion = pred[128,8192]{0,1:T(8,128)(4,1)S(1)} fusion(s32[128]{0:T(128)S(1)} %fusion.51, s32[128]{0:T(128)S(1)} %convert_reduce_fusion.1, s32[8192]{0:T(1024)S(1)} %add.96, s32[8192]{0:T(1024)S(1)} %convert_reduce_fusion), kind=kLoop, calls=%fused_computation.16 | loop fusion | flops 3145728 | bytes 1115136 | tf_op jit(solution)/shard_map/while/body/eval_jaxpr/and | solution.py:414
  7.6 70.3 %shard_map.95 = (bf16[8,8,64,512]{3,2,1,0:T(8,128)(2,1)}, bf16[8,8,64,256]{3,2,1,0:T(8,128)(2,1)}) custom-call(bf16[64,512]{1,0:T(8,128)(2,1)} %pad_maximum_fusion.1.first_ref, bf16[64,256]{1,0:T(8,128)(2,1)} %bitcast.123), custom_call_target="tpu_custom_call" | custom-call | tf_op jit(solution)/shard_map/pallas_call | solution.py:210
  77.9 3.3 %convolution_convert_fusion.1 = bf16[132,512]{1,0:T(8,128)(2,1)S(1)} fusion(bf16[4096,512]{1,0:T(8,128)(2,1)} %bitcast.126, bf16[4,4096]{1,0:T(4,128)(2,1)} %param.9, bf16[128,4096]{1,0:T(8,128)(2,1)} %param.8), kind=kOutput, calls=%fused_computation.20 | convolution fusion | flops 555878400 | bytes 5410816 | tf_op jit(solution)/shard_map/dot_general | solution.py:381
  81.2 0.1 multiply_reduce_fusion
  81.3 0.1 copy.39
  81.4 0.6 slice.55.second_ref
  82.0 0.6 slice.54.first_ref
  82.6 46.7 %shard_map.96 = (bf16[8,8,80,256]{3,2,1,0:T(8,128)(2,1)}, bf16[8,8,48,256]{3,2,1,0:T(8,128)(2,1)}) custom-call(bf16[80,256]{1,0:T(8,128)(2,1)} %slice.54.first_ref, bf16[48,256]{1,0:T(8,128)(2,1)} %slice.55.second_ref), custom_call_target="tpu_custom_call" | custom-call | tf_op jit(solution)/shard_map/pallas_call | solution.py:210
  129.3 2.7 %pad_maximum_fusion = bf16[8,8,128,256]{3,2,1,0:T(8,128)(2,1)S(1)} fusion(bf16[8,8,48,256]{3,2,1,0:T(8,128)(2,1)} %get-tuple-element.30, bf16[8,8,80,256]{3,2,1,0:T(8,128)(2,1)} %get-tuple-element.29), kind=kLoop, calls=%fused_computation.12 | loop fusion | flops 8388608 | bytes 8388608 | tf_op jit(solution)/shard_map/concatenate | solution.py:224
  132.0 0.0 copy-start
  132.1 0.7 fusion.57
  132.8 0.3 fusion.32
  133.1 0.8 copy-done
  134.0 0.5 fusion.25
  134.4 0.2 copy.40
  134.6 3.4 %fusion.58 = (f32[2,128]{1,0:T(2,128)S(1)}, f32[1,2,128,8192]{2,3,1,0:T(8,128)S(1)}) fusion(bf16[8192,256]{1,0:T(8,128)(2,1)} %bitcast.119, pred[128,8192]{0,1:T(8,128)(4,1)S(1)} %compare_and_fusion, bf16[132,512]{1,0:T(8,128)(2,1)S(1)} %convolution_convert_fusion.1), kind=kOutput, calls=%fused_computation.85 | convolution fusion | flops 543162112 | bytes 11600896 | tf_op jit(solution)/shard_map/while/body/eval_jaxpr/tgjd,kgd->gjtk/dot_general | solution.py:418
  138.0 0.0 copy-start.1
  138.0 1.7 fusion.4
  139.7 0.5 copy-done.1
  140.2 0.0 copy-start.2
  140.2 1.8 %fusion.29 = bf16[2,128,128]{1,2,0:T(8,128)(2,1)S(1)} fusion(bf16[8192,256]{1,0:T(8,128)(2,1)S(1)} %bitcast.120, f32[1,2,128,8192]{2,3,1,0:T(8,128)S(1)} %get-tuple-element.52, f32[2,128]{1,0:T(2,128)S(1)} %broadcast_maximum_fusion, pred[128,8192]{0,1:T(8,128)(4,1)S(1)} %compare_and_fusion, f32[2,128]{1,0:T(2,128)S(1)} %get-tuple-element.48, ...), kind=kOutput, calls=%fused_computation.33 | convolution fusion | flops 543260672 | bytes 11602944 | tf_op jit(solution)/shard_map/while/body/eval_jaxpr/gjtk,kgd->gjtd/dot_general | solution.py:431
  142.0 0.0 copy-done.2
  142.0 1.8 %convolution_convert_fusion.part_ref = bf16[132,4096]{1,0:T(8,128)(2,1)} fusion(bf16[4096,256]{1,0:T(8,128)(2,1)S(1)} %bitcast.121, bf16[4,256]{0,1:T(8,128)(2,1)S(1)} %copy.40, bf16[128,256]{0,1:T(8,128)(2,1)S(1)} %bitcast.122), kind=kOutput, calls=%fused_computation.9 | convolution fusion | flops 277499904 | bytes 3246080 | tf_op jit(solution)/shard_map/dot_general | solution.py:492
  143.8 31.7 %shard_map.97 = bf16[8,132,512]{2,1,0:T(8,128)(2,1)} custom-call(bf16[132,4096]{1,0:T(8,128)(2,1)} %convolution_convert_fusion.part_ref), custom_call_target="tpu_custom_call" | custom-call | tf_op jit(solution)/shard_map/pallas_call | solution.py:275
  175.5 1.4 reduce_sum.73
  177.0 0.6 slice.63
  177.6 0.7 slice.62
  (11 shorter events, 0.1 us)
Async XLA Ops:
  132.0 1.9 %copy-start = (bf16[8,8,128,256]{3,2,1,0:T(8,128)(2,1)}, bf16[8,8,128,256]{3,2,1,0:T(8,128)(2,1)S(1)}, u32[]{:S(2)}) copy-start(bf16[8,8,128,256]{3,2,1,0:T(8,128)(2,1)S(1)} %pad_maximum_fusion) | copy-start | bytes 12582916
  138.0 2.2 %copy-start.1 = (bf16[8,8,128,256]{3,2,1,0:T(8,128)(2,1)S(1)}, bf16[8,8,128,256]{3,2,1,0:T(8,128)(2,1)}, u32[]{:S(2)}) copy-start(bf16[8,8,128,256]{3,2,1,0:T(8,128)(2,1)} %copy-done) | copy-start | bytes 12582916
  140.2 1.8 %copy-start.2 = (bf16[8,8,64,256]{3,2,1,0:T(8,128)(2,1)S(1)}, bf16[8,8,64,256]{3,2,1,0:T(8,128)(2,1)}, u32[]{:S(2)}) copy-start(bf16[8,8,64,256]{3,2,1,0:T(8,128)(2,1)} %get-tuple-element.31) | copy-start | bytes 6291460

commit v14 on v13

--- a/solution.py
+++ b/solution.py
@@ -3,6 +3,7 @@
 
 import jax
 import jax.numpy as jnp
+import numpy as np
 from jax import lax
 from jax.experimental import pallas as pl
 from jax.experimental.pallas import tpu as pltpu
@@ -405,12 +406,10 @@
     token_request = request_index(token_pos, request_ends)
     query_heads = local_query.reshape(local_rows, kv_heads, query_group_count, head_dim)
 
-    def attend(running, shard_pieces, first_row):
+    def attend(running, shard_pieces, key_pos, key_request):
         peak_run, total_run, mixed_run = running
         key_piece, value_piece = shard_pieces
         row_count = key_piece.shape[0]
-        key_pos = lax.dynamic_slice_in_dim(cache_pos, first_row, row_count, 0)
-        key_request = lax.dynamic_slice_in_dim(cache_request, first_row, row_count, 0)
         allowed = (key_request[None, :] == token_request[:, None]) & (
             key_pos[None, :] <= token_pos[:, None]
         )
@@ -443,34 +442,41 @@
     )
     dec_heads = dec_query.reshape(request_count, kv_heads, query_group_count, head_dim)
     request_ids = jnp.arange(request_count, dtype=jnp.int32)
-    cache_both = gather_ctx(
-        jnp.concatenate([local_keys, local_values], axis=1), layout, 1
-    )
-    cache_keys = cache_both[:, :kv_width]
-    cache_values = cache_both[:, kv_width:]
-    total_rows = cache_keys.shape[0]
-    step_rows = total_rows
-    cache_pos = (
-        block_map[:, None] * block_rows + jnp.arange(block_rows, dtype=jnp.int32)[None, :]
-    ).reshape(total_rows)
-    cache_request = request_index(cache_pos, request_ends)
-
-    def key_step(running, step_index):
-        first_row = step_index * step_rows
-        pieces = (
-            lax.dynamic_slice_in_dim(cache_keys, first_row, step_rows, 0),
-            lax.dynamic_slice_in_dim(cache_values, first_row, step_rows, 0),
-        )
-        return (attend(running, pieces, first_row), None)
-
-    final_state, unused = lax.scan(
-        key_step, start_state, jnp.arange(total_rows // step_rows, dtype=jnp.int32)
-    )
+    kv_sets = gather_ctx(
+        jnp.concatenate([local_keys, local_values], axis=1), layout, 1, parts=True
+    )
+    block_count = z_count * p_count
+    offsets = (0, kv_sets[0].shape[2])
+    key_sets = []
+    for part, offset in zip(kv_sets, offsets):
+        part_rows = part.shape[2]
+        flat = part.reshape(block_count * part_rows, 2 * kv_width)
+        row_ids = (
+            np.arange(block_count, dtype=np.int32)[:, None] * local_rows
+            + offset
+            + np.arange(part_rows, dtype=np.int32)[None, :]
+        ).reshape(-1)
+        part_pos = jnp.take(block_map, row_ids // block_rows) * block_rows + row_ids % block_rows
+        key_sets.append(
+            (flat[:, :kv_width], flat[:, kv_width:], part_pos, request_index(part_pos, request_ends))
+        )
+    final_state = start_state
+    for set_keys, set_values, set_pos, set_request in key_sets:
+        final_state = attend(final_state, (set_keys, set_values), set_pos, set_request)
     peak_run, total_run, mixed_run = final_state
-    owned = (cache_request[None, :] == request_ids[:, None])[:, None, None, :]
-    cache_peak, cache_total, cache_mixed = softmax_parts(
-        dec_heads, cache_keys, cache_values, owned, kv_heads, head_dim, score_scale
-    )
+    dec_parts = []
+    for set_keys, set_values, set_pos, set_request in key_sets:
+        owned = (set_request[None, :] == request_ids[:, None])[:, None, None, :]
+        dec_parts.append(
+            softmax_parts(dec_heads, set_keys, set_values, owned, kv_heads, head_dim, score_scale)
+        )
+    cache_peak = jnp.maximum(dec_parts[0][0], dec_parts[1][0])
+    cache_total = 0.0
+    cache_mixed = 0.0
+    for part_peak, part_total, part_mixed in dec_parts:
+        part_scale = jnp.exp(part_peak - cache_peak)
+        cache_total = cache_total + part_total * part_scale
+        cache_mixed = cache_mixed + part_mixed * part_scale[..., None]
     attended = (
         (mixed_run / total_run[..., None]).transpose(2, 0, 1, 3).reshape(local_rows, query_width)
     )

time: 180 us -> 232 us (1.29)
  local copies, waits for them, and re-layouts: 4.14 us -> 53.7 us
  matrix products: 11.5 us -> 14 us
    gather x0 -> x2, local copies, waits for them, and re-layouts: none -> 49.4 us  [on_device(): jnp.take(block_map, row_ids // block_rows) * block_rows]
    dot_general x1 -> x2, matrix products: 0.74 us -> 3.66 us  [softmax_parts(): jnp.einsum('rgjd,tgd->rgjt', dec_heads, projected_key_rows.reshape(row_co...]
    concatenate x1 -> x0, other arithmetic: 2.72 us -> none  [gather_ctx(): joined = jnp.concatenate([first, second], axis=3 if by_columns else 2)]
    and x1 -> x2, other arithmetic: 2.76 us -> 5.2 us  [attend(): (key_request[None, :] == token_request[:, None]) & (key_pos[None, :] <= t...]
where the time goes in v14:
time: 232 us; the launch traced here: 230 us
  Pallas kernels  149 us (64%)
  local copies, waits for them, and re-layouts  53.7 us (23%)
  matrix products  14 us (6%)
  other arithmetic  12.3 us (5%)
    pallas_call x2, Pallas kernels, gather_ctx(): pl.pallas_call(kernel, out_shape=(jax.ShapeDtypeStruct((z_count, p_count)...  117 us
    gather x2, local copies, waits for them, and re-layouts, on_device(): jnp.take(block_map, row_ids // block_rows) * block_rows  49.4 us
    pallas_call x1, Pallas kernels, scatter_sum_tp(): pl.pallas_call(functools.partial(_scatter_kernel, count), out_shape=jax.S...  31.7 us
    and x2, other arithmetic, attend(): (key_request[None, :] == token_request[:, None]) & (key_pos[None, :] <= t...  5.2 us

profile of v14, /device:TPU:1, one launch (start us, length us, event | category | flops | bytes accessed | tf_op | source)
XLA Modules:
  0.0 229.6 jit_solution(12394236689901691282)
XLA Ops:
  0.6 0.0 copy-start
  0.6 0.8 reduce-window.8
  1.5 0.8 select_reduce_fusion
  2.3 0.1 convert_reduce_fusion.2
  2.4 0.7 broadcast_clamp_fusion.1
  3.1 0.0 copy-done
  3.2 18.7 %gather_fusion.1 = s32[3072]{0:T(1024)S(1)} fusion(s32[128]{0:T(128)S(1)} %copy-done, s32[3072]{0:T(1024)S(1)} %broadcast_clamp_fusion.1), kind=kCustom, calls=%fused_computation.1 | custom fusion | bytes 36864 | tf_op jit(solution)/shard_map/jit(_take)/gather | solution.py:459
  21.8 0.0 copy-done.7
  21.8 0.1 convert_reduce_fusion.1
  22.0 0.0 copy-done.3
  22.0 0.0 copy-start.4
  22.0 0.0 copy-start.2
  22.0 0.0 copy-start.5
  22.0 0.0 copy-start.6
  22.1 0.0 copy-start.11
  22.1 0.0 copy-start.12
  22.1 30.7 %gather_fusion = s32[5120]{0:T(1024)S(1)} fusion(s32[128]{0:T(128)S(1)} %copy-done, s32[5120]{0:T(1024)S(1)} %broadcast_clamp_fusion), kind=kCustom, calls=%fused_computation | custom fusion | bytes 61440 | tf_op jit(solution)/shard_map/jit(_take)/gather | solution.py:459
  52.9 0.1 convert_reduce_fusion
  53.0 0.6 pad_maximum_fusion.first_ref
  53.7 1.9 compare_and_fusion.1
  55.6 3.3 %compare_and_fusion = pred[128,5120]{0,1:T(8,128)(4,1)S(1)} fusion(s32[128]{0:T(128)S(1)} %fusion.81, s32[128]{0:T(128)S(1)} %convert_reduce_fusion.2, s32[5120]{0:T(1024)S(1)} %multiply_add_fusion, s32[5120]{0:T(1024)S(1)} %convert_reduce_fusion), kind=kLoop, calls=%fused_computation.24 | loop fusion | flops 1966080 | bytes 697344 | tf_op jit(solution)/shard_map/and | solution.py:413
  58.9 70.3 %shard_map.131 = (bf16[8,8,64,512]{3,2,1,0:T(8,128)(2,1)}, bf16[8,8,64,256]{3,2,1,0:T(8,128)(2,1)}) custom-call(bf16[64,512]{1,0:T(8,128)(2,1)} %pad_maximum_fusion.first_ref, bf16[64,256]{1,0:T(8,128)(2,1)} %bitcast.154), custom_call_target="tpu_custom_call" | custom-call | tf_op jit(solution)/shard_map/pallas_call | solution.py:211
  129.2 2.9 %convolution_convert_fusion.1 = bf16[132,512]{1,0:T(8,128)(2,1)S(1)} fusion(bf16[4096,512]{1,0:T(8,128)(2,1)} %bitcast.158, bf16[4,4096]{1,0:T(4,128)(2,1)S(1)} %copy-done.12, bf16[128,4096]{1,0:T(8,128)(2,1)S(1)} %copy-done.11), kind=kOutput, calls=%fused_computation.35 | convolution fusion | flops 555878400 | bytes 5410816 | tf_op jit(solution)/shard_map/dot_general | solution.py:382
  132.2 0.1 multiply_reduce_fusion
  132.3 0.1 copy.66
  132.4 0.6 slice.67.second_ref
  133.0 0.6 slice.66.first_ref
  133.6 46.7 %shard_map.132 = (bf16[8,8,80,256]{3,2,1,0:T(8,128)(2,1)}, bf16[8,8,48,256]{3,2,1,0:T(8,128)(2,1)}) custom-call(bf16[80,256]{1,0:T(8,128)(2,1)} %slice.66.first_ref, bf16[48,256]{1,0:T(8,128)(2,1)} %slice.67.second_ref), custom_call_target="tpu_custom_call" | custom-call | tf_op jit(solution)/shard_map/pallas_call | solution.py:211
  180.3 1.7 fusion.89
  181.9 0.2 fusion.63
  182.2 2.0 fusion.90
  184.2 0.2 fusion.54
  184.4 1.4 fusion.42
  185.8 0.4 fusion.44
  186.2 0.2 copy.67
  186.4 0.7 fusion.92
  187.1 1.0 copy-done.9
  188.1 1.1 fusion.91
  189.2 0.8 fusion.19
  190.0 0.6 fusion.16
  190.7 1.0 fusion.4
  191.7 1.2 fusion.48
  192.9 0.4 copy-done.1
  193.3 1.9 convolution_convert_fusion.part_ref
  195.2 31.7 %shard_map.133 = bf16[8,132,512]{2,1,0:T(8,128)(2,1)} custom-call(bf16[132,4096]{1,0:T(8,128)(2,1)} %convolution_convert_fusion.part_ref), custom_call_target="tpu_custom_call" | custom-call | tf_op jit(solution)/shard_map/pallas_call | solution.py:276
  226.9 1.4 reduce_sum.102
  228.3 0.6 slice.77
  228.9 0.7 slice.76
  (29 shorter events, 0.2 us)
Async XLA Ops:
  0.6 2.5 %copy-start = (s32[128]{0:T(128)S(1)}, s32[128]{0:T(128)}, u32[]{:S(2)}) copy-start(s32[128]{0:T(128)} %param.19) | copy-start | bytes 1540
  3.1 18.7 %copy-start.7 = (s32[3072]{0:T(1024)S(1)}, s32[3072]{0:T(1024)}, u32[]{:S(2)}) copy-start(s32[3072]{0:T(1024)} %constant.97.clone) | copy-start | bytes 36868
  3.1 18.8 %copy-start.3 = (s32[5120]{0:T(1024)S(1)}, s32[5120]{0:T(1024)}, u32[]{:S(2)}) copy-start(s32[5120]{0:T(1024)} %constant.114) | copy-start | bytes 61444
  22.0 30.8 %copy-start.4 = (s32[5120]{0:T(1024)S(1)}, s32[5120]{0:T(1024)}, u32[]{:S(2)}) copy-start(s32[5120]{0:T(1024)} %constant.95.clone) | copy-start | bytes 61444
  22.0 31.0 %copy-start.2 = (bf16[64,256]{1,0:T(8,128)(2,1)S(1)}, bf16[64,256]{1,0:T(8,128)(2,1)}, u32[]{:S(2)}) copy-start(bf16[64,256]{1,0:T(8,128)(2,1)} %param.14) | copy-start | bytes 98308
  22.0 31.0 %copy-start.5 = (bf16[64,128]{1,0:T(8,128)(2,1)S(1)}, bf16[64,128]{1,0:T(8,128)(2,1)}, u32[]{:S(2)}) copy-start(bf16[64,128]{1,0:T(8,128)(2,1)} %param.16) | copy-start | bytes 49156
  22.0 31.0 %copy-start.6 = (bf16[64,128]{1,0:T(8,128)(2,1)S(1)}, bf16[64,128]{1,0:T(8,128)(2,1)}, u32[]{:S(2)}) copy-start(bf16[64,128]{1,0:T(8,128)(2,1)} %param.15) | copy-start | bytes 49156
  22.1 107.1 %copy-start.11 = (bf16[128,4096]{1,0:T(8,128)(2,1)S(1)}, bf16[128,4096]{1,0:T(8,128)(2,1)}, u32[]{:S(2)}) copy-start(bf16[128,4096]{1,0:T(8,128)(2,1)} %param.12) | copy-start | bytes 3145732
  22.1 107.1 %copy-start.12 = (bf16[4,4096]{1,0:T(4,128)(2,1)S(1)}, bf16[4,4096]{1,0:T(4,128)(2,1)}, u32[]{:S(2)}) copy-start(bf16[4,4096]{1,0:T(4,128)(2,1)} %param.13) | copy-start | bytes 98308
  180.2 5.6 %copy-start.8 = (bf16[8,8,80,256]{3,2,1,0:T(8,128)(2,1)S(1)}, bf16[8,8,80,256]{3,2,1,0:T(8,128)(2,1)}, u32[]{:S(2)}) copy-start(bf16[8,8,80,256]{3,2,1,0:T(8,128)(2,1)} %get-tuple-element.7) | copy-start | bytes 7864324
  182.2 4.2 %copy-start.10 = (bf16[8,8,48,256]{3,2,1,0:T(8,128)(2,1)S(1)}, bf16[8,8,48,256]{3,2,1,0:T(8,128)(2,1)}, u32[]{:S(2)}) copy-start(bf16[8,8,48,256]{3,2,1,0:T(8,128)(2,1)} %get-tuple-element.8) | copy-start | bytes 4718596
  186.4 1.7 copy-start.9
  191.7 1.6 copy-start.1

commit v15 on v13

--- a/solution.py
+++ b/solution.py
@@ -207,6 +207,28 @@
             sems[8],
         )
 
+    if not by_columns and not parts:
+        split_rows = shapes[0][0]
+
+        def owned_kernel(piece_ref, out_ref, *sems):
+            kernel(
+                piece_ref.at[pl.ds(0, split_rows)],
+                piece_ref.at[pl.ds(split_rows, rows - split_rows)],
+                out_ref.at[:, :, pl.ds(0, split_rows)],
+                out_ref.at[:, :, pl.ds(split_rows, rows - split_rows)],
+                *sems,
+            )
+
+        whole = pl.pallas_call(
+            owned_kernel,
+            out_shape=jax.ShapeDtypeStruct((z_count, p_count, rows, cols), piece.dtype),
+            in_specs=[pl.BlockSpec(memory_space=pl.ANY)],
+            out_specs=pl.BlockSpec(memory_space=pl.ANY),
+            scratch_shapes=dma_pairs + [dma_pairs[2], dma_pairs[3], dma_pairs[0], dma_pairs[1]]
+            + [pltpu.SemaphoreType.DMA((2,))],
+            compiler_params=pltpu.CompilerParams(collective_id=kernel_id, has_side_effects=True),
+        )(piece)
+        return whole.reshape(z_count * p_count * rows, cols)
     first, second = pl.pallas_call(
         kernel,
         out_shape=(

time: 180 us -> 179 us (level)
  matrix products: 11.5 us -> 14.7 us
  other arithmetic: 13.1 us -> 10.4 us
    pallas_call x0 -> x1, Pallas kernels: none -> 46.7 us  [gather_ctx(): pl.pallas_call(owned_kernel, out_shape=jax.ShapeDtypeStruct((z_count, p_c...]
    pallas_call x2 -> x1, Pallas kernels: 117 us -> 70.3 us  [gather_ctx(): pl.pallas_call(kernel, out_shape=(jax.ShapeDtypeStruct((z_count, p_count)...]
    concatenate x1 -> x0, other arithmetic: 2.72 us -> none  [gather_ctx(): joined = jnp.concatenate([first, second], axis=3 if by_columns else 2)]
where the time goes in v15:
time: 179 us; the launch traced here: 177 us
  Pallas kernels  149 us (83%)
  matrix products  14.7 us (8%)
  other arithmetic  10.4 us (6%)
  local copies, waits for them, and re-layouts  2.72 us (2%)
    pallas_call x1, Pallas kernels, gather_ctx(): pl.pallas_call(kernel, out_shape=(jax.ShapeDtypeStruct((z_count, p_count)...  70.3 us
    pallas_call x1, Pallas kernels, gather_ctx(): pl.pallas_call(owned_kernel, out_shape=jax.ShapeDtypeStruct((z_count, p_c...  46.7 us
    pallas_call x1, Pallas kernels, scatter_sum_tp(): pl.pallas_call(functools.partial(_scatter_kernel, count), out_shape=jax.S...  31.7 us

profile of v15, /device:TPU:1, one launch (start us, length us, event | category | flops | bytes accessed | tf_op | source)
XLA Modules:
  0.0 177.2 jit_solution(6739602777358221893)
XLA Ops:
  0.6 0.8 reduce-window.8
  1.5 0.7 broadcast_multiply_fusion
  2.1 0.8 select_reduce_fusion
  3.0 0.1 convert_reduce_fusion.1
  3.1 0.1 iota_add_fusion
  3.2 0.1 add.96
  3.2 0.2 convert_reduce_fusion
  3.4 1.4 pad_maximum_fusion.first_ref
  4.9 2.8 %compare_and_fusion = pred[128,8192]{0,1:T(8,128)(4,1)S(1)} fusion(s32[128]{0:T(128)S(1)} %fusion.51, s32[128]{0:T(128)S(1)} %convert_reduce_fusion.1, s32[8192]{0:T(1024)S(1)} %add.96, s32[8192]{0:T(1024)S(1)} %convert_reduce_fusion), kind=kLoop, calls=%fused_computation.15 | loop fusion | flops 3145728 | bytes 1115136 | tf_op jit(solution)/shard_map/while/body/eval_jaxpr/and | solution.py:436
  7.6 70.3 %shard_map.95 = (bf16[8,8,64,512]{3,2,1,0:T(8,128)(2,1)}, bf16[8,8,64,256]{3,2,1,0:T(8,128)(2,1)}) custom-call(bf16[64,512]{1,0:T(8,128)(2,1)} %pad_maximum_fusion.first_ref, bf16[64,256]{1,0:T(8,128)(2,1)} %bitcast.121), custom_call_target="tpu_custom_call" | custom-call | tf_op jit(solution)/shard_map/pallas_call | solution.py:232
  77.9 3.3 %convolution_convert_fusion.1 = bf16[132,512]{1,0:T(8,128)(2,1)S(1)} fusion(bf16[4096,512]{1,0:T(8,128)(2,1)} %bitcast.124, bf16[4,4096]{1,0:T(4,128)(2,1)} %param.9, bf16[128,4096]{1,0:T(8,128)(2,1)} %param.8), kind=kOutput, calls=%fused_computation.19 | convolution fusion | flops 555878400 | bytes 5410816 | tf_op jit(solution)/shard_map/dot_general | solution.py:403
  81.2 0.1 multiply_reduce_fusion
  81.3 0.1 copy.39
  81.4 0.6 slice_bitcast_fusion.26
  82.1 46.7 %shard_map.96 = bf16[8,8,128,256]{3,2,1,0:T(8,128)(2,1)} custom-call(bf16[128,256]{1,0:T(8,128)(2,1)} %get-tuple-element.29.piece_ref), custom_call_target="tpu_custom_call" | custom-call | tf_op jit(solution)/shard_map/pallas_call | solution.py:222
  128.7 2.3 %fusion.57 = (f32[4,2]{0,1:T(2,128)S(1)}, f32[4,1,2,8192]{3,0,2,1:T(4,128)S(1)}) fusion(bf16[132,512]{1,0:T(8,128)(2,1)S(1)} %convolution_convert_fusion.1, bf16[8192,256]{1,0:T(8,128)(2,1)} %bitcast.115, pred[4,8192]{1,0:T(4,128)(4,1)S(1)} %iota_compare_fusion), kind=kOutput, calls=%fused_computation.83 | convolution fusion | flops 16973816 | bytes 2394144 | tf_op jit(solution)/shard_map/rgjd,tgd->rgjt/dot_general | solution.py:357
  131.1 0.3 fusion.32
  131.4 2.0 %fusion.25 = bf16[4,256]{1,0:T(4,128)(2,1)S(1)} fusion(bf16[8192,256]{1,0:T(8,128)(2,1)} %bitcast.116, f32[4,1,2,8192]{3,0,2,1:T(4,128)S(1)} %get-tuple-element.48, f32[4,2]{0,1:T(2,128)S(1)} %get-tuple-element.47, pred[4,8192]{1,0:T(4,128)(4,1)S(1)} %iota_compare_fusion, f32[4,2]{0,1:T(2,128)S(1)} %get-tuple-element.44, ...), kind=kOutput, calls=%fused_computation.30 | convolution fusion | flops 16978944 | bytes 2396288 | tf_op jit(solution)/shard_map/rgjt,tgd->rgjd/dot_general | solution.py:369
  133.4 0.2 copy.40
  133.6 3.4 %fusion.58 = (f32[2,128]{1,0:T(2,128)S(1)}, f32[1,2,128,8192]{2,3,1,0:T(8,128)S(1)}) fusion(bf16[16,2,8,128]{3,2,1,0:T(8,128)(2,1)S(1)} %get-tuple-element.28, bf16[8192,256]{1,0:T(8,128)(2,1)} %bitcast.117, pred[128,8192]{0,1:T(8,128)(4,1)S(1)} %compare_and_fusion), kind=kOutput, calls=%fused_computation.84 | convolution fusion | flops 543162112 | bytes 11600896 | tf_op jit(solution)/shard_map/while/body/eval_jaxpr/tgjd,kgd->gjtk/dot_general | solution.py:440
  137.0 0.0 copy-start
  137.0 1.7 fusion.4
  138.7 0.5 copy-done
  139.2 0.0 copy-start.1
  139.2 1.8 %fusion.29 = bf16[2,128,128]{1,2,0:T(8,128)(2,1)S(1)} fusion(bf16[8192,256]{1,0:T(8,128)(2,1)S(1)} %bitcast.118, f32[1,2,128,8192]{2,3,1,0:T(8,128)S(1)} %get-tuple-element.50, f32[2,128]{1,0:T(2,128)S(1)} %broadcast_maximum_fusion, pred[128,8192]{0,1:T(8,128)(4,1)S(1)} %compare_and_fusion, f32[2,128]{1,0:T(2,128)S(1)} %get-tuple-element.46, ...), kind=kOutput, calls=%fused_computation.32 | convolution fusion | flops 543260672 | bytes 11602944 | tf_op jit(solution)/shard_map/while/body/eval_jaxpr/gjtk,kgd->gjtd/dot_general | solution.py:453
  141.0 0.0 copy-done.1
  141.0 1.8 %convolution_convert_fusion.part_ref = bf16[132,4096]{1,0:T(8,128)(2,1)} fusion(bf16[4096,256]{1,0:T(8,128)(2,1)S(1)} %bitcast.119, bf16[4,256]{0,1:T(8,128)(2,1)S(1)} %copy.40, bf16[128,256]{0,1:T(8,128)(2,1)S(1)} %bitcast.120), kind=kOutput, calls=%fused_computation.9 | convolution fusion | flops 277499904 | bytes 3246080 | tf_op jit(solution)/shard_map/dot_general | solution.py:514
  142.8 31.7 %shard_map.97 = bf16[8,132,512]{2,1,0:T(8,128)(2,1)} custom-call(bf16[132,4096]{1,0:T(8,128)(2,1)} %convolution_convert_fusion.part_ref), custom_call_target="tpu_custom_call" | custom-call | tf_op jit(solution)/shard_map/pallas_call | solution.py:297
  174.5 1.4 reduce_sum.73
  175.9 0.6 slice.51
  176.5 0.7 slice.50
  (11 shorter events, 0.1 us)
Async XLA Ops:
  137.0 2.2 %copy-start = (bf16[8,8,128,256]{3,2,1,0:T(8,128)(2,1)S(1)}, bf16[8,8,128,256]{3,2,1,0:T(8,128)(2,1)}, u32[]{:S(2)}) copy-start(bf16[8,8,128,256]{3,2,1,0:T(8,128)(2,1)} %shard_map.96) | copy-start | bytes 12582916
  139.2 1.8 %copy-start.1 = (bf16[8,8,64,256]{3,2,1,0:T(8,128)(2,1)S(1)}, bf16[8,8,64,256]{3,2,1,0:T(8,128)(2,1)}, u32[]{:S(2)}) copy-start(bf16[8,8,64,256]{3,2,1,0:T(8,128)(2,1)} %get-tuple-element.27) | copy-start | bytes 6291460

commit v16 on v15

--- a/solution.py
+++ b/solution.py
@@ -447,7 +447,7 @@
         )
         scores = jnp.where(allowed, scores, floor_value)
         peak_new = jnp.maximum(peak_run, jnp.max(scores, axis=3))
-        weights = jnp.where(allowed, jnp.exp(scores - peak_new[..., None]), 0.0)
+        weights = jnp.exp(scores - peak_new[..., None])
         rescale = jnp.exp(peak_run - peak_new)
         total_new = total_run * rescale + jnp.sum(weights, axis=3)
         mixed_new = mixed_run * rescale[..., None] + jnp.einsum(

time: 179 us -> 179 us (level)
  no operation moved by 1% of the time
where the time goes in v16:
time: 179 us; the launch traced here: 177 us
  Pallas kernels  149 us (83%)
  matrix products  14.4 us (8%)
  other arithmetic  9.84 us (5%)
  local copies, waits for them, and re-layouts  3.35 us (2%)
    pallas_call x1, Pallas kernels, gather_ctx(): pl.pallas_call(kernel, out_shape=(jax.ShapeDtypeStruct((z_count, p_count)...  70.3 us
    pallas_call x1, Pallas kernels, gather_ctx(): pl.pallas_call(owned_kernel, out_shape=jax.ShapeDtypeStruct((z_count, p_c...  46.7 us
    pallas_call x1, Pallas kernels, scatter_sum_tp(): pl.pallas_call(functools.partial(_scatter_kernel, count), out_shape=jax.S...  31.6 us

profile of v16, /device:TPU:1, one launch (start us, length us, event | category | flops | bytes accessed | tf_op | source)
XLA Modules:
  0.0 176.9 jit_solution(10518055198894664781)
XLA Ops:
  0.6 0.8 reduce-window.8
  1.5 0.7 broadcast_multiply_fusion
  2.1 0.8 select_reduce_fusion
  3.0 0.1 convert_reduce_fusion.1
  3.1 0.1 iota_add_fusion
  3.2 0.1 add.96
  3.2 0.2 convert_reduce_fusion
  3.4 1.4 pad_maximum_fusion.first_ref
  4.9 2.8 %compare_and_fusion = pred[128,8192]{0,1:T(8,128)(4,1)S(1)} fusion(s32[128]{0:T(128)S(1)} %fusion.49, s32[128]{0:T(128)S(1)} %convert_reduce_fusion.1, s32[8192]{0:T(1024)S(1)} %add.96, s32[8192]{0:T(1024)S(1)} %convert_reduce_fusion), kind=kLoop, calls=%fused_computation.13 | loop fusion | flops 3145728 | bytes 1115136 | tf_op jit(solution)/shard_map/while/body/eval_jaxpr/and | solution.py:436
  7.6 70.3 %shard_map.95 = (bf16[8,8,64,512]{3,2,1,0:T(8,128)(2,1)}, bf16[8,8,64,256]{3,2,1,0:T(8,128)(2,1)}) custom-call(bf16[64,512]{1,0:T(8,128)(2,1)} %pad_maximum_fusion.first_ref, bf16[64,256]{1,0:T(8,128)(2,1)} %bitcast.121), custom_call_target="tpu_custom_call" | custom-call | tf_op jit(solution)/shard_map/pallas_call | solution.py:232
  77.9 3.3 %convolution_convert_fusion.1 = bf16[132,512]{1,0:T(8,128)(2,1)S(1)} fusion(bf16[4096,512]{1,0:T(8,128)(2,1)} %bitcast.124, bf16[4,4096]{1,0:T(4,128)(2,1)} %param.9, bf16[128,4096]{1,0:T(8,128)(2,1)} %param.8), kind=kOutput, calls=%fused_computation.17 | convolution fusion | flops 555878400 | bytes 5410816 | tf_op jit(solution)/shard_map/dot_general | solution.py:403
  81.2 0.1 multiply_reduce_fusion
  81.3 0.1 copy.39
  81.4 0.6 slice_bitcast_fusion.26
  82.1 46.7 %shard_map.96 = bf16[8,8,128,256]{3,2,1,0:T(8,128)(2,1)} custom-call(bf16[128,256]{1,0:T(8,128)(2,1)} %get-tuple-element.29.piece_ref), custom_call_target="tpu_custom_call" | custom-call | tf_op jit(solution)/shard_map/pallas_call | solution.py:222
  128.7 2.3 %fusion.54 = (f32[4,2]{0,1:T(2,128)S(1)}, f32[4,1,2,8192]{3,0,2,1:T(4,128)S(1)}) fusion(bf16[132,512]{1,0:T(8,128)(2,1)S(1)} %convolution_convert_fusion.1, bf16[8192,256]{1,0:T(8,128)(2,1)} %bitcast.115, pred[4,8192]{1,0:T(4,128)(4,1)S(1)} %iota_compare_fusion), kind=kOutput, calls=%fused_computation.80 | convolution fusion | flops 16973816 | bytes 2394144 | tf_op jit(solution)/shard_map/rgjd,tgd->rgjt/dot_general | solution.py:357
  131.1 0.3 fusion.30
  131.4 2.0 %fusion.23 = bf16[4,256]{1,0:T(4,128)(2,1)S(1)} fusion(bf16[8192,256]{1,0:T(8,128)(2,1)} %bitcast.116, f32[4,1,2,8192]{3,0,2,1:T(4,128)S(1)} %get-tuple-element.48, f32[4,2]{0,1:T(2,128)S(1)} %get-tuple-element.47, pred[4,8192]{1,0:T(4,128)(4,1)S(1)} %iota_compare_fusion, f32[4,2]{0,1:T(2,128)S(1)} %get-tuple-element.44, ...), kind=kOutput, calls=%fused_computation.28 | convolution fusion | flops 16978944 | bytes 2396288 | tf_op jit(solution)/shard_map/rgjt,tgd->rgjd/dot_general | solution.py:369
  133.5 0.2 copy.40
  133.6 3.4 %fusion.55 = (f32[2,128]{1,0:T(2,128)S(1)}, f32[1,2,128,8192]{2,3,1,0:T(8,128)S(1)}) fusion(bf16[16,2,8,128]{3,2,1,0:T(8,128)(2,1)S(1)} %get-tuple-element.28, bf16[8192,256]{1,0:T(8,128)(2,1)} %bitcast.117, pred[128,8192]{0,1:T(8,128)(4,1)S(1)} %compare_and_fusion), kind=kOutput, calls=%fused_computation.81 | convolution fusion | flops 543162112 | bytes 11600896 | tf_op jit(solution)/shard_map/while/body/eval_jaxpr/tgjd,kgd->gjtk/dot_general | solution.py:440
  137.0 0.0 copy-start
  137.0 1.1 fusion.4
  138.1 1.1 copy-done
  139.2 0.0 copy-start.1
  139.2 1.5 fusion.27
  140.7 0.1 copy-done.1
  140.8 1.8 %convolution_convert_fusion.part_ref = bf16[132,4096]{1,0:T(8,128)(2,1)} fusion(bf16[4096,256]{1,0:T(8,128)(2,1)S(1)} %bitcast.119, bf16[4,256]{0,1:T(8,128)(2,1)S(1)} %copy.40, bf16[128,256]{0,1:T(8,128)(2,1)S(1)} %bitcast.120), kind=kOutput, calls=%fused_computation.9 | convolution fusion | flops 277499904 | bytes 3246080 | tf_op jit(solution)/shard_map/dot_general | solution.py:514
  142.6 31.6 %shard_map.97 = bf16[8,132,512]{2,1,0:T(8,128)(2,1)} custom-call(bf16[132,4096]{1,0:T(8,128)(2,1)} %convolution_convert_fusion.part_ref), custom_call_target="tpu_custom_call" | custom-call | tf_op jit(solution)/shard_map/pallas_call | solution.py:297
  174.2 1.4 reduce_sum.73
  175.6 0.6 slice.51
  176.2 0.7 slice.50
  (11 shorter events, 0.1 us)
Async XLA Ops:
  137.0 2.2 %copy-start = (bf16[8,8,128,256]{3,2,1,0:T(8,128)(2,1)S(1)}, bf16[8,8,128,256]{3,2,1,0:T(8,128)(2,1)}, u32[]{:S(2)}) copy-start(bf16[8,8,128,256]{3,2,1,0:T(8,128)(2,1)} %shard_map.96) | copy-start | bytes 12582916
  139.2 1.6 copy-start.1

commit v17 on v16

--- a/solution.py
+++ b/solution.py
@@ -292,7 +292,7 @@
     own.wait()
 
 
-def scatter_sum_tp(part, count, kernel_id):
+def scatter_sum_tp(part, count, kernel_id, split=None):
     rows, cols = part.shape
     pieces = pl.pallas_call(
         functools.partial(_scatter_kernel, count),
@@ -306,6 +306,11 @@
         ],
         compiler_params=pltpu.CompilerParams(collective_id=kernel_id, has_side_effects=True),
     )(part)
+    if split is not None:
+        return (
+            jnp.sum(pieces[:, :split].astype(jnp.float32), axis=0).astype(part.dtype),
+            jnp.sum(pieces[:, split:].astype(jnp.float32), axis=0).astype(part.dtype),
+        )
     return jnp.sum(pieces.astype(jnp.float32), axis=0)
 
 
@@ -517,9 +522,7 @@
         (((1,), (1,)), ((), ())),
         preferred_element_type=jnp.float32,
     )
-    summed_rows = scatter_sum_tp(projected.astype(jnp.bfloat16), tp_count, 2)
-    summed_rows = summed_rows.astype(jnp.bfloat16)
-    return (summed_rows[:local_rows], summed_rows[local_rows:])
+    return scatter_sum_tp(projected.astype(jnp.bfloat16), tp_count, 2, split=local_rows)
 
 
 def solution(mesh):

time: 179 us -> 180 us (level)
  other arithmetic: 9.84 us -> 11.9 us
    reduce_sum x1 -> x2, other arithmetic: 1.42 us -> 3.52 us  [the longest x1 2.06 us: scatter_sum_tp(): jnp.sum(pieces[:, :split].astype(jnp.float32), axis=0).astype(part.dtype)]
where the time goes in v17:
time: 180 us; the launch traced here: 178 us
  Pallas kernels  149 us (83%)
  matrix products  14.4 us (8%)
  other arithmetic  11.9 us (7%)
  local copies, waits for them, and re-layouts  2.09 us (1%)
    pallas_call x1, Pallas kernels, gather_ctx(): pl.pallas_call(kernel, out_shape=(jax.ShapeDtypeStruct((z_count, p_count)...  70.3 us
    pallas_call x1, Pallas kernels, gather_ctx(): pl.pallas_call(owned_kernel, out_shape=jax.ShapeDtypeStruct((z_count, p_c...  46.7 us
    pallas_call x1, Pallas kernels, scatter_sum_tp(): pl.pallas_call(functools.partial(_scatter_kernel, count), out_shape=jax.S...  31.6 us

profile of v17, /device:TPU:1, one launch (start us, length us, event | category | flops | bytes accessed | tf_op | source)
XLA Modules:
  0.0 177.7 jit_solution(9952582638715897890)
XLA Ops:
  0.6 0.8 reduce-window.8
  1.5 0.7 broadcast_multiply_fusion
  2.1 0.8 select_reduce_fusion
  3.0 0.1 convert_reduce_fusion.1
  3.1 0.1 iota_add_fusion
  3.2 0.1 add.96
  3.2 0.2 convert_reduce_fusion
  3.4 1.4 pad_maximum_fusion.first_ref
  4.9 2.8 %compare_and_fusion = pred[128,8192]{0,1:T(8,128)(4,1)S(1)} fusion(s32[128]{0:T(128)S(1)} %fusion.49, s32[128]{0:T(128)S(1)} %convert_reduce_fusion.1, s32[8192]{0:T(1024)S(1)} %add.96, s32[8192]{0:T(1024)S(1)} %convert_reduce_fusion), kind=kLoop, calls=%fused_computation.13 | loop fusion | flops 3145728 | bytes 1115136 | tf_op jit(solution)/shard_map/while/body/eval_jaxpr/and | solution.py:441
  7.6 70.3 %shard_map.95 = (bf16[8,8,64,512]{3,2,1,0:T(8,128)(2,1)}, bf16[8,8,64,256]{3,2,1,0:T(8,128)(2,1)}) custom-call(bf16[64,512]{1,0:T(8,128)(2,1)} %pad_maximum_fusion.first_ref, bf16[64,256]{1,0:T(8,128)(2,1)} %bitcast.121), custom_call_target="tpu_custom_call" | custom-call | tf_op jit(solution)/shard_map/pallas_call | solution.py:232
  77.9 3.3 %convolution_convert_fusion.1 = bf16[132,512]{1,0:T(8,128)(2,1)S(1)} fusion(bf16[4096,512]{1,0:T(8,128)(2,1)} %bitcast.124, bf16[4,4096]{1,0:T(4,128)(2,1)} %param.9, bf16[128,4096]{1,0:T(8,128)(2,1)} %param.8), kind=kOutput, calls=%fused_computation.17 | convolution fusion | flops 555878400 | bytes 5410816 | tf_op jit(solution)/shard_map/dot_general | solution.py:408
  81.2 0.1 multiply_reduce_fusion
  81.3 0.1 copy.39
  81.4 0.6 slice_bitcast_fusion.26
  82.1 46.7 %shard_map.96 = bf16[8,8,128,256]{3,2,1,0:T(8,128)(2,1)} custom-call(bf16[128,256]{1,0:T(8,128)(2,1)} %get-tuple-element.29.piece_ref), custom_call_target="tpu_custom_call" | custom-call | tf_op jit(solution)/shard_map/pallas_call | solution.py:222
  128.7 2.3 %fusion.54 = (f32[4,2]{0,1:T(2,128)S(1)}, f32[4,1,2,8192]{3,0,2,1:T(4,128)S(1)}) fusion(bf16[132,512]{1,0:T(8,128)(2,1)S(1)} %convolution_convert_fusion.1, bf16[8192,256]{1,0:T(8,128)(2,1)} %bitcast.115, pred[4,8192]{1,0:T(4,128)(4,1)S(1)} %iota_compare_fusion), kind=kOutput, calls=%fused_computation.82 | convolution fusion | flops 16973816 | bytes 2394144 | tf_op jit(solution)/shard_map/rgjd,tgd->rgjt/dot_general | solution.py:362
  131.1 0.3 fusion.30
  131.4 2.0 %fusion.23 = bf16[4,256]{1,0:T(4,128)(2,1)S(1)} fusion(bf16[8192,256]{1,0:T(8,128)(2,1)} %bitcast.116, f32[4,1,2,8192]{3,0,2,1:T(4,128)S(1)} %get-tuple-element.48, f32[4,2]{0,1:T(2,128)S(1)} %get-tuple-element.47, pred[4,8192]{1,0:T(4,128)(4,1)S(1)} %iota_compare_fusion, f32[4,2]{0,1:T(2,128)S(1)} %get-tuple-element.44, ...), kind=kOutput, calls=%fused_computation.28 | convolution fusion | flops 16978944 | bytes 2396288 | tf_op jit(solution)/shard_map/rgjt,tgd->rgjd/dot_general | solution.py:374
  133.5 0.2 copy.40
  133.6 3.4 %fusion.55 = (f32[2,128]{1,0:T(2,128)S(1)}, f32[1,2,128,8192]{2,3,1,0:T(8,128)S(1)}) fusion(bf16[16,2,8,128]{3,2,1,0:T(8,128)(2,1)S(1)} %get-tuple-element.28, bf16[8192,256]{1,0:T(8,128)(2,1)} %bitcast.117, pred[128,8192]{0,1:T(8,128)(4,1)S(1)} %compare_and_fusion), kind=kOutput, calls=%fused_computation.83 | convolution fusion | flops 543162112 | bytes 11600896 | tf_op jit(solution)/shard_map/while/body/eval_jaxpr/tgjd,kgd->gjtk/dot_general | solution.py:445
  137.0 0.0 copy-start
  137.0 1.1 fusion.4
  138.1 1.1 copy-done
  139.2 0.0 copy-start.1
  139.2 1.5 fusion.27
  140.7 0.1 copy-done.1
  140.8 1.8 %convolution_convert_fusion.part_ref = bf16[132,4096]{1,0:T(8,128)(2,1)} fusion(bf16[4096,256]{1,0:T(8,128)(2,1)S(1)} %bitcast.119, bf16[4,256]{0,1:T(8,128)(2,1)S(1)} %copy.40, bf16[128,256]{0,1:T(8,128)(2,1)S(1)} %bitcast.120), kind=kOutput, calls=%fused_computation.9 | convolution fusion | flops 277499904 | bytes 3246080 | tf_op jit(solution)/shard_map/dot_general | solution.py:519
  142.6 31.6 %shard_map.97 = bf16[8,132,512]{2,1,0:T(8,128)(2,1)} custom-call(bf16[132,4096]{1,0:T(8,128)(2,1)} %convolution_convert_fusion.part_ref), custom_call_target="tpu_custom_call" | custom-call | tf_op jit(solution)/shard_map/pallas_call | solution.py:297
  174.2 1.5 slice_reduce_fusion.1
  175.7 2.1 %slice_reduce_fusion = bf16[128,512]{1,0:T(8,128)(2,1)} fusion(bf16[8,132,512]{2,1,0:T(8,128)(2,1)} %shard_map.97), kind=kLoop, calls=%fused_computation.31 | loop fusion | flops 458752 | bytes 1179648 | tf_op jit(solution)/shard_map/reduce_sum | solution.py:311
  (11 shorter events, 0.1 us)
Async XLA Ops:
  137.0 2.2 %copy-start = (bf16[8,8,128,256]{3,2,1,0:T(8,128)(2,1)S(1)}, bf16[8,8,128,256]{3,2,1,0:T(8,128)(2,1)}, u32[]{:S(2)}) copy-start(bf16[8,8,128,256]{3,2,1,0:T(8,128)(2,1)} %shard_map.96) | copy-start | bytes 12582916
  139.2 1.6 copy-start.1

commit v18 on v15

--- a/solution.py
+++ b/solution.py
@@ -287,7 +287,18 @@
         remote(peer, peer).wait_recv()
         return carry
 
-    lax.fori_loop(1, count, send, 0)
+    if count % 2 == 0 and count >= 4:
+        outer = count // 2
+        order = sorted(range(outer), key=lambda hop: -min(hop, outer - hop))
+        for hop in order:
+            for core in range(2):
+                peer = lax.rem(me // 2 + hop, outer) * 2 + core
+
+                @pl.when(peer != me)
+                def _():
+                    remote(peer, me).start()
+    else:
+        lax.fori_loop(1, count, send, 0)
     lax.fori_loop(1, count, finish, 0)
     own.wait()
 

time: 179 us -> 180 us (level)
    pallas_call x1, Pallas kernels: 31.7 us -> 33.6 us  [scatter_sum_tp(): pl.pallas_call(functools.partial(_scatter_kernel, count), out_shape=jax.S...]
where the time goes in v18:
time: 180 us; the launch traced here: 179 us
  Pallas kernels  150 us (83%)
  matrix products  14.7 us (8%)
  other arithmetic  10.4 us (6%)
  local copies, waits for them, and re-layouts  2.72 us (2%)
    pallas_call x1, Pallas kernels, gather_ctx(): pl.pallas_call(kernel, out_shape=(jax.ShapeDtypeStruct((z_count, p_count)...  70.3 us
    pallas_call x1, Pallas kernels, gather_ctx(): pl.pallas_call(owned_kernel, out_shape=jax.ShapeDtypeStruct((z_count, p_c...  46.7 us
    pallas_call x1, Pallas kernels, scatter_sum_tp(): pl.pallas_call(functools.partial(_scatter_kernel, count), out_shape=jax.S...  33.6 us

profile of v18, /device:TPU:1, one launch (start us, length us, event | category | flops | bytes accessed | tf_op | source)
XLA Modules:
  0.0 179.1 jit_solution(11640220921313047001)
XLA Ops:
  0.6 0.8 reduce-window.8
  1.5 0.7 broadcast_multiply_fusion
  2.1 0.8 select_reduce_fusion
  3.0 0.1 convert_reduce_fusion.1
  3.1 0.1 iota_add_fusion
  3.2 0.1 add.96
  3.2 0.2 convert_reduce_fusion
  3.4 1.4 pad_maximum_fusion.first_ref
  4.9 2.8 %compare_and_fusion = pred[128,8192]{0,1:T(8,128)(4,1)S(1)} fusion(s32[128]{0:T(128)S(1)} %fusion.51, s32[128]{0:T(128)S(1)} %convert_reduce_fusion.1, s32[8192]{0:T(1024)S(1)} %add.96, s32[8192]{0:T(1024)S(1)} %convert_reduce_fusion), kind=kLoop, calls=%fused_computation.15 | loop fusion | flops 3145728 | bytes 1115136 | tf_op jit(solution)/shard_map/while/body/eval_jaxpr/and | solution.py:447
  7.6 70.3 %shard_map.95 = (bf16[8,8,64,512]{3,2,1,0:T(8,128)(2,1)}, bf16[8,8,64,256]{3,2,1,0:T(8,128)(2,1)}) custom-call(bf16[64,512]{1,0:T(8,128)(2,1)} %pad_maximum_fusion.first_ref, bf16[64,256]{1,0:T(8,128)(2,1)} %bitcast.121), custom_call_target="tpu_custom_call" | custom-call | tf_op jit(solution)/shard_map/pallas_call | solution.py:232
  77.9 3.3 %convolution_convert_fusion.1 = bf16[132,512]{1,0:T(8,128)(2,1)S(1)} fusion(bf16[4096,512]{1,0:T(8,128)(2,1)} %bitcast.124, bf16[4,4096]{1,0:T(4,128)(2,1)} %param.9, bf16[128,4096]{1,0:T(8,128)(2,1)} %param.8), kind=kOutput, calls=%fused_computation.19 | convolution fusion | flops 555878400 | bytes 5410816 | tf_op jit(solution)/shard_map/dot_general | solution.py:414
  81.2 0.1 multiply_reduce_fusion
  81.3 0.1 copy.39
  81.4 0.6 slice_bitcast_fusion.26
  82.1 46.7 %shard_map.96 = bf16[8,8,128,256]{3,2,1,0:T(8,128)(2,1)} custom-call(bf16[128,256]{1,0:T(8,128)(2,1)} %get-tuple-element.29.piece_ref), custom_call_target="tpu_custom_call" | custom-call | tf_op jit(solution)/shard_map/pallas_call | solution.py:222
  128.7 2.3 %fusion.57 = (f32[4,2]{0,1:T(2,128)S(1)}, f32[4,1,2,8192]{3,0,2,1:T(4,128)S(1)}) fusion(bf16[132,512]{1,0:T(8,128)(2,1)S(1)} %convolution_convert_fusion.1, bf16[8192,256]{1,0:T(8,128)(2,1)} %bitcast.115, pred[4,8192]{1,0:T(4,128)(4,1)S(1)} %iota_compare_fusion), kind=kOutput, calls=%fused_computation.83 | convolution fusion | flops 16973816 | bytes 2394144 | tf_op jit(solution)/shard_map/rgjd,tgd->rgjt/dot_general | solution.py:368
  131.1 0.3 fusion.32
  131.4 2.0 %fusion.25 = bf16[4,256]{1,0:T(4,128)(2,1)S(1)} fusion(bf16[8192,256]{1,0:T(8,128)(2,1)} %bitcast.116, f32[4,1,2,8192]{3,0,2,1:T(4,128)S(1)} %get-tuple-element.48, f32[4,2]{0,1:T(2,128)S(1)} %get-tuple-element.47, pred[4,8192]{1,0:T(4,128)(4,1)S(1)} %iota_compare_fusion, f32[4,2]{0,1:T(2,128)S(1)} %get-tuple-element.44, ...), kind=kOutput, calls=%fused_computation.30 | convolution fusion | flops 16978944 | bytes 2396288 | tf_op jit(solution)/shard_map/rgjt,tgd->rgjd/dot_general | solution.py:380
  133.4 0.2 copy.40
  133.6 3.4 %fusion.58 = (f32[2,128]{1,0:T(2,128)S(1)}, f32[1,2,128,8192]{2,3,1,0:T(8,128)S(1)}) fusion(bf16[16,2,8,128]{3,2,1,0:T(8,128)(2,1)S(1)} %get-tuple-element.28, bf16[8192,256]{1,0:T(8,128)(2,1)} %bitcast.117, pred[128,8192]{0,1:T(8,128)(4,1)S(1)} %compare_and_fusion), kind=kOutput, calls=%fused_computation.84 | convolution fusion | flops 543162112 | bytes 11600896 | tf_op jit(solution)/shard_map/while/body/eval_jaxpr/tgjd,kgd->gjtk/dot_general | solution.py:451
  137.0 0.0 copy-start
  137.0 1.7 fusion.4
  138.7 0.5 copy-done
  139.2 0.0 copy-start.1
  139.2 1.8 fusion.29
  141.0 0.0 copy-done.1
  141.0 1.8 %convolution_convert_fusion.part_ref = bf16[132,4096]{1,0:T(8,128)(2,1)} fusion(bf16[4096,256]{1,0:T(8,128)(2,1)S(1)} %bitcast.119, bf16[4,256]{0,1:T(8,128)(2,1)S(1)} %copy.40, bf16[128,256]{0,1:T(8,128)(2,1)S(1)} %bitcast.120), kind=kOutput, calls=%fused_computation.9 | convolution fusion | flops 277499904 | bytes 3246080 | tf_op jit(solution)/shard_map/dot_general | solution.py:525
  142.8 33.6 %shard_map.97 = bf16[8,132,512]{2,1,0:T(8,128)(2,1)} custom-call(bf16[132,4096]{1,0:T(8,128)(2,1)} %convolution_convert_fusion.part_ref), custom_call_target="tpu_custom_call" | custom-call | tf_op jit(solution)/shard_map/pallas_call | solution.py:308
  176.4 1.4 reduce_sum.73
  177.8 0.6 slice.51
  178.4 0.7 slice.50
  (11 shorter events, 0.1 us)
Async XLA Ops:
  137.0 2.2 %copy-start = (bf16[8,8,128,256]{3,2,1,0:T(8,128)(2,1)S(1)}, bf16[8,8,128,256]{3,2,1,0:T(8,128)(2,1)}, u32[]{:S(2)}) copy-start(bf16[8,8,128,256]{3,2,1,0:T(8,128)(2,1)} %shard_map.96) | copy-start | bytes 12582916
  139.2 1.8 %copy-start.1 = (bf16[8,8,64,256]{3,2,1,0:T(8,128)(2,1)S(1)}, bf16[8,8,64,256]{3,2,1,0:T(8,128)(2,1)}, u32[]{:S(2)}) copy-start(bf16[8,8,64,256]{3,2,1,0:T(8,128)(2,1)} %get-tuple-element.27) | copy-start | bytes 6291460

commit v19 on v18

--- a/solution.py
+++ b/solution.py
@@ -121,7 +121,14 @@
         return carry
 
     rounds = max(z_count, p_count)
-    lax.fori_loop(1, rounds, start_one, 0)
+    for hop in sorted(range(1, z_count), key=lambda hop: -min(hop, z_count - hop)):
+        first_one(z_peer(hop), z_me).start()
+
+    def start_second(step, carry):
+        second_one(p_peer(step), p_me).start()
+        return carry
+
+    lax.fori_loop(1, p_count, start_second, 0)
 
     def forward_first(slot):
         def body(step, carry):

time: 180 us -> 181 us (level)
    pallas_call x1, Pallas kernels: 33.6 us -> 29.7 us  [scatter_sum_tp(): pl.pallas_call(functools.partial(_scatter_kernel, count), out_shape=jax.S...]
    pallas_call x1, Pallas kernels: 46.7 us -> 49.1 us  [gather_ctx(): pl.pallas_call(owned_kernel, out_shape=jax.ShapeDtypeStruct((z_count, p_c...]
where the time goes in v19:
time: 181 us; the launch traced here: 179 us
  Pallas kernels  151 us (83%)
  matrix products  14.7 us (8%)
  other arithmetic  10.4 us (6%)
  local copies, waits for them, and re-layouts  2.72 us (2%)
    pallas_call x1, Pallas kernels, gather_ctx(): pl.pallas_call(kernel, out_shape=(jax.ShapeDtypeStruct((z_count, p_count)...  71.7 us
    pallas_call x1, Pallas kernels, gather_ctx(): pl.pallas_call(owned_kernel, out_shape=jax.ShapeDtypeStruct((z_count, p_c...  49.1 us
    pallas_call x1, Pallas kernels, scatter_sum_tp(): pl.pallas_call(functools.partial(_scatter_kernel, count), out_shape=jax.S...  29.7 us

profile of v19, /device:TPU:1, one launch (start us, length us, event | category | flops | bytes accessed | tf_op | source)
XLA Modules:
  0.0 179.2 jit_solution(17706905392122389719)
XLA Ops:
  0.6 0.8 reduce-window.8
  1.5 0.7 broadcast_multiply_fusion
  2.1 0.8 select_reduce_fusion
  3.0 0.1 convert_reduce_fusion.1
  3.1 0.1 iota_add_fusion
  3.2 0.1 add.96
  3.2 0.2 convert_reduce_fusion
  3.4 1.4 pad_maximum_fusion.first_ref
  4.9 2.8 %compare_and_fusion = pred[128,8192]{0,1:T(8,128)(4,1)S(1)} fusion(s32[128]{0:T(128)S(1)} %fusion.51, s32[128]{0:T(128)S(1)} %convert_reduce_fusion.1, s32[8192]{0:T(1024)S(1)} %add.96, s32[8192]{0:T(1024)S(1)} %convert_reduce_fusion), kind=kLoop, calls=%fused_computation.15 | loop fusion | flops 3145728 | bytes 1115136 | tf_op jit(solution)/shard_map/while/body/eval_jaxpr/and | solution.py:454
  7.6 71.7 %shard_map.95 = (bf16[8,8,64,512]{3,2,1,0:T(8,128)(2,1)}, bf16[8,8,64,256]{3,2,1,0:T(8,128)(2,1)}) custom-call(bf16[64,512]{1,0:T(8,128)(2,1)} %pad_maximum_fusion.first_ref, bf16[64,256]{1,0:T(8,128)(2,1)} %bitcast.121), custom_call_target="tpu_custom_call" | custom-call | tf_op jit(solution)/shard_map/pallas_call | solution.py:239
  79.4 3.3 %convolution_convert_fusion.1 = bf16[132,512]{1,0:T(8,128)(2,1)S(1)} fusion(bf16[4096,512]{1,0:T(8,128)(2,1)} %bitcast.124, bf16[4,4096]{1,0:T(4,128)(2,1)} %param.9, bf16[128,4096]{1,0:T(8,128)(2,1)} %param.8), kind=kOutput, calls=%fused_computation.19 | convolution fusion | flops 555878400 | bytes 5410816 | tf_op jit(solution)/shard_map/dot_general | solution.py:421
  82.7 0.1 multiply_reduce_fusion
  82.8 0.1 copy.39
  82.9 0.6 slice_bitcast_fusion.26
  83.5 49.1 %shard_map.96 = bf16[8,8,128,256]{3,2,1,0:T(8,128)(2,1)} custom-call(bf16[128,256]{1,0:T(8,128)(2,1)} %get-tuple-element.29.piece_ref), custom_call_target="tpu_custom_call" | custom-call | tf_op jit(solution)/shard_map/pallas_call | solution.py:229
  132.7 2.3 %fusion.57 = (f32[4,2]{0,1:T(2,128)S(1)}, f32[4,1,2,8192]{3,0,2,1:T(4,128)S(1)}) fusion(bf16[132,512]{1,0:T(8,128)(2,1)S(1)} %convolution_convert_fusion.1, bf16[8192,256]{1,0:T(8,128)(2,1)} %bitcast.115, pred[4,8192]{1,0:T(4,128)(4,1)S(1)} %iota_compare_fusion), kind=kOutput, calls=%fused_computation.83 | convolution fusion | flops 16973816 | bytes 2394144 | tf_op jit(solution)/shard_map/rgjd,tgd->rgjt/dot_general | solution.py:375
  135.0 0.3 fusion.32
  135.3 2.0 %fusion.25 = bf16[4,256]{1,0:T(4,128)(2,1)S(1)} fusion(bf16[8192,256]{1,0:T(8,128)(2,1)} %bitcast.116, f32[4,1,2,8192]{3,0,2,1:T(4,128)S(1)} %get-tuple-element.48, f32[4,2]{0,1:T(2,128)S(1)} %get-tuple-element.47, pred[4,8192]{1,0:T(4,128)(4,1)S(1)} %iota_compare_fusion, f32[4,2]{0,1:T(2,128)S(1)} %get-tuple-element.44, ...), kind=kOutput, calls=%fused_computation.30 | convolution fusion | flops 16978944 | bytes 2396288 | tf_op jit(solution)/shard_map/rgjt,tgd->rgjd/dot_general | solution.py:387
  137.4 0.2 copy.40
  137.5 3.4 %fusion.58 = (f32[2,128]{1,0:T(2,128)S(1)}, f32[1,2,128,8192]{2,3,1,0:T(8,128)S(1)}) fusion(bf16[16,2,8,128]{3,2,1,0:T(8,128)(2,1)S(1)} %get-tuple-element.28, bf16[8192,256]{1,0:T(8,128)(2,1)} %bitcast.117, pred[128,8192]{0,1:T(8,128)(4,1)S(1)} %compare_and_fusion), kind=kOutput, calls=%fused_computation.84 | convolution fusion | flops 543162112 | bytes 11600896 | tf_op jit(solution)/shard_map/while/body/eval_jaxpr/tgjd,kgd->gjtk/dot_general | solution.py:458
  140.9 0.0 copy-start
  140.9 1.7 fusion.4
  142.6 0.5 copy-done
  143.1 0.0 copy-start.1
  143.1 1.8 fusion.29
  144.9 0.0 copy-done.1
  144.9 1.8 %convolution_convert_fusion.part_ref = bf16[132,4096]{1,0:T(8,128)(2,1)} fusion(bf16[4096,256]{1,0:T(8,128)(2,1)S(1)} %bitcast.119, bf16[4,256]{0,1:T(8,128)(2,1)S(1)} %copy.40, bf16[128,256]{0,1:T(8,128)(2,1)S(1)} %bitcast.120), kind=kOutput, calls=%fused_computation.9 | convolution fusion | flops 277499904 | bytes 3246080 | tf_op jit(solution)/shard_map/dot_general | solution.py:532
  146.7 29.7 %shard_map.97 = bf16[8,132,512]{2,1,0:T(8,128)(2,1)} custom-call(bf16[132,4096]{1,0:T(8,128)(2,1)} %convolution_convert_fusion.part_ref), custom_call_target="tpu_custom_call" | custom-call | tf_op jit(solution)/shard_map/pallas_call | solution.py:315
  176.5 1.4 reduce_sum.73
  177.9 0.6 slice.51
  178.5 0.7 slice.50
  (11 shorter events, 0.1 us)
Async XLA Ops:
  140.9 2.2 %copy-start = (bf16[8,8,128,256]{3,2,1,0:T(8,128)(2,1)S(1)}, bf16[8,8,128,256]{3,2,1,0:T(8,128)(2,1)}, u32[]{:S(2)}) copy-start(bf16[8,8,128,256]{3,2,1,0:T(8,128)(2,1)} %shard_map.96) | copy-start | bytes 12582916
  143.1 1.8 %copy-start.1 = (bf16[8,8,64,256]{3,2,1,0:T(8,128)(2,1)S(1)}, bf16[8,8,64,256]{3,2,1,0:T(8,128)(2,1)}, u32[]{:S(2)}) copy-start(bf16[8,8,64,256]{3,2,1,0:T(8,128)(2,1)} %get-tuple-element.27) | copy-start | bytes 6291460

commit v20 on v17

--- a/solution.py
+++ b/solution.py
@@ -287,7 +287,18 @@
         remote(peer, peer).wait_recv()
         return carry
 
-    lax.fori_loop(1, count, send, 0)
+    if count % 2 == 0 and count >= 4:
+        outer = count // 2
+        order = sorted(range(outer), key=lambda hop: -min(hop, outer - hop))
+        for hop in order:
+            for core in range(2):
+                peer = lax.rem(me // 2 + hop, outer) * 2 + core
+
+                @pl.when(peer != me)
+                def _():
+                    remote(peer, me).start()
+    else:
+        lax.fori_loop(1, count, send, 0)
     lax.fori_loop(1, count, finish, 0)
     own.wait()
 

time: 180 us -> 180 us (level); the launches traced: 178 us -> 180 us
  Pallas kernels: 149 us -> 151 us
    pallas_call x1, Pallas kernels: 31.6 us -> 33.7 us  [scatter_sum_tp(): pl.pallas_call(functools.partial(_scatter_kernel, count), out_shape=jax.S...]
where the time goes in v20:
time: 180 us
  Pallas kernels  151 us (84%)
  matrix products  14.4 us (8%)
  other arithmetic  11.9 us (7%)
  local copies, waits for them, and re-layouts  2.09 us (1%)
    pallas_call x1, Pallas kernels, gather_ctx(): pl.pallas_call(kernel, out_shape=(jax.ShapeDtypeStruct((z_count, p_count)...  70.3 us
    pallas_call x1, Pallas kernels, gather_ctx(): pl.pallas_call(owned_kernel, out_shape=jax.ShapeDtypeStruct((z_count, p_c...  46.7 us
    pallas_call x1, Pallas kernels, scatter_sum_tp(): pl.pallas_call(functools.partial(_scatter_kernel, count), out_shape=jax.S...  33.7 us

profile of v20, /device:TPU:1, one launch (start us, length us, event | category | flops | bytes accessed | tf_op | source)
XLA Modules:
  0.0 179.8 jit_solution(8239103047315417405)
XLA Ops:
  0.6 0.8 reduce-window.8
  1.5 0.7 broadcast_multiply_fusion
  2.1 0.8 select_reduce_fusion
  3.0 0.1 convert_reduce_fusion.1
  3.1 0.1 iota_add_fusion
  3.2 0.1 add.96
  3.2 0.2 convert_reduce_fusion
  3.4 1.4 pad_maximum_fusion.first_ref
  4.9 2.8 %compare_and_fusion = pred[128,8192]{0,1:T(8,128)(4,1)S(1)} fusion(s32[128]{0:T(128)S(1)} %fusion.49, s32[128]{0:T(128)S(1)} %convert_reduce_fusion.1, s32[8192]{0:T(1024)S(1)} %add.96, s32[8192]{0:T(1024)S(1)} %convert_reduce_fusion), kind=kLoop, calls=%fused_computation.13 | loop fusion | flops 3145728 | bytes 1115136 | tf_op jit(solution)/shard_map/while/body/eval_jaxpr/and | solution.py:452
  7.6 70.3 %shard_map.95 = (bf16[8,8,64,512]{3,2,1,0:T(8,128)(2,1)}, bf16[8,8,64,256]{3,2,1,0:T(8,128)(2,1)}) custom-call(bf16[64,512]{1,0:T(8,128)(2,1)} %pad_maximum_fusion.first_ref, bf16[64,256]{1,0:T(8,128)(2,1)} %bitcast.121), custom_call_target="tpu_custom_call" | custom-call | tf_op jit(solution)/shard_map/pallas_call | solution.py:232
  77.9 3.3 %convolution_convert_fusion.1 = bf16[132,512]{1,0:T(8,128)(2,1)S(1)} fusion(bf16[4096,512]{1,0:T(8,128)(2,1)} %bitcast.124, bf16[4,4096]{1,0:T(4,128)(2,1)} %param.9, bf16[128,4096]{1,0:T(8,128)(2,1)} %param.8), kind=kOutput, calls=%fused_computation.17 | convolution fusion | flops 555878400 | bytes 5410816 | tf_op jit(solution)/shard_map/dot_general | solution.py:419
  81.2 0.1 multiply_reduce_fusion
  81.3 0.1 copy.39
  81.4 0.6 slice_bitcast_fusion.26
  82.1 46.7 %shard_map.96 = bf16[8,8,128,256]{3,2,1,0:T(8,128)(2,1)} custom-call(bf16[128,256]{1,0:T(8,128)(2,1)} %get-tuple-element.29.piece_ref), custom_call_target="tpu_custom_call" | custom-call | tf_op jit(solution)/shard_map/pallas_call | solution.py:222
  128.7 2.3 %fusion.54 = (f32[4,2]{0,1:T(2,128)S(1)}, f32[4,1,2,8192]{3,0,2,1:T(4,128)S(1)}) fusion(bf16[132,512]{1,0:T(8,128)(2,1)S(1)} %convolution_convert_fusion.1, bf16[8192,256]{1,0:T(8,128)(2,1)} %bitcast.115, pred[4,8192]{1,0:T(4,128)(4,1)S(1)} %iota_compare_fusion), kind=kOutput, calls=%fused_computation.82 | convolution fusion | flops 16973816 | bytes 2394144 | tf_op jit(solution)/shard_map/rgjd,tgd->rgjt/dot_general | solution.py:373
  131.1 0.3 fusion.30
  131.4 2.0 %fusion.23 = bf16[4,256]{1,0:T(4,128)(2,1)S(1)} fusion(bf16[8192,256]{1,0:T(8,128)(2,1)} %bitcast.116, f32[4,1,2,8192]{3,0,2,1:T(4,128)S(1)} %get-tuple-element.48, f32[4,2]{0,1:T(2,128)S(1)} %get-tuple-element.47, pred[4,8192]{1,0:T(4,128)(4,1)S(1)} %iota_compare_fusion, f32[4,2]{0,1:T(2,128)S(1)} %get-tuple-element.44, ...), kind=kOutput, calls=%fused_computation.28 | convolution fusion | flops 16978944 | bytes 2396288 | tf_op jit(solution)/shard_map/rgjt,tgd->rgjd/dot_general | solution.py:385
  133.5 0.2 copy.40
  133.6 3.4 %fusion.55 = (f32[2,128]{1,0:T(2,128)S(1)}, f32[1,2,128,8192]{2,3,1,0:T(8,128)S(1)}) fusion(bf16[16,2,8,128]{3,2,1,0:T(8,128)(2,1)S(1)} %get-tuple-element.28, bf16[8192,256]{1,0:T(8,128)(2,1)} %bitcast.117, pred[128,8192]{0,1:T(8,128)(4,1)S(1)} %compare_and_fusion), kind=kOutput, calls=%fused_computation.83 | convolution fusion | flops 543162112 | bytes 11600896 | tf_op jit(solution)/shard_map/while/body/eval_jaxpr/tgjd,kgd->gjtk/dot_general | solution.py:456
  137.0 0.0 copy-start
  137.0 1.1 fusion.4
  138.1 1.1 copy-done
  139.2 0.0 copy-start.1
  139.2 1.5 fusion.27
  140.7 0.1 copy-done.1
  140.8 1.8 %convolution_convert_fusion.part_ref = bf16[132,4096]{1,0:T(8,128)(2,1)} fusion(bf16[4096,256]{1,0:T(8,128)(2,1)S(1)} %bitcast.119, bf16[4,256]{0,1:T(8,128)(2,1)S(1)} %copy.40, bf16[128,256]{0,1:T(8,128)(2,1)S(1)} %bitcast.120), kind=kOutput, calls=%fused_computation.9 | convolution fusion | flops 277499904 | bytes 3246080 | tf_op jit(solution)/shard_map/dot_general | solution.py:530
  142.6 33.7 %shard_map.97 = bf16[8,132,512]{2,1,0:T(8,128)(2,1)} custom-call(bf16[132,4096]{1,0:T(8,128)(2,1)} %convolution_convert_fusion.part_ref), custom_call_target="tpu_custom_call" | custom-call | tf_op jit(solution)/shard_map/pallas_call | solution.py:308
  176.3 1.5 slice_reduce_fusion.1
  177.8 2.1 %slice_reduce_fusion = bf16[128,512]{1,0:T(8,128)(2,1)} fusion(bf16[8,132,512]{2,1,0:T(8,128)(2,1)} %shard_map.97), kind=kLoop, calls=%fused_computation.31 | loop fusion | flops 458752 | bytes 1179648 | tf_op jit(solution)/shard_map/reduce_sum | solution.py:322
  (11 shorter events, 0.1 us)
Async XLA Ops:
  137.0 2.2 %copy-start = (bf16[8,8,128,256]{3,2,1,0:T(8,128)(2,1)S(1)}, bf16[8,8,128,256]{3,2,1,0:T(8,128)(2,1)}, u32[]{:S(2)}) copy-start(bf16[8,8,128,256]{3,2,1,0:T(8,128)(2,1)} %shard_map.96) | copy-start | bytes 12582916
  139.2 1.6 copy-start.1

commit v21 on v20

--- a/solution.py
+++ b/solution.py
@@ -463,7 +463,7 @@
         )
         scores = jnp.where(allowed, scores, floor_value)
         peak_new = jnp.maximum(peak_run, jnp.max(scores, axis=3))
-        weights = jnp.exp(scores - peak_new[..., None])
+        weights = jnp.where(allowed, jnp.exp(scores - peak_new[..., None]), 0.0)
         rescale = jnp.exp(peak_run - peak_new)
         total_new = total_run * rescale + jnp.sum(weights, axis=3)
         mixed_new = mixed_run * rescale[..., None] + jnp.einsum(

time: 180 us -> 180 us (level)
  no operation moved by 1% of the time
where the time goes in v21:
time: 180 us
  Pallas kernels  150 us (83%)
  matrix products  14.7 us (8%)
  other arithmetic  12.5 us (7%)
    pallas_call x1, Pallas kernels, gather_ctx(): pl.pallas_call(kernel, out_shape=(jax.ShapeDtypeStruct((z_count, p_count)...  70.3 us
    pallas_call x1, Pallas kernels, gather_ctx(): pl.pallas_call(owned_kernel, out_shape=jax.ShapeDtypeStruct((z_count, p_c...  46.7 us
    pallas_call x1, Pallas kernels, scatter_sum_tp(): pl.pallas_call(functools.partial(_scatter_kernel, count), out_shape=jax.S...  33.6 us

profile of v21, /device:TPU:1, one launch (start us, length us, event | category | flops | bytes accessed | tf_op | source)
XLA Modules:
  0.0 179.9 jit_solution(5681363180507944418)
XLA Ops:
  0.6 0.8 reduce-window.8
  1.5 0.7 broadcast_multiply_fusion
  2.1 0.8 select_reduce_fusion
  3.0 0.1 convert_reduce_fusion.1
  3.1 0.1 iota_add_fusion
  3.2 0.1 add.96
  3.2 0.2 convert_reduce_fusion
  3.4 1.4 pad_maximum_fusion.first_ref
  4.9 2.8 %compare_and_fusion = pred[128,8192]{0,1:T(8,128)(4,1)S(1)} fusion(s32[128]{0:T(128)S(1)} %fusion.51, s32[128]{0:T(128)S(1)} %convert_reduce_fusion.1, s32[8192]{0:T(1024)S(1)} %add.96, s32[8192]{0:T(1024)S(1)} %convert_reduce_fusion), kind=kLoop, calls=%fused_computation.15 | loop fusion | flops 3145728 | bytes 1115136 | tf_op jit(solution)/shard_map/while/body/eval_jaxpr/and | solution.py:452
  7.6 70.3 %shard_map.95 = (bf16[8,8,64,512]{3,2,1,0:T(8,128)(2,1)}, bf16[8,8,64,256]{3,2,1,0:T(8,128)(2,1)}) custom-call(bf16[64,512]{1,0:T(8,128)(2,1)} %pad_maximum_fusion.first_ref, bf16[64,256]{1,0:T(8,128)(2,1)} %bitcast.121), custom_call_target="tpu_custom_call" | custom-call | tf_op jit(solution)/shard_map/pallas_call | solution.py:232
  77.9 3.3 %convolution_convert_fusion.1 = bf16[132,512]{1,0:T(8,128)(2,1)S(1)} fusion(bf16[4096,512]{1,0:T(8,128)(2,1)} %bitcast.124, bf16[4,4096]{1,0:T(4,128)(2,1)} %param.9, bf16[128,4096]{1,0:T(8,128)(2,1)} %param.8), kind=kOutput, calls=%fused_computation.19 | convolution fusion | flops 555878400 | bytes 5410816 | tf_op jit(solution)/shard_map/dot_general | solution.py:419
  81.2 0.1 multiply_reduce_fusion
  81.3 0.1 copy.39
  81.4 0.6 slice_bitcast_fusion.26
  82.1 46.7 %shard_map.96 = bf16[8,8,128,256]{3,2,1,0:T(8,128)(2,1)} custom-call(bf16[128,256]{1,0:T(8,128)(2,1)} %get-tuple-element.29.piece_ref), custom_call_target="tpu_custom_call" | custom-call | tf_op jit(solution)/shard_map/pallas_call | solution.py:222
  128.7 2.3 %fusion.57 = (f32[4,2]{0,1:T(2,128)S(1)}, f32[4,1,2,8192]{3,0,2,1:T(4,128)S(1)}) fusion(bf16[132,512]{1,0:T(8,128)(2,1)S(1)} %convolution_convert_fusion.1, bf16[8192,256]{1,0:T(8,128)(2,1)} %bitcast.115, pred[4,8192]{1,0:T(4,128)(4,1)S(1)} %iota_compare_fusion), kind=kOutput, calls=%fused_computation.85 | convolution fusion | flops 16973816 | bytes 2394144 | tf_op jit(solution)/shard_map/rgjd,tgd->rgjt/dot_general | solution.py:373
  131.1 0.3 fusion.32
  131.4 2.0 %fusion.25 = bf16[4,256]{1,0:T(4,128)(2,1)S(1)} fusion(bf16[8192,256]{1,0:T(8,128)(2,1)} %bitcast.116, f32[4,1,2,8192]{3,0,2,1:T(4,128)S(1)} %get-tuple-element.48, f32[4,2]{0,1:T(2,128)S(1)} %get-tuple-element.47, pred[4,8192]{1,0:T(4,128)(4,1)S(1)} %iota_compare_fusion, f32[4,2]{0,1:T(2,128)S(1)} %get-tuple-element.44, ...), kind=kOutput, calls=%fused_computation.30 | convolution fusion | flops 16978944 | bytes 2396288 | tf_op jit(solution)/shard_map/rgjt,tgd->rgjd/dot_general | solution.py:385
  133.4 0.2 copy.40
  133.6 3.4 %fusion.58 = (f32[2,128]{1,0:T(2,128)S(1)}, f32[1,2,128,8192]{2,3,1,0:T(8,128)S(1)}) fusion(bf16[16,2,8,128]{3,2,1,0:T(8,128)(2,1)S(1)} %get-tuple-element.28, bf16[8192,256]{1,0:T(8,128)(2,1)} %bitcast.117, pred[128,8192]{0,1:T(8,128)(4,1)S(1)} %compare_and_fusion), kind=kOutput, calls=%fused_computation.86 | convolution fusion | flops 543162112 | bytes 11600896 | tf_op jit(solution)/shard_map/while/body/eval_jaxpr/tgjd,kgd->gjtk/dot_general | solution.py:456
  137.0 0.0 copy-start
  137.0 1.7 fusion.4
  138.7 0.5 copy-done
  139.2 0.0 copy-start.1
  139.2 1.8 fusion.29
  141.0 0.0 copy-done.1
  141.0 1.8 %convolution_convert_fusion.part_ref = bf16[132,4096]{1,0:T(8,128)(2,1)} fusion(bf16[4096,256]{1,0:T(8,128)(2,1)S(1)} %bitcast.119, bf16[4,256]{0,1:T(8,128)(2,1)S(1)} %copy.40, bf16[128,256]{0,1:T(8,128)(2,1)S(1)} %bitcast.120), kind=kOutput, calls=%fused_computation.9 | convolution fusion | flops 277499904 | bytes 3246080 | tf_op jit(solution)/shard_map/dot_general | solution.py:530
  142.8 33.6 %shard_map.97 = bf16[8,132,512]{2,1,0:T(8,128)(2,1)} custom-call(bf16[132,4096]{1,0:T(8,128)(2,1)} %convolution_convert_fusion.part_ref), custom_call_target="tpu_custom_call" | custom-call | tf_op jit(solution)/shard_map/pallas_call | solution.py:308
  176.4 1.5 slice_reduce_fusion.1
  177.8 2.1 %slice_reduce_fusion = bf16[128,512]{1,0:T(8,128)(2,1)} fusion(bf16[8,132,512]{2,1,0:T(8,128)(2,1)} %shard_map.97), kind=kLoop, calls=%fused_computation.33 | loop fusion | flops 458752 | bytes 1179648 | tf_op jit(solution)/shard_map/reduce_sum | solution.py:322
  (11 shorter events, 0.1 us)
Async XLA Ops:
  137.0 2.2 %copy-start = (bf16[8,8,128,256]{3,2,1,0:T(8,128)(2,1)S(1)}, bf16[8,8,128,256]{3,2,1,0:T(8,128)(2,1)}, u32[]{:S(2)}) copy-start(bf16[8,8,128,256]{3,2,1,0:T(8,128)(2,1)} %shard_map.96) | copy-start | bytes 12582916
  139.2 1.8 %copy-start.1 = (bf16[8,8,64,256]{3,2,1,0:T(8,128)(2,1)S(1)}, bf16[8,8,64,256]{3,2,1,0:T(8,128)(2,1)}, u32[]{:S(2)}) copy-start(bf16[8,8,64,256]{3,2,1,0:T(8,128)(2,1)} %get-tuple-element.27) | copy-start | bytes 6291460
